TPU v7x, 32 devices: a whole 2x2x4 slice. The times are simulated.
32 devices in a mesh: cols: 8 (over y, x, core), rows: 4 (over z).
Axes of the slice: x: 2, y: 2, z: 4, core: 2. Of those that a mesh axis runs over, the one named last changes fastest.
Arguments:
- panel: bfloat16 [8, 24, 1024, 128], P('rows', 'cols'), may hold values from -0.1875 to 0.1875
- row_k: bfloat16 [24, 1024, 128], P('cols', 'rows'), as said below
- mask: int32 [8, 24], P('rows', 'cols'), may hold values 0 or 1
- a_low: bfloat16 [8, 1024, 128], P('rows'), may hold values from -0.375 to 0.375
- a_diag: float32 [1024, 1024], P('rows'), as said below
- sketch: bfloat16 [1024, 64], replicated, may hold values from -6 to 6
Outputs:
- panel_out: float32 [8, 1024, 128], P('rows')
- diag_factor: float32 [1024, 1024], P('rows')
Inputs may be any that keep to these rules, and one draw needn't show every extreme that they name: row_k entries are normal with deviation 1024 ** -0.5, cut at six deviations. a_diag - update is symmetric, with every eigenvalue 2 or more.
All inputs are finite; a program needn't handle non-finite values. No bound on the sum of `mask` on one device may be relied on, other than what follows from the above.
Results may differ from a plain program's by a relative error of at most 0.02.
Values may be sent and summed in bfloat16 or wider, within the bound.
No kernel may reach another device: no remote copies, remote signals or barrier semaphores. Data moves between devices by JAX's collectives and lax.ppermute only.
A program may use at most 128 MiB of HBM per device.

v0:
```python
import jax
import jax.numpy as jnp
from jax import lax
from jax.sharding import PartitionSpec as P


def apply_inverse(gram_matrix, field):
    lower_factor = jnp.linalg.cholesky(gram_matrix)
    turned = lax.linalg.triangular_solve(
        lower_factor, jnp.transpose(field, (1, 2, 0)), left_side=True, lower=True
    )
    return jnp.transpose(turned, (2, 0, 1))


def shards(panel, row_k, mask, a_low, a_diag, sketch):
    f32 = jnp.float32
    bf16 = jnp.bfloat16
    half_width = panel.shape[-1] // 2
    tile_order = panel.shape[2]
    rows_here = panel.shape[0]
    rank_cols = sketch.shape[1]
    share_count = tile_order // lax.axis_size("cols")
    share_offset = lax.axis_index("cols") * share_count

    def flatten_rows(values):
        return values.reshape(values.shape[0], rows_here * rank_cols)

    def split_rows(values):
        return values.reshape(values.shape[0], rows_here, rank_cols)

    whole_row = lax.all_gather(row_k, "rows", axis=1, tiled=True)
    k_left = whole_row[..., :half_width]
    k_right = whole_row[..., half_width:]
    own_left = row_k[..., :half_width]
    diag_core = jnp.einsum("jbr,jbs->jrs", k_right, k_right, preferred_element_type=f32).astype(
        bf16
    )
    own_mixed = jnp.einsum("jbr,jrs->jbs", own_left, diag_core, preferred_element_type=f32).astype(
        bf16
    )
    diag_part = jnp.einsum("jbs,jcs->bc", own_mixed, k_left, preferred_element_type=f32)
    diag_sum = lax.psum(diag_part.astype(jnp.bfloat16), "cols").astype(jnp.float32)
    whole_diag = lax.all_gather(
        (a_diag - diag_sum).astype(jnp.bfloat16), "rows", axis=0, tiled=True
    ).astype(jnp.float32)
    factor = jnp.linalg.cholesky(whole_diag)
    slab_rows = a_diag.shape[0]
    diag_out = lax.dynamic_slice_in_dim(factor, lax.axis_index("rows") * slab_rows, slab_rows, 0)
    left_part = panel[..., :half_width]
    right_part = panel[..., half_width:]
    weights = mask.astype(f32)[:, :, None, None]
    core = (
        jnp.einsum("ijbr,jbs->ijrs", right_part, k_right, preferred_element_type=f32) * weights
    ).astype(bf16)
    mixed_left = jnp.einsum("ijbr,ijrs->ijbs", left_part, core, preferred_element_type=f32).astype(
        bf16
    )
    probe_core = jnp.einsum("jbr,bp->jrp", k_left, sketch, preferred_element_type=f32).astype(bf16)
    a_up = a_low[..., :half_width]
    a_down = a_low[..., half_width:]

    def low_term(outer, inner, field):
        inner_core = jnp.einsum("ibr,bip->irp", inner, field, preferred_element_type=f32).astype(
            bf16
        )
        return jnp.einsum("ibr,irp->bip", outer, inner_core, preferred_element_type=f32)

    inner_first = jnp.einsum("ibr,bp->irp", a_down, sketch, preferred_element_type=f32).astype(bf16)
    a_first = jnp.einsum("ibr,irp->bip", a_up, inner_first, preferred_element_type=f32)
    piece = mixed_left
    terms = jnp.einsum("ijbs,jsp->bip", piece, probe_core, preferred_element_type=f32)
    first_share = lax.psum_scatter(
        terms.reshape(lax.axis_size("cols") * share_count, rows_here * rank_cols),
        "cols",
        scatter_dimension=0,
        tiled=True,
    )
    own_first = (
        lax.dynamic_slice_in_dim(flatten_rows(a_first), share_offset, share_count, 0) - first_share
    )
    first_b = split_rows(lax.all_gather(own_first.astype(bf16), "cols", axis=0, tiled=True))
    back_core = jnp.einsum(
        "ijbs,bip->ijsp", mixed_left, first_b, preferred_element_type=f32
    ).astype(bf16)
    a_second = low_term(a_down, a_up, first_b)
    piece = k_left
    terms = jnp.einsum("jbr,ijrp->bip", piece, back_core, preferred_element_type=f32)
    second_share = lax.psum_scatter(
        terms.reshape(lax.axis_size("cols") * share_count, rows_here * rank_cols),
        "cols",
        scatter_dimension=0,
        tiled=True,
    )
    own_second = (
        lax.dynamic_slice_in_dim(flatten_rows(a_second), share_offset, share_count, 0)
        - second_share
    )
    second_b = split_rows(lax.all_gather(own_second.astype(bf16), "cols", axis=0, tiled=True))
    fore_core = jnp.einsum("jbr,bip->ijrp", k_left, second_b, preferred_element_type=f32).astype(
        bf16
    )
    third_terms = jnp.einsum("ijbs,ijsp->bip", mixed_left, fore_core, preferred_element_type=f32)
    a_third = low_term(a_up, a_down, second_b)
    third = a_third - split_rows(
        lax.psum(flatten_rows(third_terms).astype(jnp.bfloat16), "cols").astype(jnp.float32)
    )
    gram_matrix = jnp.einsum("bip,biq->ipq", third, third, precision=lax.Precision.HIGHEST)
    basis_cols = apply_inverse(gram_matrix, third)
    basis_b = basis_cols.astype(bf16)
    last_core = jnp.einsum(
        "ijbs,bip->ijsp", mixed_left, basis_b, preferred_element_type=f32
    ).astype(bf16)
    last_terms = jnp.einsum("jbr,ijrp->bip", k_left, last_core, preferred_element_type=f32)
    projected = low_term(a_down, a_up, basis_b) - split_rows(
        lax.psum(flatten_rows(last_terms).astype(jnp.bfloat16), "cols").astype(jnp.float32)
    )
    solved = lax.linalg.triangular_solve(
        factor, flatten_rows(projected), left_side=True, lower=True
    )
    solved = split_rows(solved)
    panel_out = jnp.concatenate(
        [jnp.transpose(basis_cols, (1, 0, 2)), jnp.transpose(solved, (1, 0, 2))], axis=2
    )
    return (panel_out, diag_out)


def solution(mesh):
    return jax.shard_map(
        shards,
        mesh=mesh,
        in_specs=(
            P("rows", "cols", None, None),
            P("cols", "rows", None),
            P("rows", "cols"),
            P("rows", None, None),
            P("rows", None),
            P(),
        ),
        out_specs=(P("rows", None, None), P("rows", None)),
        check_vma=False,
    )
```

profile of v0, /device:TPU:0, one launch (start us, length us, event | category | flops | bytes accessed | tf_op | source)
XLA Modules:
  0.0 659.4 jit_solution(9756238469067348571)
XLA Ops:
  8.4 21.3 %all_gather.12 = bf16[3,1024,128]{1,2,0:T(8,128)(2,1)S(1)} all-gather(bf16[3,256,128]{1,2,0:T(8,128)(2,1)S(1)} %copy.21), channel_id=1, replica_groups=mesh['cols'=8,'rows'=4] {'rows'}, dimensions={1}, use_global_device_ids=true | all-gather | bytes 983040 | tf_op jit(solution)/shard_map/all_gather | solution.py:31
  30.3 3.1 fusion.10
  33.5 1.5 fusion.41
  35.7 32.9 %reduce-scatter.3.cloned.1.call-done = f32[128,128]{0,1:T(8,128)} async-done(((f32[1024,128]{0,1:T(8,128)}), f32[128,128]{0,1:T(8,128)}) %reduce-scatter.3.cloned.1.call-update) | async-done | bytes 65552 | tf_op jit(solution)/shard_map/reduce_scatter | solution.py:72
  69.4 9.3 %all_gather.13 = bf16[1024,128]{0,1:T(8,128)(2,1)S(1)} all-gather(bf16[128,128]{0,1:T(8,128)(2,1)S(1)} %subtract_convert_fusion.2), channel_id=1, replica_groups=mesh['cols'=8,'rows'=4] {'cols'}, dimensions={0}, use_global_device_ids=true | all-gather | bytes 294912 | tf_op jit(solution)/shard_map/all_gather | solution.py:81
  78.8 1.4 fusion.31
  80.6 1.3 fusion.9
  82.3 32.2 %reduce-scatter.5.cloned.1.call-done = f32[128,128]{0,1:T(8,128)} async-done(((f32[1024,128]{0,1:T(8,128)}), f32[128,128]{0,1:T(8,128)}) %reduce-scatter.5.cloned.1.call-update) | async-done | bytes 65552 | tf_op jit(solution)/shard_map/reduce_scatter | solution.py:88
  115.4 9.3 %all_gather.14 = bf16[1024,128]{0,1:T(8,128)(2,1)S(1)} all-gather(bf16[128,128]{0,1:T(8,128)(2,1)S(1)} %subtract_convert_fusion.1), channel_id=1, replica_groups=mesh['cols'=8,'rows'=4] {'cols'}, dimensions={0}, use_global_device_ids=true | all-gather | bytes 294912 | tf_op jit(solution)/shard_map/all_gather | solution.py:98
  124.7 1.4 fusion.18
  126.2 54.0 %all-reduce.5.cloned.1.call-done = bf16[1024,2,64]{0,2,1:T(8,128)(2,1)} async-done(((bf16[1024,2,64]{0,2,1:T(8,128)(2,1)}), bf16[1024,2,64]{0,2,1:T(8,128)(2,1)}) %all-reduce.5.cloned.1.call-update) | async-done | bytes 262160 | tf_op jit(solution)/shard_map/psum | solution.py:105
  180.2 1.5 fusion.13
  182.4 11.7 %custom-call.69 = f32[2,64,64]{2,1,0:T(8,128)S(1)} custom-call(f32[2,64,64]{2,1,0:T(8,128)S(1)} %fusion.139), custom_call_target="Cholesky" | custom-call | tf_op jit(solution)/shard_map/jit(cholesky)/cholesky | solution.py:8
  194.3 9.8 %custom-call.70 = f32[2,1,64,64]{2,3,1,0:T(8,128)S(1)} custom-call(f32[2,1,64,64]{3,2,1,0:T(8,128)S(1)} %select_bitcast_fusion.7), custom_call_target="InvertDiagBlocksLowerTriangular" | custom-call | tf_op jit(solution)/shard_map/triangular_solve | solution.py:9
  204.8 1.4 fusion.17
  206.3 1.6 copy.26
  207.8 53.7 %all-reduce.7.cloned.1.call-done = (bf16[256,1024]{0,1:T(8,128)(2,1)}, bf16[1024,2,64]{0,2,1:T(8,128)(2,1)}) async-done(((bf16[256,1024]{0,1:T(8,128)(2,1)}, bf16[1024,2,64]{0,2,1:T(8,128)(2,1)}), (bf16[256,1024]{0,1:T(8,128)(2,1)}, bf16[1024,2,64]{0,2,1:T(8,128)(2,1)})) %all-reduce.7.cloned.1.call-update) | async-done | bytes 786448 | tf_op jit(solution)/shard_map/psum | solution.py:42
  261.5 1.9 subtract_convert_fusion
  263.5 1.4 fusion.14
  264.9 44.3 %all-gather.2.cloned.1.call-done = bf16[1024,1024]{0,1:T(8,128)(2,1)} async-done(((bf16[256,1024]{0,1:T(8,128)(2,1)}), bf16[1024,1024]{0,1:T(8,128)(2,1)}) %all-gather.2.cloned.1.call-update) | async-done | bytes 2097168 | tf_op jit(solution)/shard_map/all_gather | solution.py:43
  309.2 4.4 copy.27
  313.6 2.9 fusion
  316.5 1.9 copy-done.2
  318.5 11.7 %cholesky.250 = f32[128,128]{1,0:T(8,128)S(1)} custom-call(f32[128,128]{1,0:T(8,128)S(1)} %cholesky.616), custom_call_target="Cholesky" | custom-call | tf_op jit(solution)/shard_map/jit(cholesky)/cholesky | solution.py:46
  330.2 2.5 cholesky.280
  332.7 9.8 %custom-call.71 = f32[1,128,128]{1,2,0:T(8,128)S(1)} custom-call(f32[1,128,128]{2,1,0:T(8,128)S(1)} %get-tuple-element.82), custom_call_target="InvertDiagBlocksLowerTriangular" | custom-call | tf_op jit(solution)/shard_map/jit(cholesky)/cholesky | solution.py:46
  342.5 2.3 constant_dynamic-update-slice_fusion.29
  344.9 1.5 convolution_subtract_fusion
  346.4 11.7 %cholesky.273 = f32[128,128]{1,0:T(8,128)S(1)} custom-call(f32[128,128]{1,0:T(8,128)S(1)} %cholesky.620), custom_call_target="Cholesky" | custom-call | tf_op jit(solution)/shard_map/jit(cholesky)/cholesky | solution.py:46
  358.8 10.0 %custom-call.72 = f32[1,128,128]{1,2,0:T(8,128)S(1)} custom-call(f32[1,128,128]{2,1,0:T(8,128)S(1)} %get-tuple-element.79), custom_call_target="InvertDiagBlocksLowerTriangular" | custom-call | tf_op jit(solution)/shard_map/jit(cholesky)/cholesky | solution.py:46
  370.0 2.1 convolution_subtract_fusion.1
  372.2 11.7 %cholesky.504 = f32[128,128]{1,0:T(8,128)S(1)} custom-call(f32[128,128]{1,0:T(8,128)S(1)} %cholesky.625), custom_call_target="Cholesky" | custom-call | tf_op jit(solution)/shard_map/jit(cholesky)/cholesky | solution.py:46
  385.2 9.8 %custom-call.73 = f32[1,128,128]{1,2,0:T(8,128)S(1)} custom-call(f32[1,128,128]{2,1,0:T(8,128)S(1)} %get-tuple-element.76), custom_call_target="InvertDiagBlocksLowerTriangular" | custom-call | tf_op jit(solution)/shard_map/jit(cholesky)/cholesky | solution.py:46
  396.1 2.3 convolution_subtract_fusion.2
  398.5 12.1 %cholesky.523 = f32[128,128]{1,0:T(8,128)S(1)} custom-call(f32[128,128]{1,0:T(8,128)S(1)} %cholesky.630), custom_call_target="Cholesky" | custom-call | tf_op jit(solution)/shard_map/jit(cholesky)/cholesky | solution.py:46
  411.9 9.8 %custom-call.74 = f32[1,128,128]{1,2,0:T(8,128)S(1)} custom-call(f32[1,128,128]{2,1,0:T(8,128)S(1)} %get-tuple-element.73), custom_call_target="InvertDiagBlocksLowerTriangular" | custom-call | tf_op jit(solution)/shard_map/jit(cholesky)/cholesky | solution.py:46
  422.8 2.3 convolution_subtract_fusion.3
  425.2 11.7 %cholesky.542 = f32[128,128]{1,0:T(8,128)S(1)} custom-call(f32[128,128]{1,0:T(8,128)S(1)} %cholesky.635), custom_call_target="Cholesky" | custom-call | tf_op jit(solution)/shard_map/jit(cholesky)/cholesky | solution.py:46
  438.3 9.8 %custom-call.75 = f32[1,128,128]{1,2,0:T(8,128)S(1)} custom-call(f32[1,128,128]{2,1,0:T(8,128)S(1)} %get-tuple-element.70), custom_call_target="InvertDiagBlocksLowerTriangular" | custom-call | tf_op jit(solution)/shard_map/jit(cholesky)/cholesky | solution.py:46
  449.3 2.3 convolution_subtract_fusion.4
  451.6 11.7 %cholesky.562 = f32[128,128]{1,0:T(8,128)S(1)} custom-call(f32[128,128]{1,0:T(8,128)S(1)} %cholesky.640), custom_call_target="Cholesky" | custom-call | tf_op jit(solution)/shard_map/jit(cholesky)/cholesky | solution.py:46
  464.6 9.8 %custom-call.76 = f32[1,128,128]{1,2,0:T(8,128)S(1)} custom-call(f32[1,128,128]{2,1,0:T(8,128)S(1)} %get-tuple-element.67), custom_call_target="InvertDiagBlocksLowerTriangular" | custom-call | tf_op jit(solution)/shard_map/jit(cholesky)/cholesky | solution.py:46
  475.3 2.0 convolution_subtract_fusion.5
  477.4 11.7 %cholesky.582 = f32[128,128]{1,0:T(8,128)S(1)} custom-call(f32[128,128]{1,0:T(8,128)S(1)} %cholesky.645), custom_call_target="Cholesky" | custom-call | tf_op jit(solution)/shard_map/jit(cholesky)/cholesky | solution.py:46
  490.3 10.0 %custom-call.77 = f32[1,128,128]{1,2,0:T(8,128)S(1)} custom-call(f32[1,128,128]{2,1,0:T(8,128)S(1)} %get-tuple-element.64), custom_call_target="InvertDiagBlocksLowerTriangular" | custom-call | tf_op jit(solution)/shard_map/jit(cholesky)/cholesky | solution.py:46
  501.1 1.8 convolution_subtract_fusion.11
  502.9 11.7 %cholesky.600 = f32[128,128]{1,0:T(8,128)S(1)} custom-call(f32[128,128]{1,0:T(8,128)S(1)} %convolution_subtract_fusion.11), custom_call_target="Cholesky" | custom-call | tf_op jit(solution)/shard_map/jit(cholesky)/cholesky | solution.py:46
  521.7 6.6 fusion.1
  528.2 27.5 %while.1 = (s32[]{:T(128)}, f32[1024,1024]{1,0:T(8,128)}, s32[8,2]{0,1:T(2,128)S(1)}, f32[8,128,128]{2,1,0:T(8,128)}, s32[]{:T(128)}) while((s32[]{:T(128)}, f32[1024,1024]{1,0:T(8,128)}, s32[8,2]{0,1:T(2,128)S(1)}, f32[8,128,128]{2,1,0:T(8,128)}, s32[]{:T(128)}) %tuple.71), condition=%wide.while_cond, body=%wide.while_body.sunk | while | flops 2 | bytes 132705 | solution.py:117
  528.8 2.8 bitcast_dynamic-update-slice_fusion.2
  532.3 2.8 bitcast_dynamic-update-slice_fusion.2
  535.7 2.8 bitcast_dynamic-update-slice_fusion.2
  539.2 2.8 bitcast_dynamic-update-slice_fusion.2
  542.6 2.8 bitcast_dynamic-update-slice_fusion.2
  546.0 2.8 bitcast_dynamic-update-slice_fusion.2
  549.5 2.8 bitcast_dynamic-update-slice_fusion.2
  552.9 2.8 bitcast_dynamic-update-slice_fusion.2
  555.7 79.6 %custom-call.78 = f32[8,128,128]{1,2,0:T(8,128)S(1)} custom-call(f32[8,128,128]{2,1,0:T(8,128)} %get-tuple-element.9), custom_call_target="InvertDiagBlocksLowerTriangular" | custom-call | tf_op jit(solution)/shard_map/triangular_solve | solution.py:117
  638.7 1.4 convolution_subtract_fusion.13
  640.4 1.5 convolution_subtract_fusion.12
  642.2 1.7 convolution_subtract_fusion.8
  644.2 1.8 convolution_subtract_fusion.7
  646.3 1.9 convolution_subtract_fusion.6
  650.1 2.3 constant_dynamic-slice_fusion.1
  (96 shorter events, 33.6 us)
Async XLA Ops:
  7.2 26.3 %copy-start = (bf16[1024,64]{0,1:T(8,128)(2,1)S(1)}, bf16[1024,64]{0,1:T(8,128)(2,1)}, u32[]{:S(2)}) copy-start(bf16[1024,64]{0,1:T(8,128)(2,1)} %param.11) | copy-start | bytes 393220
  7.2 27.8 %copy-start.1 = (bf16[2,1024,128]{2,1,0:T(8,128)(2,1)S(1)}, bf16[2,1024,128]{2,1,0:T(8,128)(2,1)}, u32[]{:S(2)}) copy-start(bf16[2,1024,128]{2,1,0:T(8,128)(2,1)} %param.9) | copy-start | bytes 1572868
  7.2 61.4 %reduce-scatter.3.cloned.1.call-start = ((), (), s32[]{:S(2)}) async-start(), calls=%async_computation.2 | async-start | bytes 589824 | tf_op jit(solution)/shard_map/reduce_scatter | solution.py:72
  33.4 47.1 %copy-start.4 = (bf16[3,256,128]{2,1,0:T(8,128)(2,1)S(1)}, bf16[3,256,128]{2,1,0:T(8,128)(2,1)}, u32[]{:S(2)}) copy-start(bf16[3,256,128]{2,1,0:T(8,128)(2,1)} %param.7) | copy-start | bytes 589828
  35.0 79.6 %reduce-scatter.5.cloned.1.call-start = ((), (), s32[]{:S(2)}) async-start(), calls=%async_computation.3 | async-start | bytes 589824 | tf_op jit(solution)/shard_map/reduce_scatter | solution.py:88
  80.2 99.9 %all-reduce.5.cloned.1.call-start = ((), (), s32[]{:S(2)}) async-start(), calls=%async_computation.4 | async-start | bytes 524288 | tf_op jit(solution)/shard_map/psum | solution.py:105
  126.1 135.4 %all-reduce.7.cloned.1.call-start = ((), (), s32[]{:S(2)}) async-start(), calls=%async_computation.6 | async-start | bytes 1572864 | tf_op jit(solution)/shard_map/psum | solution.py:42
  206.2 103.0 %all-gather.2.cloned.1.call-start = ((), (), s32[]{:S(2)}) async-start(), calls=%async_computation.5 | async-start | bytes 2621440 | tf_op jit(solution)/shard_map/all_gather | solution.py:43
  309.2 4.4 copy-start.3
  316.5 1.9 copy-start.2
Sparse Core Ops, SparseCore 0:
  35.1 33.4 reduce-scatter.2
  80.4 34.1 reduce-scatter.4
  126.2 53.8 all-reduce.4
  206.3 55.1 all-reduce.6
  263.6 45.5 all-gather.1
where the time goes:
time: 668 us; the launch traced here: 659 us
  other arithmetic  288 us (43%)
  waiting for transfers between devices  217 us (32%)
  matrix products  51.8 us (8%)
  local copies, waits for them, and re-layouts  43 us (6%)
  blocking collectives  39.9 us (6%)
  between operations  19.7 us (3%)
    another operation x30, other arithmetic, shards(): factor = jnp.linalg.cholesky(whole_diag)  172 us
    another operation x3, other arithmetic, shards(): lax.linalg.triangular_solve(factor, flatten_rows(projected), left_side=Tr...  86.2 us
    reduce_scatter x2, waiting for transfers between devices, shards(): lax.psum_scatter(terms.reshape(lax.axis_size('cols') * share_count, rows_...  65.1 us
    psum x1, waiting for transfers between devices, shards(): lax.psum(flatten_rows(third_terms).astype(jnp.bfloat16), 'cols')  54 us
    psum x1, waiting for transfers between devices, shards(): lax.psum(diag_part.astype(jnp.bfloat16), 'cols').astype(jnp.float32)  53.7 us
    all_gather x1, waiting for transfers between devices, shards(): lax.all_gather((a_diag - diag_sum).astype(jnp.bfloat16), 'rows', axis=0,...  44.3 us
    another operation x24, local copies, waits for them, and re-layouts  27.5 us
    another operation x14, matrix products, shards(): factor = jnp.linalg.cholesky(whole_diag)  23.2 us
  transfers between devices with their start and end apart: 5, of which 5 were waited for; matrix products, arithmetic and copies ran while one was open for 1% of the time, Pallas kernels for 0%

commit v1 on v0

v1 whole, which is shorter than its diff:
```python
import functools

import jax
import jax.numpy as jnp
from jax import lax
from jax.experimental import pallas as pl
from jax.experimental.pallas import tpu as pltpu
from jax.sharding import PartitionSpec as P

f32 = jnp.float32
bf16 = jnp.bfloat16
WIDE = 256
HALF = 128
SMEM = pl.BlockSpec(memory_space=pltpu.SMEM)
VMEM = pl.BlockSpec(memory_space=pltpu.VMEM)


def nt(first, second, **kw):
    return lax.dot_general(
        first, second, (((1,), (1,)), ((), ())), preferred_element_type=f32, **kw
    )


def tn(first, second):
    return lax.dot_general(first, second, (((0,), (0,)), ((), ())), preferred_element_type=f32)


def nn(first, second, **kw):
    return jnp.dot(first, second, preferred_element_type=f32, **kw)


def shaped(shape, kind):
    return jax.ShapeDtypeStruct(shape, kind)


def call(body, name, outs, *args, scratch=()):
    return pl.pallas_call(
        body,
        out_shape=outs,
        in_specs=[SMEM] + [VMEM] * (len(args) - 1),
        out_specs=jax.tree.map(lambda _: VMEM, outs),
        scratch_shapes=list(scratch),
        name=name,
    )(*args)


def eliminate(block):
    size = block.shape[0]
    lane = lax.broadcasted_iota(jnp.int32, (8, size), 1)
    sub = lax.broadcasted_iota(jnp.int32, (8, size), 0)
    tiles = [block[8 * g : 8 * g + 8] for g in range(size // 8)]

    def spread(tile, j):
        return jnp.broadcast_to(tile[:, j : j + 1], (8, size))

    def lift(tile, i):
        return jnp.broadcast_to(tile[i : i + 1], (8, size))

    uppers, inverses = [], []
    for own in range(size // 8):
        base = 8 * own
        tile = tiles[own]
        cols = [spread(tile, base + j) for j in range(8)]
        s = {(i, j): lift(cols[j], i) for j in range(8) for i in range(j, 8)}
        inside = (lane >= base) & (lane < base + 8)
        u = [
            jnp.where(inside, jnp.where(lane == base + i, 1.0, 0.0), lift(tile, i))
            for i in range(8)
        ]
        inv, m = [], {}
        for k in range(8):
            inv.append(1.0 / s[k, k])
            for i in range(k + 1, 8):
                m[i, k] = s[i, k] * inv[k]
            for i in range(k + 1, 8):
                for j in range(k + 1, i + 1):
                    s[i, j] = s[i, j] - m[i, k] * s[j, k]
                u[i] = u[i] - m[i, k] * u[k]
        w = [u[i] * inv[i] for i in range(8)]
        for i in range(6, -1, -1):
            for k in range(7, i, -1):
                w[i] = w[i] - m[k, i] * w[k]
        for g in range(own + 1, size // 8):
            rest = jnp.where(inside, 0.0, tiles[g])
            for j in range(7, -1, -1):
                rest = rest - spread(tiles[g], base + j) * w[j]
            tiles[g] = rest
        low = jnp.zeros((8, size), f32)
        up = jnp.zeros((8, size), f32)
        for i in range(8):
            root = lax.rsqrt(s[i, i])
            row = u[i] * root
            low = jnp.where(sub == i, row, low)
            for j in range(i, 8):
                row = jnp.where(lane == base + j, s[j, i] * root, row)
            up = jnp.where(sub == i, row, up)
        inverses.append(jnp.where(lane <= sub + base, low, 0.0))
        uppers.append(jnp.where(lane >= sub + base, up, 0.0))
    return jnp.concatenate(uppers, 0), jnp.concatenate(inverses, 0)


def prepare_body(place, row_ref, diag_ref, low_ref, sketch_ref, *outs):
    left_ref, right_ref, piece_ref, low_t_ref, sketch_t_ref = outs
    count, slab, width = row_ref.shape
    half = width // 2
    per = max(slab // half, 1)
    core, block = place[0], place[5]
    for j in range(count):
        turned = row_ref[j].astype(f32).T.astype(bf16)
        left_ref[j * half : (j + 1) * half, :] = turned[:half]
        right_ref[j * half : (j + 1) * half, :] = turned[half:]
        gram = nt(turned[half:], turned[half:])
        top = count * half + (j // per) * half
        if j % per == 0:
            left_ref[top : top + half, :] = jnp.zeros((half, slab), bf16)
        at = (j % per) * half
        left_ref[top : top + half, at : at + half] = gram.astype(bf16)
    wide = diag_ref[:, pl.ds(pl.multiple_of(block * HALF, HALF), HALF)]
    lane = lax.broadcasted_iota(jnp.int32, wide.shape, 1)
    piece_ref[...] = jnp.where((lane >= place[6]) & (lane < place[7]), wide, 0.0).astype(bf16)
    turned = low_ref[core].astype(f32).T
    low_t_ref[...] = turned.astype(bf16)
    sketch_t_ref[...] = sketch_ref[...].astype(f32).T.astype(bf16)


def diagonal_body(count, parts, place, *refs):
    lefts, pieces = refs[:parts], refs[parts : 2 * parts]
    left_ref, own0_ref, own1_ref, away0_ref, away1_ref, total, turned = refs[2 * parts :]
    slab = lefts[0].shape[1]
    half = turned.shape[0] // count
    per = max(slab // half, 1)
    core, z, block = place[0], place[1], place[5]
    for d in range(parts):
        source = lax.rem(z - d + parts, parts)
        left_ref[:, pl.ds(pl.multiple_of(source * slab, HALF), slab)] = lefts[d][: count * half]
    for j in range(count):
        rows = slice(j * half, (j + 1) * half)
        top, at = count * half + (j // per) * half, (j % per) * half
        core_sum = sum(lefts[d][top : top + half, at : at + half].astype(f32) for d in range(parts))
        turned[rows, :] = (-nn(core_sum.astype(bf16), left_ref[rows, :])).astype(bf16)
    total[...] = tn(turned[...], left_ref[...])
    for d in range(parts):
        source = lax.rem(z - d + parts, parts)
        at = (
            pl.ds(pl.multiple_of(source * slab, slab), slab),
            pl.ds(pl.multiple_of(block * HALF, HALF), HALF),
        )
        total[at] = total[at] + pieces[d][...].astype(f32)
    order = total.shape[0]
    for out0, out1, side in ((own0_ref, own1_ref, core), (away0_ref, away1_ref, 1 - core)):
        fill = 0
        for g in range(order // WIDE):
            for b in range(g, order // WIDE):
                from_row = pl.multiple_of(b * WIDE + side * HALF, HALF)
                value = total[pl.ds(from_row, HALF), g * WIDE : (g + 1) * WIDE].astype(bf16)
                if g == 0:
                    out0[b * HALF : (b + 1) * HALF, :] = value
                else:
                    out1[fill : fill + HALF, :] = value
                    fill += HALF


def factor_body(group, at, place, own_ref, other_ref, *refs):
    earlier = refs[:group]
    slab_ref, half_ref, inverse_ref, acc, whole = refs[group:]
    core, z = place[0], place[1]
    order = whole.shape[0]
    first = group * WIDE
    count = order - first
    for b in range(count // WIDE):
        rows = slice(at + b * HALF, at + (b + 1) * HALF)
        acc[pl.ds(pl.multiple_of(b * WIDE + core * HALF, HALF), HALF), :] = own_ref[rows].astype(f32)
        acc[pl.ds(pl.multiple_of(b * WIDE + HALF - core * HALF, HALF), HALF), :] = other_ref[
            rows
        ].astype(f32)
    if group:
        total = acc[...]
        for h in range(group):
            skip = (group - h) * WIDE
            total = total - nt(earlier[h][skip:, :], earlier[h][skip : skip + WIDE, :])
        acc[...] = total
        whole[:first, :] = jnp.zeros((first, WIDE), f32)
    for start in range(0, WIDE, HALF):
        cols = slice(start, start + HALF)
        upper, inverse = eliminate(acc[cols, cols])
        inverse = inverse.astype(bf16)
        lower = upper.T
        whole[first + start : first + start + HALF, cols] = lower
        half_ref[cols, cols] = lower.astype(bf16)
        inverse_ref[cols, cols] = inverse
        if start:
            whole[first : first + start, cols] = jnp.zeros((start, HALF), f32)
            half_ref[:start, cols] = jnp.zeros((start, HALF), bf16)
            inverse_ref[:start, cols] = jnp.zeros((start, HALF), bf16)
            between = nn(half_ref[cols, :start], inverse_ref[:start, :start]).astype(bf16)
            inverse_ref[cols, :start] = (-nn(inverse, between)).astype(bf16)
        below = start + HALF
        if below < count:
            under = nt(acc[below:, cols].astype(bf16), inverse)
            whole[first + below :, cols] = under
            under = under.astype(bf16)
            half_ref[below:, cols] = under
            if below < WIDE:
                acc[below:, below:] = acc[below:, below:] - nt(under, under[: WIDE - below])
    slab = slab_ref.shape[0]
    slab_ref[...] = whole[pl.ds(pl.multiple_of(z * slab, slab), slab), :]


def mixed_body(parts, place, mask_ref, *refs):
    rights, panel_ref = refs[:parts], refs[parts]
    own_ref, away_ref, right = refs[parts + 1 :]
    slab = rights[0].shape[1]
    core, z = place[0], place[1]
    for d in range(parts):
        source = lax.rem(z - d + parts, parts)
        right[:, pl.ds(pl.multiple_of(source * slab, HALF), slab)] = rights[d][...]
    count, half = panel_ref.shape[1], panel_ref.shape[3] // 2
    for out, row in ((own_ref, core), (away_ref, 1 - core)):
        for j in range(count):
            rows = slice(j * half, (j + 1) * half)
            both = nn(right[rows, :], panel_ref[row, j])
            sign = -mask_ref[row, j].astype(f32)
            inner = (both[:, half:] * sign).astype(bf16)
            out[rows, :] = nt(inner, panel_ref[row, j, :, :half]).astype(bf16)


def apply_stage(value, inners, outers):
    total = None
    for inner, outer in zip(inners, outers):
        part = nn(nt(value, inner).astype(bf16), outer)
        total = part if total is None else total + part
    return total.astype(bf16)


def put_halves(value, refs):
    rows = value.shape[0] // 2
    refs[0][...] = value[:rows]
    refs[1][...] = value[rows:]


def get_halves(refs):
    low = refs[4][...]
    return low + jnp.concatenate(
        [refs[i][...].astype(f32) + refs[i + 2][...].astype(f32) for i in range(2)], axis=0
    )


def low_body(forward, place, value_ref, low_ref, out_ref):
    half = low_ref.shape[0] // 2
    up, down = low_ref[:half], low_ref[half:]
    inner, outer = (down, up) if forward else (up, down)
    out_ref[...] = nn(nt(value_ref[...], inner).astype(bf16), outer)


def first_body(place, value_ref, u0, u1, m0, m1, *outs):
    put_halves(apply_stage(value_ref[...], (u0[...], u1[...]), (m0[...], m1[...])), outs)


def middle_body(forward, place, a0, a1, b0, b1, low, u0, u1, m0, m1, value_ref, *outs):
    ups, downs = (m0[...], m1[...]), (u0[...], u1[...])
    value = get_halves((a0, a1, b0, b1, low)).astype(bf16)
    value_ref[...] = value
    inners, outers = (downs, ups) if forward else (ups, downs)
    put_halves(apply_stage(value, inners, outers), outs)


def basis_body(place, a0, a1, b0, b1, low, u0, u1, m0, m1, basis_ref, *outs):
    third = get_halves((a0, a1, b0, b1, low))
    gram = nt(third, third, precision=lax.Precision.HIGHEST)
    _, inverse = eliminate(gram)
    basis = nn(inverse, third, precision=lax.Precision.HIGHEST).astype(bf16)
    basis_ref[...] = basis
    put_halves(apply_stage(basis, (m0[...], m1[...]), (u0[...], u1[...])), outs)


def solve_body(groups, place, a0, a1, b0, b1, low, *refs):
    factors, inverses, out_ref = refs[:groups], refs[groups : 2 * groups], refs[2 * groups]
    value = get_halves((a0, a1, b0, b1, low))
    solved = []
    for g in range(groups):
        cols = slice(g * WIDE, (g + 1) * WIDE)
        rest = value[:, cols]
        for h in range(g):
            skip = (g - h) * WIDE
            rest = rest - nt(solved[h], factors[h][skip : skip + WIDE, :])
        solved.append(nt(rest.astype(bf16), inverses[g][...]).astype(bf16))
        out_ref[:, cols] = solved[g]


def finish_body(place, basis_own, basis_other, solved_own, solved_other, out_ref):
    core = place[0]
    half = basis_own.shape[0]
    for row, basis, solved in (
        (core, basis_own, solved_own),
        (1 - core, basis_other, solved_other),
    ):
        both = jnp.concatenate([basis[...], solved[...]], axis=0).astype(f32)
        out_ref[row] = both.T


def shards(panel, row_k, mask, a_low, a_diag, sketch):
    cols, parts = lax.axis_size("cols"), lax.axis_size("rows")
    here, z = lax.axis_index("cols"), lax.axis_index("rows")
    count, slab, width = row_k.shape
    half = width // 2
    order, rank = sketch.shape
    groups = order // WIDE
    piece = max(order // cols, 1)
    place = jnp.stack(
        [
            here % 2,
            z,
            here,
            here // 2,
            here * 0,
            here * piece // HALF,
            here * piece % HALF,
            here * piece % HALF + piece,
        ]
    ).astype(jnp.int32)
    partner = [(i, i ^ 1) for i in range(cols)]
    masks = [2 << i for i in range((cols // 2).bit_length() - 1)]

    def swap(value):
        return lax.ppermute(value, "cols", partner)

    def cross(value, bit):
        return lax.ppermute(value, "cols", [(i, i ^ bit) for i in range(cols)])

    def spread_rows(value):
        return [value] + [
            lax.ppermute(value, "rows", [(i, (i + d) % parts) for i in range(parts)])
            for d in range(1, parts)
        ]

    def add(first, second):
        return (first.astype(f32) + second.astype(f32)).astype(bf16)

    def sum_chips(pair):
        orders = (masks, masks[::-1])
        value = list(pair)
        for step in range(len(masks)):
            got = [cross(value[i], orders[i][step]) for i in range(2)]
            if step == len(masks) - 1:
                return value[0], value[1], got[0], got[1]
            value = [add(value[i], got[i]) for i in range(2)]

    blocks = -(-count // max(slab // half, 1))
    left, right, corner, low_t, sketch_t = call(
        prepare_body,
        "prepare",
        (
            shaped(((count + blocks) * half, slab), bf16),
            shaped((count * half, slab), bf16),
            shaped((slab, HALF), bf16),
            shaped((width, order), bf16),
            shaped((rank, order), bf16),
        ),
        place,
        row_k,
        a_diag,
        a_low,
        sketch,
    )
    lefts = spread_rows(left)
    corners = spread_rows(corner)
    rights = spread_rows(right)
    rest_rows = sum((groups - g) * HALF for g in range(1, groups))
    left_t, own0, own1, away0, away1 = call(
        functools.partial(diagonal_body, count, parts),
        "diagonal",
        (
            shaped((count * half, order), bf16),
            shaped((groups * HALF, WIDE), bf16),
            shaped((rest_rows, WIDE), bf16),
            shaped((groups * HALF, WIDE), bf16),
            shaped((rest_rows, WIDE), bf16),
        ),
        place,
        *lefts,
        *corners,
        scratch=(pltpu.VMEM((order, order), f32), pltpu.VMEM((count * half, order), bf16)),
    )

    def whole_chunk(own, away):
        value = add(own, swap(away))
        rows = value.shape[0] // 2
        a0, a1, b0, b1 = sum_chips((value[:rows], value[rows:]))
        value = jnp.concatenate([add(a0, b0), add(a1, b1)], axis=0)
        return value, swap(value)

    head = whole_chunk(own0, away0)
    tail = whole_chunk(own1, away1)
    left_other = swap(left_t)
    mixed_own, mixed_away = pl.pallas_call(
        functools.partial(mixed_body, parts),
        out_shape=(shaped((count * half, order), bf16),) * 2,
        in_specs=[SMEM, SMEM] + [VMEM] * (parts + 1),
        out_specs=(VMEM, VMEM),
        scratch_shapes=[pltpu.VMEM((count * half, order), bf16)],
        name="mixed",
    )(place, mask, *rights, panel)
    mixed_other = swap(mixed_away)
    factors = (left_t, left_other, mixed_own, mixed_other)
    pair = (shaped((rank // 2, order), bf16),) * 2

    slabs, halves, inverses = [], [], []
    at = 0
    for g in range(groups):
        rows = order - g * WIDE
        own, other = head if g == 0 else tail
        slab_part, half_part, inverse = call(
            functools.partial(factor_body, g, at),
            "factor%d" % g,
            (
                shaped((slab, WIDE), f32),
                shaped((rows, WIDE), bf16),
                shaped((WIDE, WIDE), bf16),
            ),
            place,
            own,
            other,
            *halves,
            scratch=(pltpu.VMEM((rows, WIDE), f32), pltpu.VMEM((order, WIDE), f32)),
        )
        if g:
            at += rows // 2
        slabs.append(slab_part)
        halves.append(half_part)
        inverses.append(inverse)
    diag_out = jnp.concatenate(slabs, axis=1)

    whole = shaped((rank, order), bf16)

    def low_term(value, forward):
        return call(
            functools.partial(low_body, forward),
            "low",
            shaped((rank, order), f32),
            place,
            value,
            low_t,
        )

    low = low_term(sketch_t, True)
    value = sum_chips(call(first_body, "first", pair, place, sketch_t, *factors))
    for forward, name in ((False, "second"), (True, "third")):
        start, *value = call(
            functools.partial(middle_body, forward),
            name,
            (whole,) + pair,
            place,
            *value,
            low,
            *factors,
        )
        low = low_term(start, forward)
        value = sum_chips(value)
    basis, *value = call(basis_body, "basis", (whole,) + pair, place, *value, low, *factors)
    low = low_term(basis, False)
    basis_other = swap(basis)
    value = sum_chips(value)
    solved = call(
        functools.partial(solve_body, groups),
        "solve",
        whole,
        place,
        *value,
        low,
        *halves,
        *inverses,
    )
    panel_out = call(
        finish_body,
        "finish",
        shaped((2, order, 2 * rank), f32),
        place,
        basis,
        basis_other,
        solved,
        swap(solved),
    )
    return panel_out, diag_out


def solution(mesh):
    return jax.shard_map(
        shards,
        mesh=mesh,
        in_specs=(
            P("rows", "cols", None, None),
            P("cols", "rows", None),
            P("rows", "cols"),
            P("rows", None, None),
            P("rows", None),
            P(),
        ),
        out_specs=(P("rows", None, None), P("rows", None)),
        check_vma=False,
    )
```

time: 668 us -> 187 us (0.28)
  other arithmetic: 288 us -> 6.82 us
  waiting for transfers between devices: 217 us -> 34.7 us
  Pallas kernels: 0 us -> 85.4 us
  matrix products: 51.8 us -> 0 us
  starting transfers between devices: 0.21 us -> 43.7 us
  blocking collectives: 39.9 us -> 0 us
  local copies, waits for them, and re-layouts: 43 us -> 11.7 us
  between operations: 19.7 us -> 1.57 us
    another operation x40 -> x0, other arithmetic: 280 us -> none  [the longest x30 172 us: shards(): factor = jnp.linalg.cholesky(whole_diag)]
    psum x2 -> x0, waiting for transfers between devices: 108 us -> none  [the longest x1 54 us: shards(): lax.psum(flatten_rows(third_terms).astype(jnp.bfloat16), 'cols')]
    pallas_call x0 -> x17, Pallas kernels: none -> 85.4 us  [the longest x16 81.2 us: call(): pl.pallas_call(body, out_shape=outs, in_specs=[SMEM] + [VMEM] * (len(args...]
    reduce_scatter x2 -> x0, waiting for transfers between devices: 65.1 us -> none  [shards(): lax.psum_scatter(terms.reshape(lax.axis_size('cols') * share_count, rows_...]
    all_gather x1 -> x0, waiting for transfers between devices: 44.3 us -> none  [shards(): lax.all_gather((a_diag - diag_sum).astype(jnp.bfloat16), 'rows', axis=0,...]
    ppermute x0 -> x41, starting transfers between devices: none -> 43.7 us  [the longest x24 26.7 us: cross(): return lax.ppermute(value, 'cols', [(i, i ^ bit) for i in range(cols)])]
    all_gather x3 -> x0, blocking collectives: 39.9 us -> none  [the longest x1 21.3 us: shards(): whole_row = lax.all_gather(row_k, 'rows', axis=1, tiled=True)]
    another operation x30 -> x0, matrix products: 36.9 us -> none  [the longest x14 23.2 us: shards(): factor = jnp.linalg.cholesky(whole_diag)]
  transfers between devices with their start and end apart: 5 -> 41, of which waited for: 5 -> 17; matrix products, arithmetic and copies ran while one was open for 1% -> 4% of each run, Pallas kernels for 0% -> 42%
where the time goes in v1:
time: 187 us; the launch traced here: 184 us
  Pallas kernels  85.4 us (46%)
  starting transfers between devices  43.7 us (23%)
  waiting for transfers between devices  34.7 us (19%)
  local copies, waits for them, and re-layouts  11.7 us (6%)
  other arithmetic  6.82 us (4%)
    pallas_call x16, Pallas kernels, call(): pl.pallas_call(body, out_shape=outs, in_specs=[SMEM] + [VMEM] * (len(args...  81.2 us
    ppermute x24, starting transfers between devices, cross(): return lax.ppermute(value, 'cols', [(i, i ^ bit) for i in range(cols)])  26.7 us
    ppermute x9, waiting for transfers between devices, spread_rows(): lax.ppermute(value, 'rows', [(i, (i + d) % parts) for i in range(parts)])  19.7 us
    ppermute x9, starting transfers between devices, spread_rows(): lax.ppermute(value, 'rows', [(i, (i + d) % parts) for i in range(parts)])  15.7 us
    ppermute x24, waiting for transfers between devices, cross(): return lax.ppermute(value, 'cols', [(i, i ^ bit) for i in range(cols)])  14.9 us
    unnamed x89, local copies, waits for them, and re-layouts  11 us
    convert_element_type x16, other arithmetic, add(): return (first.astype(f32) + second.astype(f32)).astype(bf16)  5.66 us
    pallas_call x1, Pallas kernels, shards(): pl.pallas_call(functools.partial(mixed_body, parts), out_shape=(shaped((c...  4.2 us
  transfers between devices with their start and end apart: 41, of which 17 were waited for; matrix products, arithmetic and copies ran while one was open for 4% of the time, Pallas kernels for 42%

profile of v1, /device:TPU:0, one launch (start us, length us, event | category | flops | bytes accessed | tf_op | source)
XLA Modules:
  0.0 184.0 jit_solution(778729504694500516)
XLA Ops:
  0.7 1.7 copy.8.sketch_ref
  3.1 2.6 %prepare.1 = (bf16[256,256]{1,0:T(8,128)(2,1)}, bf16[192,256]{1,0:T(8,128)(2,1)}, bf16[256,128]{1,0:T(8,128)(2,1)}, bf16[128,1024]{1,0:T(8,128)(2,1)}, bf16[64,1024]{1,0:T(8,128)(2,1)}) custom-call(s32[8]{0:T(128)} %stack.31.place, bf16[3,256,128]{2,1,0:T(8,128)(2,1)} %row_ref.1, f32[256,1024]{1,0:T(8,128)} %diag_ref.1, bf16[2,1024,128]{2,1,0:T(8,128)(2,1)} %low_ref.1, ...), custom_call_target="tpu_custom_call" | custom-call | tf_op jit(solution)/shard_map/prepare/pallas_call | solution.py:37
  5.7 5.1 %collective-permute-start.5 = (bf16[256,128]{1,0:T(8,128)(2,1)}, bf16[256,128]{1,0:T(8,128)(2,1)S(1)}, u32[]{:S(2)}, u32[]{:S(2)}) collective-permute-start(bf16[256,128]{1,0:T(8,128)(2,1)} %get-tuple-element.39.refs_4_), channel_id=1, source_target_pairs={{0,3},{1,0},{2,1},{3,2},{4,7},{5,4},{6,5},{7,6},{8,11},{9,8},{10,9... | collective-permute-start | bytes 196616 | tf_op jit(solution)/shard_map/ppermute | solution.py:332
  11.2 1.6 collective-permute-start
  12.8 2.9 %collective-permute-start.4 = (bf16[256,128]{1,0:T(8,128)(2,1)}, bf16[256,128]{1,0:T(8,128)(2,1)S(1)}, u32[]{:S(2)}, u32[]{:S(2)}) collective-permute-start(bf16[256,128]{1,0:T(8,128)(2,1)} %get-tuple-element.39.refs_4_), channel_id=1, source_target_pairs={{0,2},{1,3},{2,0},{3,1},{4,6},{5,7},{6,4},{7,5},{8,10},{9,11},{10,... | collective-permute-start | bytes 196616 | tf_op jit(solution)/shard_map/ppermute | solution.py:332
  15.7 11.9 %collective-permute-done.4.refs_6_ = bf16[256,128]{1,0:T(8,128)(2,1)S(1)} collective-permute-done((bf16[256,128]{1,0:T(8,128)(2,1)}, bf16[256,128]{1,0:T(8,128)(2,1)S(1)}, u32[]{:S(2)}, u32[]{:S(2)}) %collective-permute-start.4) | collective-permute-done | bytes 65568 | tf_op jit(solution)/shard_map/ppermute | solution.py:332
  29.1 3.5 %diagonal.1 = (bf16[192,1024]{1,0:T(8,128)(2,1)}, bf16[512,256]{1,0:T(8,128)(2,1)}, bf16[768,256]{1,0:T(8,128)(2,1)}, bf16[512,256]{1,0:T(8,128)(2,1)}, bf16[768,256]{1,0:T(8,128)(2,1)}) custom-call(s32[8]{0:T(128)} %stack.31.place, bf16[256,256]{1,0:T(8,128)(2,1)} %get-tuple-element.38.refs_0_, bf16[256,256]{1,0:T(8,128)(2,1)} %copy-done.26, ...), custom_call_target="tpu_custom_call" | custom-call | tf_op jit(solution)/shard_map/diagonal/pallas_call | solution.py:37
  32.6 3.1 %collective-permute-start.9 = (bf16[192,256]{1,0:T(8,128)(2,1)}, bf16[192,256]{1,0:T(8,128)(2,1)S(1)}, u32[]{:S(2)}, u32[]{:S(2)}) collective-permute-start(bf16[192,256]{1,0:T(8,128)(2,1)} %get-tuple-element.41.refs_0_), channel_id=1, source_target_pairs={{0,3},{1,0},{2,1},{3,2},{4,7},{5,4},{6,5},{7,6},{8,11},{9,8},{10,9... | collective-permute-start | bytes 294920 | tf_op jit(solution)/shard_map/ppermute | solution.py:332
  36.2 2.1 %collective-permute-start.7 = (bf16[192,256]{1,0:T(8,128)(2,1)}, bf16[192,256]{1,0:T(8,128)(2,1)S(1)}, u32[]{:S(2)}, u32[]{:S(2)}) collective-permute-start(bf16[192,256]{1,0:T(8,128)(2,1)} %get-tuple-element.41.refs_0_), channel_id=1, source_target_pairs={{0,1},{1,2},{2,3},{3,0},{4,5},{5,6},{6,7},{7,4},{8,9},{9,10},{10,1... | collective-permute-start | bytes 294920 | tf_op jit(solution)/shard_map/ppermute | solution.py:332
  38.3 1.0 collective-permute-done.9.refs_3_
  39.3 6.8 %collective-permute-done.8.refs_2_ = bf16[192,256]{1,0:T(8,128)(2,1)S(1)} collective-permute-done((bf16[192,256]{1,0:T(8,128)(2,1)}, bf16[192,256]{1,0:T(8,128)(2,1)S(1)}, u32[]{:S(2)}, u32[]{:S(2)}) %collective-permute-start.8) | collective-permute-done | bytes 98336 | tf_op jit(solution)/shard_map/ppermute | solution.py:332
  47.4 4.2 %mixed.1 = (bf16[192,1024]{1,0:T(8,128)(2,1)}, bf16[192,1024]{1,0:T(8,128)(2,1)}) custom-call(s32[8]{0:T(128)} %stack.31.place, s32[2,3]{1,0:T(2,128)} %mask_ref.1, bf16[192,256]{1,0:T(8,128)(2,1)} %get-tuple-element.41.refs_0_, bf16[192,256]{1,0:T(8,128)(2,1)} %copy-done.29, bf16[192,256]{1,0:T(8,128)(2,1)} %copy-done.28, bf16[192,256]{1,0:T(8,128)(2,1)} %copy-done.27, ...), custom_call_target="tpu_custom_call" | custom-call | tf_op jit(solution)/shard_map/mixed/pallas_call | solution.py:395
  52.2 1.6 collective-permute-start.29
  53.8 1.5 collective-permute-start.31
  55.3 2.2 %low.4 = f32[64,1024]{1,0:T(8,128)} custom-call(s32[8]{0:T(128)} %stack.31.place, bf16[64,1024]{1,0:T(8,128)(2,1)} %get-tuple-element.37.value_ref, bf16[128,1024]{1,0:T(8,128)(2,1)} %get-tuple-element.46.low_ref), custom_call_target="tpu_custom_call" | custom-call | tf_op jit(solution)/shard_map/low/pallas_call | solution.py:37
  58.2 1.2 collective-permute-done.31
  59.4 1.6 collective-permute-start.30
  61.6 0.7 copy-done.1
  62.5 2.6 %first.1 = (bf16[32,1024]{1,0:T(8,128)(2,1)}, bf16[32,1024]{1,0:T(8,128)(2,1)}) custom-call(s32[8]{0:T(128)} %stack.31.place, bf16[64,1024]{1,0:T(8,128)(2,1)} %get-tuple-element.37.value_ref, bf16[192,1024]{1,0:T(8,128)(2,1)} %get-tuple-element.40.u0, bf16[192,1024]{1,0:T(8,128)(2,1)} %copy-done.2, bf16[192,1024]{1,0:T(8,128)(2,1)} %get-tuple-element.42.m0, ...), custom_call_target="tpu_custom_call" | custom-call | tf_op jit(solution)/shard_map/first/pallas_call | solution.py:37
  65.1 1.5 collective-permute-start.11
  67.2 2.4 %collective-permute-done.11 = bf16[32,1024]{1,0:T(8,128)(2,1)S(1)} collective-permute-done((bf16[32,1024]{1,0:T(8,128)(2,1)}, bf16[32,1024]{1,0:T(8,128)(2,1)S(1)}, u32[]{:S(2)}, u32[]{:S(2)}) %collective-permute-start.11) | collective-permute-done | bytes 65568 | tf_op jit(solution)/shard_map/ppermute | solution.py:328
  69.6 0.9 add_convert_fusion.17.a0
  71.4 0.9 add_convert_fusion.16.a1
  72.3 1.2 collective-permute-start.14
  73.5 1.0 collective-permute-start.35
  74.4 0.9 collective-permute-done.13.b0
  75.6 1.0 collective-permute-done.14.b1
  77.2 2.8 %second.1 = (bf16[64,1024]{1,0:T(8,128)(2,1)}, bf16[32,1024]{1,0:T(8,128)(2,1)}, bf16[32,1024]{1,0:T(8,128)(2,1)}) custom-call(s32[8]{0:T(128)} %stack.31.place, bf16[32,1024]{1,0:T(8,128)(2,1)} %copy-done.12, bf16[32,1024]{1,0:T(8,128)(2,1)} %copy-done.15, bf16[32,1024]{1,0:T(8,128)(2,1)} %copy-done.35, bf16[32,1024]{1,0:T(8,128)(2,1)} %copy-done.38, ...), custom_call_target="tpu_custom_call" | custom-call | tf_op jit(solution)/shard_map/second/pallas_call | solution.py:37
  80.0 1.1 collective-permute-start.15
  81.1 2.1 %low.5 = f32[64,1024]{1,0:T(8,128)} custom-call(s32[8]{0:T(128)} %stack.31.place, bf16[64,1024]{1,0:T(8,128)(2,1)} %get-tuple-element.49.value_ref, bf16[128,1024]{1,0:T(8,128)(2,1)} %get-tuple-element.46.low_ref), custom_call_target="tpu_custom_call" | custom-call | tf_op jit(solution)/shard_map/low/pallas_call | solution.py:37
  83.2 1.5 collective-permute-start.16
  84.8 0.9 add_convert_fusion.15.a0
  85.7 0.9 collective-permute-start.17
  86.6 1.1 collective-permute-done.16
  87.7 0.9 add_convert_fusion.14.a1
  88.6 1.0 collective-permute-start.18
  90.0 3.1 %collective-permute-done.18.b1 = bf16[32,1024]{1,0:T(8,128)(2,1)S(1)} collective-permute-done((bf16[32,1024]{1,0:T(8,128)(2,1)S(1)}, bf16[32,1024]{1,0:T(8,128)(2,1)S(1)}, u32[]{:S(2)}, u32[]{:S(2)}) %collective-permute-start.18) | collective-permute-done | bytes 65568 | tf_op jit(solution)/shard_map/ppermute | solution.py:328
  93.7 2.8 %third.1 = (bf16[64,1024]{1,0:T(8,128)(2,1)}, bf16[32,1024]{1,0:T(8,128)(2,1)}, bf16[32,1024]{1,0:T(8,128)(2,1)}) custom-call(s32[8]{0:T(128)} %stack.31.place, bf16[32,1024]{1,0:T(8,128)(2,1)} %copy-done.14, bf16[32,1024]{1,0:T(8,128)(2,1)} %copy-done.16, bf16[32,1024]{1,0:T(8,128)(2,1)} %copy-done.37, bf16[32,1024]{1,0:T(8,128)(2,1)} %copy-done.39, ...), custom_call_target="tpu_custom_call" | custom-call | tf_op jit(solution)/shard_map/third/pallas_call | solution.py:37
  96.5 1.1 collective-permute-start.19
  97.7 1.0 collective-permute-start.36
  98.7 1.1 collective-permute-start.20
  99.8 1.2 collective-permute-done.19
  101.0 0.9 add_convert_fusion.13.a0
  101.8 1.6 collective-permute-start.21
  103.4 0.7 collective-permute-done.20
  104.1 0.9 add_convert_fusion.12.a1
  105.0 1.0 collective-permute-start.22
  106.1 1.2 collective-permute-start.38
  107.3 2.1 %low.6 = f32[64,1024]{1,0:T(8,128)} custom-call(s32[8]{0:T(128)} %stack.31.place, bf16[64,1024]{1,0:T(8,128)(2,1)} %get-tuple-element.52.value_ref, bf16[128,1024]{1,0:T(8,128)(2,1)} %get-tuple-element.46.low_ref), custom_call_target="tpu_custom_call" | custom-call | tf_op jit(solution)/shard_map/low/pallas_call | solution.py:37
  110.6 5.6 %basis.1 = (bf16[64,1024]{1,0:T(8,128)(2,1)}, bf16[32,1024]{1,0:T(8,128)(2,1)}, bf16[32,1024]{1,0:T(8,128)(2,1)}) custom-call(s32[8]{0:T(128)} %stack.31.place, bf16[32,1024]{1,0:T(8,128)(2,1)} %copy-done.11, bf16[32,1024]{1,0:T(8,128)(2,1)} %copy-done.13, bf16[32,1024]{1,0:T(8,128)(2,1)} %copy-done.34, bf16[32,1024]{1,0:T(8,128)(2,1)} %copy-done.36, ...), custom_call_target="tpu_custom_call" | custom-call | tf_op jit(solution)/shard_map/basis/pallas_call | solution.py:37
  116.3 1.0 collective-permute-start.24
  117.3 1.5 collective-permute-start.25
  119.0 1.8 collective-permute-done.24
  120.9 1.0 collective-permute-start.26
  121.9 1.6 collective-permute-start.27
  123.5 2.1 %low.7 = f32[64,1024]{1,0:T(8,128)} custom-call(s32[8]{0:T(128)} %stack.31.place, bf16[64,1024]{1,0:T(8,128)(2,1)} %get-tuple-element.53.value_ref.basis_own, bf16[128,1024]{1,0:T(8,128)(2,1)} %get-tuple-element.46.low_ref), custom_call_target="tpu_custom_call" | custom-call | tf_op jit(solution)/shard_map/low/pallas_call | solution.py:37
  126.3 11.9 %factor0.1 = (f32[256,256]{1,0:T(8,128)}, bf16[1024,256]{1,0:T(8,128)(2,1)}, bf16[256,256]{1,0:T(8,128)(2,1)}) custom-call(s32[8]{0:T(128)} %stack.31.place, bf16[512,256]{1,0:T(8,128)(2,1)} %copy-done.5, bf16[512,256]{1,0:T(8,128)(2,1)} %copy-done.17), custom_call_target="tpu_custom_call" | custom-call | tf_op jit(solution)/shard_map/factor0/pallas_call | solution.py:37
  138.2 0.8 copy-done.4
  138.9 11.7 %factor1.1 = (f32[256,256]{1,0:T(8,128)}, bf16[768,256]{1,0:T(8,128)(2,1)}, bf16[256,256]{1,0:T(8,128)(2,1)}) custom-call(s32[8]{0:T(128)} %stack.31.place, bf16[768,256]{1,0:T(8,128)(2,1)} %copy-done.3, bf16[768,256]{1,0:T(8,128)(2,1)} %copy-done.4, bf16[1024,256]{1,0:T(8,128)(2,1)} %get-tuple-element.58.refs_0_), custom_call_target="tpu_custom_call" | custom-call | tf_op jit(solution)/shard_map/factor1/pallas_call | solution.py:37
  150.7 12.1 %factor2.1 = (f32[256,256]{1,0:T(8,128)}, bf16[512,256]{1,0:T(8,128)(2,1)}, bf16[256,256]{1,0:T(8,128)(2,1)}) custom-call(s32[8]{0:T(128)} %stack.31.place, bf16[768,256]{1,0:T(8,128)(2,1)} %copy-done.3, bf16[768,256]{1,0:T(8,128)(2,1)} %copy-done.4, bf16[1024,256]{1,0:T(8,128)(2,1)} %get-tuple-element.58.refs_0_, bf16[768,256]{1,0:T(8,128)(2,1)} %get-tuple-element.61.refs_1_), custom_call_target="tpu_custom_call" | custom-call | tf_op jit(solution)/shard_map/factor2/pallas_call | solution.py:37
  162.8 11.8 %factor3.1 = (f32[256,256]{1,0:T(8,128)}, bf16[256,256]{1,0:T(8,128)(2,1)}, bf16[256,256]{1,0:T(8,128)(2,1)}) custom-call(s32[8]{0:T(128)} %stack.31.place, bf16[768,256]{1,0:T(8,128)(2,1)} %copy-done.3, bf16[768,256]{1,0:T(8,128)(2,1)} %copy-done.4, bf16[1024,256]{1,0:T(8,128)(2,1)} %get-tuple-element.58.refs_0_, ...), custom_call_target="tpu_custom_call" | custom-call | tf_op jit(solution)/shard_map/factor3/pallas_call | solution.py:37
  175.2 3.2 %solve.1.solved_own = bf16[64,1024]{1,0:T(8,128)(2,1)} custom-call(s32[8]{0:T(128)} %stack.31.place, bf16[32,1024]{1,0:T(8,128)(2,1)} %copy-done.9, bf16[32,1024]{1,0:T(8,128)(2,1)} %copy-done.10, bf16[32,1024]{1,0:T(8,128)(2,1)} %copy-done.31, bf16[32,1024]{1,0:T(8,128)(2,1)} %copy-done.33, f32[64,1024]{1,0:T(8,128)} %low.7, ...), custom_call_target="tpu_custom_call" | custom-call | tf_op jit(solution)/shard_map/solve/pallas_call | solution.py:37
  178.9 1.1 pad_maximum_fusion
  181.3 2.3 %finish.1 = f32[2,1024,128]{2,1,0:T(8,128)} custom-call(s32[8]{0:T(128)} %stack.31.place, bf16[64,1024]{1,0:T(8,128)(2,1)} %get-tuple-element.53.value_ref.basis_own, bf16[64,1024]{1,0:T(8,128)(2,1)} %copy-done.22, bf16[64,1024]{1,0:T(8,128)(2,1)} %solve.1.solved_own, bf16[64,1024]{1,0:T(8,128)(2,1)} %copy-done.23), custom_call_target="tpu_custom_call" | custom-call | tf_op jit(solution)/shard_map/finish/pallas_call | solution.py:37
  (146 shorter events, 14.8 us)
Async XLA Ops:
  5.7 10.0 %collective-permute-start.5 = (bf16[256,128]{1,0:T(8,128)(2,1)}, bf16[256,128]{1,0:T(8,128)(2,1)S(1)}, u32[]{:S(2)}, u32[]{:S(2)}) collective-permute-start(bf16[256,128]{1,0:T(8,128)(2,1)} %get-tuple-element.39.refs_4_), channel_id=1, source_target_pairs={{0,3},{1,0},{2,1},{3,2},{4,7},{5,4},{6,5},{7,6},{8,11},{9,8},{10,9... | collective-permute-start | bytes 196616 | tf_op jit(solution)/shard_map/ppermute | solution.py:332
  10.7 16.9 %collective-permute-start.2 = (bf16[256,256]{1,0:T(8,128)(2,1)}, bf16[256,256]{1,0:T(8,128)(2,1)S(1)}, u32[]{:S(2)}, u32[]{:S(2)}) collective-permute-start(bf16[256,256]{1,0:T(8,128)(2,1)} %get-tuple-element.38.refs_0_), channel_id=1, source_target_pairs={{0,3},{1,0},{2,1},{3,2},{4,7},{5,4},{6,5},{7,6},{8,11},{9,8},{10,9... | collective-permute-start | bytes 393224 | tf_op jit(solution)/shard_map/ppermute | solution.py:332
  11.2 16.5 %collective-permute-start.1 = (bf16[256,256]{1,0:T(8,128)(2,1)}, bf16[256,256]{1,0:T(8,128)(2,1)S(1)}, u32[]{:S(2)}, u32[]{:S(2)}) collective-permute-start(bf16[256,256]{1,0:T(8,128)(2,1)} %get-tuple-element.38.refs_0_), channel_id=1, source_target_pairs={{0,2},{1,3},{2,0},{3,1},{4,6},{5,7},{6,4},{7,5},{8,10},{9,11},{10,... | collective-permute-start | bytes 393224 | tf_op jit(solution)/shard_map/ppermute | solution.py:332
  11.2 16.5 %collective-permute-start = (bf16[256,256]{1,0:T(8,128)(2,1)}, bf16[256,256]{1,0:T(8,128)(2,1)S(1)}, u32[]{:S(2)}, u32[]{:S(2)}) collective-permute-start(bf16[256,256]{1,0:T(8,128)(2,1)} %get-tuple-element.38.refs_0_), channel_id=1, source_target_pairs={{0,1},{1,2},{2,3},{3,0},{4,5},{5,6},{6,7},{7,4},{8,9},{9,10},{10,1... | collective-permute-start | bytes 393224 | tf_op jit(solution)/shard_map/ppermute | solution.py:332
  12.8 14.9 %collective-permute-start.4 = (bf16[256,128]{1,0:T(8,128)(2,1)}, bf16[256,128]{1,0:T(8,128)(2,1)S(1)}, u32[]{:S(2)}, u32[]{:S(2)}) collective-permute-start(bf16[256,128]{1,0:T(8,128)(2,1)} %get-tuple-element.39.refs_4_), channel_id=1, source_target_pairs={{0,2},{1,3},{2,0},{3,1},{4,6},{5,7},{6,4},{7,5},{8,10},{9,11},{10,... | collective-permute-start | bytes 196616 | tf_op jit(solution)/shard_map/ppermute | solution.py:332
  15.7 12.0 %copy-start.40 = (bf16[256,128]{1,0:T(8,128)(2,1)}, bf16[256,128]{1,0:T(8,128)(2,1)S(1)}, u32[]{:S(2)}) copy-start(bf16[256,128]{1,0:T(8,128)(2,1)S(1)} %collective-permute-done.5.refs_7_) | copy-start | bytes 196612
  15.7 11.9 %collective-permute-start.3 = (bf16[256,128]{1,0:T(8,128)(2,1)}, bf16[256,128]{1,0:T(8,128)(2,1)S(1)}, u32[]{:S(2)}, u32[]{:S(2)}) collective-permute-start(bf16[256,128]{1,0:T(8,128)(2,1)} %get-tuple-element.39.refs_4_), channel_id=1, source_target_pairs={{0,1},{1,2},{2,3},{3,0},{4,5},{5,6},{6,7},{7,4},{8,9},{9,10},{10,1... | collective-permute-start | bytes 196616 | tf_op jit(solution)/shard_map/ppermute | solution.py:332
  32.5 19.0 %copy-start.43 = (bf16[768,256]{1,0:T(8,128)(2,1)S(1)}, bf16[768,256]{1,0:T(8,128)(2,1)}, u32[]{:S(2)}) copy-start(bf16[768,256]{1,0:T(8,128)(2,1)} %get-tuple-element.60) | copy-start | bytes 1179652
  32.6 19.5 %copy-start = (bf16[192,1024]{1,0:T(8,128)(2,1)S(1)}, bf16[192,1024]{1,0:T(8,128)(2,1)}, u32[]{:S(2)}) copy-start(bf16[192,1024]{1,0:T(8,128)(2,1)} %get-tuple-element.40.u0) | copy-start | bytes 1179652
  32.6 19.6 %copy-start.8 = (bf16[512,256]{1,0:T(8,128)(2,1)S(1)}, bf16[512,256]{1,0:T(8,128)(2,1)}, u32[]{:S(2)}) copy-start(bf16[512,256]{1,0:T(8,128)(2,1)} %get-tuple-element.56) | copy-start | bytes 786436
  32.6 19.6 %collective-permute-start.28 = (bf16[512,256]{1,0:T(8,128)(2,1)}, bf16[512,256]{1,0:T(8,128)(2,1)S(1)}, u32[]{:S(2)}, u32[]{:S(2)}) collective-permute-start(bf16[512,256]{1,0:T(8,128)(2,1)} %get-tuple-element.57), channel_id=1, source_target_pairs={{0,4},{4,0},{8,12},{12,8},{16,20},{20,16},{24,28},{28,24},{1,5},{5... | collective-permute-start | bytes 786440 | tf_op jit(solution)/shard_map/ppermute | solution.py:325
  32.6 6.7 %collective-permute-start.9 = (bf16[192,256]{1,0:T(8,128)(2,1)}, bf16[192,256]{1,0:T(8,128)(2,1)S(1)}, u32[]{:S(2)}, u32[]{:S(2)}) collective-permute-start(bf16[192,256]{1,0:T(8,128)(2,1)} %get-tuple-element.41.refs_0_), channel_id=1, source_target_pairs={{0,3},{1,0},{2,1},{3,2},{4,7},{5,4},{6,5},{7,6},{8,11},{9,8},{10,9... | collective-permute-start | bytes 294920 | tf_op jit(solution)/shard_map/ppermute | solution.py:332
  35.8 10.3 %collective-permute-start.8 = (bf16[192,256]{1,0:T(8,128)(2,1)}, bf16[192,256]{1,0:T(8,128)(2,1)S(1)}, u32[]{:S(2)}, u32[]{:S(2)}) collective-permute-start(bf16[192,256]{1,0:T(8,128)(2,1)} %get-tuple-element.41.refs_0_), channel_id=1, source_target_pairs={{0,2},{1,3},{2,0},{3,1},{4,6},{5,7},{6,4},{7,5},{8,10},{9,11},{10,... | collective-permute-start | bytes 294920 | tf_op jit(solution)/shard_map/ppermute | solution.py:332
  36.2 9.9 %collective-permute-start.7 = (bf16[192,256]{1,0:T(8,128)(2,1)}, bf16[192,256]{1,0:T(8,128)(2,1)S(1)}, u32[]{:S(2)}, u32[]{:S(2)}) collective-permute-start(bf16[192,256]{1,0:T(8,128)(2,1)} %get-tuple-element.41.refs_0_), channel_id=1, source_target_pairs={{0,1},{1,2},{2,3},{3,0},{4,5},{5,6},{6,7},{7,4},{8,9},{9,10},{10,1... | collective-permute-start | bytes 294920 | tf_op jit(solution)/shard_map/ppermute | solution.py:332
  39.3 6.8 %copy-start.27 = (bf16[192,256]{1,0:T(8,128)(2,1)}, bf16[192,256]{1,0:T(8,128)(2,1)S(1)}, u32[]{:S(2)}) copy-start(bf16[192,256]{1,0:T(8,128)(2,1)S(1)} %collective-permute-done.9.refs_3_) | copy-start | bytes 294916
  51.6 10.0 %collective-permute-start.10 = (bf16[192,1024]{1,0:T(8,128)(2,1)}, bf16[192,1024]{1,0:T(8,128)(2,1)S(1)}, u32[]{:S(2)}, u32[]{:S(2)}) collective-permute-start(bf16[192,1024]{1,0:T(8,128)(2,1)} %get-tuple-element.43), channel_id=1, source_target_pairs={{0,4},{4,0},{8,12},{12,8},{16,20},{20,16},{24,28},{28,24},{1,5},{5... | collective-permute-start | bytes 1179656 | tf_op jit(solution)/shard_map/ppermute | solution.py:325
  51.6 15.5 %collective-permute-start.34 = (bf16[768,256]{1,0:T(8,128)(2,1)S(1)}, bf16[768,256]{1,0:T(8,128)(2,1)S(1)}, u32[]{:S(2)}, u32[]{:S(2)}) collective-permute-start(bf16[768,256]{1,0:T(8,128)(2,1)S(1)} %copy-done.43), channel_id=1, source_target_pairs={{0,4},{4,0},{8,12},{12,8},{16,20},{20,16},{24,28},{28,24},{1,5},{5... | collective-permute-start | bytes 1179656 | tf_op jit(solution)/shard_map/ppermute | solution.py:325
  52.1 9.5 %collective-permute-start.6 = (bf16[192,1024]{1,0:T(8,128)(2,1)S(1)}, bf16[192,1024]{1,0:T(8,128)(2,1)S(1)}, u32[]{:S(2)}, u32[]{:S(2)}) collective-permute-start(bf16[192,1024]{1,0:T(8,128)(2,1)S(1)} %copy-done), channel_id=1, source_target_pairs={{0,4},{4,0},{8,12},{12,8},{16,20},{20,16},{24,28},{28,24},{1,5},{5... | collective-permute-start | bytes 1179656 | tf_op jit(solution)/shard_map/ppermute | solution.py:325
  52.2 5.9 %collective-permute-start.29 = (bf16[256,256]{1,0:T(8,128)(2,1)S(1)}, bf16[256,256]{1,0:T(8,128)(2,1)S(1)}, u32[]{:S(2)}, u32[]{:S(2)}) collective-permute-start(bf16[256,256]{1,0:T(8,128)(2,1)S(1)} %get-tuple-element.78), channel_id=1, source_target_pairs={{0,8},{4,12},{8,0},{12,4},{16,24},{20,28},{24,16},{28,20},{1,9},{5... | collective-permute-start | bytes 393224 | tf_op jit(solution)/shard_map/ppermute | solution.py:328
  53.8 5.6 %collective-permute-start.31 = (bf16[256,256]{1,0:T(8,128)(2,1)S(1)}, bf16[256,256]{1,0:T(8,128)(2,1)S(1)}, u32[]{:S(2)}, u32[]{:S(2)}) collective-permute-start(bf16[256,256]{1,0:T(8,128)(2,1)S(1)} %get-tuple-element.79), channel_id=1, source_target_pairs={{0,16},{4,20},{8,24},{12,28},{16,0},{20,4},{24,8},{28,12},{1,17},{... | collective-permute-start | bytes 393224 | tf_op jit(solution)/shard_map/ppermute | solution.py:328
  55.3 11.8 %copy-start.7 = (bf16[768,256]{1,0:T(8,128)(2,1)S(1)}, bf16[768,256]{1,0:T(8,128)(2,1)}, u32[]{:S(2)}) copy-start(bf16[768,256]{1,0:T(8,128)(2,1)} %get-tuple-element.59) | copy-start | bytes 1179652
  59.4 23.8 %collective-permute-start.30 = (bf16[256,256]{1,0:T(8,128)(2,1)S(1)}, bf16[256,256]{1,0:T(8,128)(2,1)S(1)}, u32[]{:S(2)}, u32[]{:S(2)}) collective-permute-start(bf16[256,256]{1,0:T(8,128)(2,1)S(1)} %get-tuple-element.76), channel_id=1, source_target_pairs={{0,16},{4,20},{8,24},{12,28},{16,0},{20,4},{24,8},{28,12},{1,17},{... | collective-permute-start | bytes 393224 | tf_op jit(solution)/shard_map/ppermute | solution.py:328
  61.0 28.5 %collective-permute-start.32 = (bf16[256,256]{1,0:T(8,128)(2,1)S(1)}, bf16[256,256]{1,0:T(8,128)(2,1)S(1)}, u32[]{:S(2)}, u32[]{:S(2)}) collective-permute-start(bf16[256,256]{1,0:T(8,128)(2,1)S(1)} %get-tuple-element.77), channel_id=1, source_target_pairs={{0,8},{4,12},{8,0},{12,4},{16,24},{20,28},{24,16},{28,20},{1,9},{5... | collective-permute-start | bytes 393224 | tf_op jit(solution)/shard_map/ppermute | solution.py:328
  65.1 4.5 %collective-permute-start.11 = (bf16[32,1024]{1,0:T(8,128)(2,1)}, bf16[32,1024]{1,0:T(8,128)(2,1)S(1)}, u32[]{:S(2)}, u32[]{:S(2)}) collective-permute-start(bf16[32,1024]{1,0:T(8,128)(2,1)} %get-tuple-element.44), channel_id=1, source_target_pairs={{0,8},{4,12},{8,0},{12,4},{16,24},{20,28},{24,16},{28,20},{1,9},{5... | collective-permute-start | bytes 196616 | tf_op jit(solution)/shard_map/ppermute | solution.py:328
  66.6 4.8 %collective-permute-start.12 = (bf16[32,1024]{1,0:T(8,128)(2,1)}, bf16[32,1024]{1,0:T(8,128)(2,1)S(1)}, u32[]{:S(2)}, u32[]{:S(2)}) collective-permute-start(bf16[32,1024]{1,0:T(8,128)(2,1)} %get-tuple-element.45), channel_id=1, source_target_pairs={{0,16},{4,20},{8,24},{12,28},{16,0},{20,4},{24,8},{28,12},{1,17},{... | collective-permute-start | bytes 196616 | tf_op jit(solution)/shard_map/ppermute | solution.py:328
  70.4 6.2 %copy-start.12 = (bf16[32,1024]{1,0:T(8,128)(2,1)}, bf16[32,1024]{1,0:T(8,128)(2,1)S(1)}, u32[]{:S(2)}) copy-start(bf16[32,1024]{1,0:T(8,128)(2,1)S(1)} %add_convert_fusion.17.a0) | copy-start | bytes 196612
  70.4 4.9 %collective-permute-start.13 = (bf16[32,1024]{1,0:T(8,128)(2,1)S(1)}, bf16[32,1024]{1,0:T(8,128)(2,1)S(1)}, u32[]{:S(2)}, u32[]{:S(2)}) collective-permute-start(bf16[32,1024]{1,0:T(8,128)(2,1)S(1)} %add_convert_fusion.17.a0), channel_id=1, source_target_pairs={{0,16},{4,20},{8,24},{12,28},{16,0},{20,4},{24,8},{28,12},{1,17},{... | collective-permute-start | bytes 196616 | tf_op jit(solution)/shard_map/ppermute | solution.py:328
  72.2 4.3 %copy-start.15 = (bf16[32,1024]{1,0:T(8,128)(2,1)}, bf16[32,1024]{1,0:T(8,128)(2,1)S(1)}, u32[]{:S(2)}) copy-start(bf16[32,1024]{1,0:T(8,128)(2,1)S(1)} %add_convert_fusion.16.a1) | copy-start | bytes 196612
  72.3 4.3 %collective-permute-start.14 = (bf16[32,1024]{1,0:T(8,128)(2,1)S(1)}, bf16[32,1024]{1,0:T(8,128)(2,1)S(1)}, u32[]{:S(2)}, u32[]{:S(2)}) collective-permute-start(bf16[32,1024]{1,0:T(8,128)(2,1)S(1)} %add_convert_fusion.16.a1), channel_id=1, source_target_pairs={{0,8},{4,12},{8,0},{12,4},{16,24},{20,28},{24,16},{28,20},{1,9},{5... | collective-permute-start | bytes 196616 | tf_op jit(solution)/shard_map/ppermute | solution.py:328
  73.5 24.1 %collective-permute-start.35 = (bf16[384,256]{1,0:T(8,128)(2,1)S(1)}, bf16[384,256]{1,0:T(8,128)(2,1)S(1)}, u32[]{:S(2)}, u32[]{:S(2)}) collective-permute-start(bf16[384,256]{1,0:T(8,128)(2,1)S(1)} %get-tuple-element.74), channel_id=1, source_target_pairs={{0,8},{4,12},{8,0},{12,4},{16,24},{20,28},{24,16},{28,20},{1,9},{5... | collective-permute-start | bytes 589832 | tf_op jit(solution)/shard_map/ppermute | solution.py:328
  75.4 22.2 %collective-permute-start.37 = (bf16[384,256]{1,0:T(8,128)(2,1)S(1)}, bf16[384,256]{1,0:T(8,128)(2,1)S(1)}, u32[]{:S(2)}, u32[]{:S(2)}) collective-permute-start(bf16[384,256]{1,0:T(8,128)(2,1)S(1)} %get-tuple-element.75), channel_id=1, source_target_pairs={{0,16},{4,20},{8,24},{12,28},{16,0},{20,4},{24,8},{28,12},{1,17},{... | collective-permute-start | bytes 589832 | tf_op jit(solution)/shard_map/ppermute | solution.py:328
  80.0 4.8 %collective-permute-start.15 = (bf16[32,1024]{1,0:T(8,128)(2,1)}, bf16[32,1024]{1,0:T(8,128)(2,1)S(1)}, u32[]{:S(2)}, u32[]{:S(2)}) collective-permute-start(bf16[32,1024]{1,0:T(8,128)(2,1)} %get-tuple-element.47), channel_id=1, source_target_pairs={{0,8},{4,12},{8,0},{12,4},{16,24},{20,28},{24,16},{28,20},{1,9},{5... | collective-permute-start | bytes 196616 | tf_op jit(solution)/shard_map/ppermute | solution.py:328
  83.2 4.5 %collective-permute-start.16 = (bf16[32,1024]{1,0:T(8,128)(2,1)}, bf16[32,1024]{1,0:T(8,128)(2,1)S(1)}, u32[]{:S(2)}, u32[]{:S(2)}) collective-permute-start(bf16[32,1024]{1,0:T(8,128)(2,1)} %get-tuple-element.48), channel_id=1, source_target_pairs={{0,16},{4,20},{8,24},{12,28},{16,0},{20,4},{24,8},{28,12},{1,17},{... | collective-permute-start | bytes 196616 | tf_op jit(solution)/shard_map/ppermute | solution.py:328
  85.6 7.4 %copy-start.14 = (bf16[32,1024]{1,0:T(8,128)(2,1)}, bf16[32,1024]{1,0:T(8,128)(2,1)S(1)}, u32[]{:S(2)}) copy-start(bf16[32,1024]{1,0:T(8,128)(2,1)S(1)} %add_convert_fusion.15.a0) | copy-start | bytes 196612
  85.7 4.3 %collective-permute-start.17 = (bf16[32,1024]{1,0:T(8,128)(2,1)S(1)}, bf16[32,1024]{1,0:T(8,128)(2,1)S(1)}, u32[]{:S(2)}, u32[]{:S(2)}) collective-permute-start(bf16[32,1024]{1,0:T(8,128)(2,1)S(1)} %add_convert_fusion.15.a0), channel_id=1, source_target_pairs={{0,16},{4,20},{8,24},{12,28},{16,0},{20,4},{24,8},{28,12},{1,17},{... | collective-permute-start | bytes 196616 | tf_op jit(solution)/shard_map/ppermute | solution.py:328
  88.5 4.5 %copy-start.16 = (bf16[32,1024]{1,0:T(8,128)(2,1)}, bf16[32,1024]{1,0:T(8,128)(2,1)S(1)}, u32[]{:S(2)}) copy-start(bf16[32,1024]{1,0:T(8,128)(2,1)S(1)} %add_convert_fusion.14.a1) | copy-start | bytes 196612
  88.6 4.5 %collective-permute-start.18 = (bf16[32,1024]{1,0:T(8,128)(2,1)S(1)}, bf16[32,1024]{1,0:T(8,128)(2,1)S(1)}, u32[]{:S(2)}, u32[]{:S(2)}) collective-permute-start(bf16[32,1024]{1,0:T(8,128)(2,1)S(1)} %add_convert_fusion.14.a1), channel_id=1, source_target_pairs={{0,8},{4,12},{8,0},{12,4},{16,24},{20,28},{24,16},{28,20},{1,9},{5... | collective-permute-start | bytes 196616 | tf_op jit(solution)/shard_map/ppermute | solution.py:328
  96.5 4.5 %collective-permute-start.19 = (bf16[32,1024]{1,0:T(8,128)(2,1)}, bf16[32,1024]{1,0:T(8,128)(2,1)S(1)}, u32[]{:S(2)}, u32[]{:S(2)}) collective-permute-start(bf16[32,1024]{1,0:T(8,128)(2,1)} %get-tuple-element.50), channel_id=1, source_target_pairs={{0,8},{4,12},{8,0},{12,4},{16,24},{20,28},{24,16},{28,20},{1,9},{5... | collective-permute-start | bytes 196616 | tf_op jit(solution)/shard_map/ppermute | solution.py:328
  97.7 21.1 %collective-permute-start.36 = (bf16[384,256]{1,0:T(8,128)(2,1)S(1)}, bf16[384,256]{1,0:T(8,128)(2,1)S(1)}, u32[]{:S(2)}, u32[]{:S(2)}) collective-permute-start(bf16[384,256]{1,0:T(8,128)(2,1)S(1)} %get-tuple-element.72), channel_id=1, source_target_pairs={{0,16},{4,20},{8,24},{12,28},{16,0},{20,4},{24,8},{28,12},{1,17},{... | collective-permute-start | bytes 589832 | tf_op jit(solution)/shard_map/ppermute | solution.py:328
  98.7 5.5 %collective-permute-start.20 = (bf16[32,1024]{1,0:T(8,128)(2,1)}, bf16[32,1024]{1,0:T(8,128)(2,1)S(1)}, u32[]{:S(2)}, u32[]{:S(2)}) collective-permute-start(bf16[32,1024]{1,0:T(8,128)(2,1)} %get-tuple-element.51), channel_id=1, source_target_pairs={{0,16},{4,20},{8,24},{12,28},{16,0},{20,4},{24,8},{28,12},{1,17},{... | collective-permute-start | bytes 196616 | tf_op jit(solution)/shard_map/ppermute | solution.py:328
  101.8 7.7 %copy-start.11 = (bf16[32,1024]{1,0:T(8,128)(2,1)}, bf16[32,1024]{1,0:T(8,128)(2,1)S(1)}, u32[]{:S(2)}) copy-start(bf16[32,1024]{1,0:T(8,128)(2,1)S(1)} %add_convert_fusion.13.a0) | copy-start | bytes 196612
  101.8 7.6 %collective-permute-start.21 = (bf16[32,1024]{1,0:T(8,128)(2,1)S(1)}, bf16[32,1024]{1,0:T(8,128)(2,1)S(1)}, u32[]{:S(2)}, u32[]{:S(2)}) collective-permute-start(bf16[32,1024]{1,0:T(8,128)(2,1)S(1)} %add_convert_fusion.13.a0), channel_id=1, source_target_pairs={{0,16},{4,20},{8,24},{12,28},{16,0},{20,4},{24,8},{28,12},{1,17},{... | collective-permute-start | bytes 196616 | tf_op jit(solution)/shard_map/ppermute | solution.py:328
  105.0 4.5 %copy-start.13 = (bf16[32,1024]{1,0:T(8,128)(2,1)}, bf16[32,1024]{1,0:T(8,128)(2,1)S(1)}, u32[]{:S(2)}) copy-start(bf16[32,1024]{1,0:T(8,128)(2,1)S(1)} %add_convert_fusion.12.a1) | copy-start | bytes 196612
  105.0 4.5 %collective-permute-start.22 = (bf16[32,1024]{1,0:T(8,128)(2,1)S(1)}, bf16[32,1024]{1,0:T(8,128)(2,1)S(1)}, u32[]{:S(2)}, u32[]{:S(2)}) collective-permute-start(bf16[32,1024]{1,0:T(8,128)(2,1)S(1)} %add_convert_fusion.12.a1), channel_id=1, source_target_pairs={{0,8},{4,12},{8,0},{12,4},{16,24},{20,28},{24,16},{28,20},{1,9},{5... | collective-permute-start | bytes 196616 | tf_op jit(solution)/shard_map/ppermute | solution.py:328
  106.0 12.8 %copy-start.5 = (bf16[512,256]{1,0:T(8,128)(2,1)}, bf16[512,256]{1,0:T(8,128)(2,1)S(1)}, u32[]{:S(2)}) copy-start(bf16[512,256]{1,0:T(8,128)(2,1)S(1)} %pad_maximum_fusion.2.own_ref) | copy-start | bytes 786436
  106.0 19.6 %collective-permute-start.33 = (bf16[512,256]{1,0:T(8,128)(2,1)S(1)}, bf16[512,256]{1,0:T(8,128)(2,1)S(1)}, u32[]{:S(2)}, u32[]{:S(2)}) collective-permute-start(bf16[512,256]{1,0:T(8,128)(2,1)S(1)} %pad_maximum_fusion.2.own_ref), channel_id=1, source_target_pairs={{0,4},{4,0},{8,12},{12,8},{16,20},{20,16},{24,28},{28,24},{1,5},{5... | collective-permute-start | bytes 786440 | tf_op jit(solution)/shard_map/ppermute | solution.py:325
  106.1 12.8 %collective-permute-start.38 = (bf16[384,256]{1,0:T(8,128)(2,1)S(1)}, bf16[384,256]{1,0:T(8,128)(2,1)S(1)}, u32[]{:S(2)}, u32[]{:S(2)}) collective-permute-start(bf16[384,256]{1,0:T(8,128)(2,1)S(1)} %get-tuple-element.73), channel_id=1, source_target_pairs={{0,8},{4,12},{8,0},{12,4},{16,24},{20,28},{24,16},{28,20},{1,9},{5... | collective-permute-start | bytes 589832 | tf_op jit(solution)/shard_map/ppermute | solution.py:328
  116.3 4.6 %copy-start.32 = (bf16[32,1024]{1,0:T(8,128)(2,1)S(1)}, bf16[32,1024]{1,0:T(8,128)(2,1)}, u32[]{:S(2)}) copy-start(bf16[32,1024]{1,0:T(8,128)(2,1)} %get-tuple-element.54) | copy-start | bytes 196612
  116.3 5.6 %copy-start.30 = (bf16[32,1024]{1,0:T(8,128)(2,1)S(1)}, bf16[32,1024]{1,0:T(8,128)(2,1)}, u32[]{:S(2)}) copy-start(bf16[32,1024]{1,0:T(8,128)(2,1)} %get-tuple-element.55) | copy-start | bytes 196612
  116.3 9.3 %copy-start.6 = (bf16[64,1024]{1,0:T(8,128)(2,1)S(1)}, bf16[64,1024]{1,0:T(8,128)(2,1)}, u32[]{:S(2)}) copy-start(bf16[64,1024]{1,0:T(8,128)(2,1)} %get-tuple-element.53.value_ref.basis_own) | copy-start | bytes 393220
  116.3 4.5 %collective-permute-start.24 = (bf16[32,1024]{1,0:T(8,128)(2,1)}, bf16[32,1024]{1,0:T(8,128)(2,1)S(1)}, u32[]{:S(2)}, u32[]{:S(2)}) collective-permute-start(bf16[32,1024]{1,0:T(8,128)(2,1)} %get-tuple-element.54), channel_id=1, source_target_pairs={{0,8},{4,12},{8,0},{12,4},{16,24},{20,28},{24,16},{28,20},{1,9},{5... | collective-permute-start | bytes 196616 | tf_op jit(solution)/shard_map/ppermute | solution.py:328
  117.3 4.6 %collective-permute-start.25 = (bf16[32,1024]{1,0:T(8,128)(2,1)}, bf16[32,1024]{1,0:T(8,128)(2,1)S(1)}, u32[]{:S(2)}, u32[]{:S(2)}) collective-permute-start(bf16[32,1024]{1,0:T(8,128)(2,1)} %get-tuple-element.55), channel_id=1, source_target_pairs={{0,16},{4,20},{8,24},{12,28},{16,0},{20,4},{24,8},{28,12},{1,17},{... | collective-permute-start | bytes 196616 | tf_op jit(solution)/shard_map/ppermute | solution.py:328
  119.0 19.2 %copy-start.3 = (bf16[768,256]{1,0:T(8,128)(2,1)}, bf16[768,256]{1,0:T(8,128)(2,1)S(1)}, u32[]{:S(2)}) copy-start(bf16[768,256]{1,0:T(8,128)(2,1)S(1)} %pad_maximum_fusion.1.own_ref) | copy-start | bytes 1179652
  119.0 19.2 %collective-permute-start.39 = (bf16[768,256]{1,0:T(8,128)(2,1)S(1)}, bf16[768,256]{1,0:T(8,128)(2,1)S(1)}, u32[]{:S(2)}, u32[]{:S(2)}) collective-permute-start(bf16[768,256]{1,0:T(8,128)(2,1)S(1)} %pad_maximum_fusion.1.own_ref), channel_id=1, source_target_pairs={{0,4},{4,0},{8,12},{12,8},{16,20},{20,16},{24,28},{28,24},{1,5},{5... | collective-permute-start | bytes 1179656 | tf_op jit(solution)/shard_map/ppermute | solution.py:325
  120.8 41.9 %copy-start.9 = (bf16[32,1024]{1,0:T(8,128)(2,1)}, bf16[32,1024]{1,0:T(8,128)(2,1)S(1)}, u32[]{:S(2)}) copy-start(bf16[32,1024]{1,0:T(8,128)(2,1)S(1)} %add_convert_fusion.11.a0) | copy-start | bytes 196612
  120.9 53.7 %collective-permute-start.26 = (bf16[32,1024]{1,0:T(8,128)(2,1)S(1)}, bf16[32,1024]{1,0:T(8,128)(2,1)S(1)}, u32[]{:S(2)}, u32[]{:S(2)}) collective-permute-start(bf16[32,1024]{1,0:T(8,128)(2,1)S(1)} %add_convert_fusion.11.a0), channel_id=1, source_target_pairs={{0,16},{4,20},{8,24},{12,28},{16,0},{20,4},{24,8},{28,12},{1,17},{... | collective-permute-start | bytes 196616 | tf_op jit(solution)/shard_map/ppermute | solution.py:328
  121.9 40.9 %copy-start.10 = (bf16[32,1024]{1,0:T(8,128)(2,1)}, bf16[32,1024]{1,0:T(8,128)(2,1)S(1)}, u32[]{:S(2)}) copy-start(bf16[32,1024]{1,0:T(8,128)(2,1)S(1)} %add_convert_fusion.10.a1) | copy-start | bytes 196612
  121.9 52.7 %collective-permute-start.27 = (bf16[32,1024]{1,0:T(8,128)(2,1)S(1)}, bf16[32,1024]{1,0:T(8,128)(2,1)S(1)}, u32[]{:S(2)}, u32[]{:S(2)}) collective-permute-start(bf16[32,1024]{1,0:T(8,128)(2,1)S(1)} %add_convert_fusion.10.a1), channel_id=1, source_target_pairs={{0,8},{4,12},{8,0},{12,4},{16,24},{20,28},{24,16},{28,20},{1,9},{5... | collective-permute-start | bytes 196616 | tf_op jit(solution)/shard_map/ppermute | solution.py:328
  125.6 54.4 %collective-permute-start.23 = (bf16[64,1024]{1,0:T(8,128)(2,1)S(1)}, bf16[64,1024]{1,0:T(8,128)(2,1)S(1)}, u32[]{:S(2)}, u32[]{:S(2)}) collective-permute-start(bf16[64,1024]{1,0:T(8,128)(2,1)S(1)} %copy-done.6), channel_id=1, source_target_pairs={{0,4},{4,0},{8,12},{12,8},{16,20},{20,16},{24,28},{28,24},{1,5},{5... | collective-permute-start | bytes 393224 | tf_op jit(solution)/shard_map/ppermute | solution.py:325
  174.5 4.4 %copy-start.18 = (f32[256,256]{1,0:T(8,128)S(1)}, f32[256,256]{1,0:T(8,128)}, u32[]{:S(2)}) copy-start(f32[256,256]{1,0:T(8,128)} %get-tuple-element.68) | copy-start | bytes 786436
  174.5 4.4 %copy-start.19 = (f32[256,256]{1,0:T(8,128)S(1)}, f32[256,256]{1,0:T(8,128)}, u32[]{:S(2)}) copy-start(f32[256,256]{1,0:T(8,128)} %get-tuple-element.69) | copy-start | bytes 786436
  174.5 4.4 %copy-start.20 = (f32[256,256]{1,0:T(8,128)S(1)}, f32[256,256]{1,0:T(8,128)}, u32[]{:S(2)}) copy-start(f32[256,256]{1,0:T(8,128)} %get-tuple-element.70) | copy-start | bytes 786436
  174.5 4.4 %copy-start.21 = (f32[256,256]{1,0:T(8,128)S(1)}, f32[256,256]{1,0:T(8,128)}, u32[]{:S(2)}) copy-start(f32[256,256]{1,0:T(8,128)} %get-tuple-element.71) | copy-start | bytes 786436
  178.4 1.7 collective-permute-start.40
  (21 other events, 17.1 us)

commit v2 on v1

v2 whole, which is shorter than its diff:
```python
import functools

import jax
import jax.numpy as jnp
from jax import lax
from jax.experimental import pallas as pl
from jax.experimental.pallas import tpu as pltpu
from jax.sharding import PartitionSpec as P


f32 = jnp.float32
bf16 = jnp.bfloat16
WIDE = 256
HALF = 128
ROOM = 4 << 20
SMEM = pl.BlockSpec(memory_space=pltpu.SMEM)
VMEM = pl.BlockSpec(memory_space=pltpu.VMEM)


def nt(first, second, **kw):
    return lax.dot_general(
        first, second, (((1,), (1,)), ((), ())), preferred_element_type=f32, **kw
    )


def tn(first, second):
    return lax.dot_general(first, second, (((0,), (0,)), ((), ())), preferred_element_type=f32)


def nn(first, second, **kw):
    return jnp.dot(first, second, preferred_element_type=f32, **kw)


def shaped(shape, kind):
    return jax.ShapeDtypeStruct(shape, kind)


def held(shape, kind):
    size = jnp.dtype(kind).itemsize
    for length in shape:
        size *= length
    return size


def call(body, outs, *args, scratch=(), scalars=1):
    room = sum(held(v.shape, v.dtype) for v in [*args, *jax.tree.leaves(outs), *scratch])
    return pl.pallas_call(
        body,
        out_shape=outs,
        in_specs=[SMEM] * scalars + [VMEM] * (len(args) - scalars),
        out_specs=jax.tree.map(lambda _: VMEM, outs),
        scratch_shapes=[pltpu.VMEM(v.shape, v.dtype) for v in scratch],
        compiler_params=pltpu.CompilerParams(vmem_limit_bytes=room + ROOM),
    )(*args)


def eliminate(block, zero):
    size = block.shape[0]
    lane = lax.broadcasted_iota(jnp.int32, (8, size), 1)
    sub = lax.broadcasted_iota(jnp.int32, (8, size), 0)
    tiles = [block[8 * g : 8 * g + 8] for g in range(size // 8)]

    def spread(tile, j):
        return jnp.broadcast_to(tile[:, j : j + 1], (8, size))

    def lift(tile, i):
        return jnp.broadcast_to(tile[i : i + 1], (8, size))

    uppers, inverses = [], []
    for own in range(size // 8):
        base = 8 * own
        inside = (lane >= base) & (lane < base + 8)
        plain = tiles[own]
        cols = [spread(plain, base + j) + zero for j in range(8)]
        full = jnp.where(inside, jnp.where(lane == base + sub, 1.0, 0.0), plain)
        rows, up, diag, blocks = full, full, full, []
        for k in range(0, 8, 2):
            one, two = cols[k], cols[k + 1]
            a, b, c = lift(one, k), lift(one, k + 1), lift(two, k + 1)
            over = 1.0 / (a * c - b * b)
            ratio = b * (1.0 / a)
            pivots = (sub == k) | (sub == k + 1)
            first = jnp.where(pivots, 0.0, one * c - two * b)
            second = jnp.where(pivots, 0.0, two * a - one * b)

            def cleared(value):
                return value - over * (first * lift(value, k) + second * lift(value, k + 1))

            def kept(into, value):
                into = jnp.where(sub == k + 1, value - ratio * lift(value, k), into)
                return jnp.where(sub == k, value, into)

            rows, up = kept(rows, full), kept(up, plain)
            diag = jnp.where(sub == k, a, jnp.where(sub == k + 1, c - b * ratio, diag))
            for j in range(k + 2, 8):
                cols[j] = cleared(cols[j])
            full = cleared(full)
            if k < 6:
                plain = cleared(plain)
            blocks.append((a * over, b * over, c * over))
        weights = []
        for k in range(0, 8, 2):
            a, b, c = blocks[k // 2]
            one, two = lift(full, k), lift(full, k + 1)
            weights += [c * one - b * two, a * two - b * one]
        for g in range(own + 1, size // 8):
            rest = jnp.where(inside, 0.0, tiles[g])
            even = spread(tiles[g], base) * weights[0]
            odd = spread(tiles[g], base + 1) * weights[1]
            for j in range(2, 8, 2):
                even = even + spread(tiles[g], base + j) * weights[j]
                odd = odd + spread(tiles[g], base + j + 1) * weights[j + 1]
            tiles[g] = rest - (even + odd)
        root = lax.rsqrt(diag)
        inverses.append(jnp.where(lane <= sub + base, rows * root, 0.0))
        uppers.append(jnp.where(lane >= sub + base, up * root, 0.0))
    return jnp.concatenate(uppers, 0), jnp.concatenate(inverses, 0)


def put_corner(corner_ref, start, stop, out_ref, at):
    rows, slab = corner_ref.shape[0], out_ref.shape[1]
    for k in range(start // slab, stop // slab):
        out_ref[at : at + rows, :] = corner_ref[:, k * slab : (k + 1) * slab]
        at += rows


def left_body(place, row_ref, corner_ref, left_ref):
    count, slab, width = row_ref.shape
    half = width // 2
    per = max(slab // half, 1)
    for j in range(count):
        left_ref[j * half : (j + 1) * half, :] = row_ref[j].T[:half]
        right = row_ref[j, :, half:]
        top, at = count * half + (j // per) * half, (j % per) * half
        if j % per == 0:
            left_ref[top : top + half, :] = jnp.zeros((half, slab), bf16)
        left_ref[top : top + half, at : at + half] = tn(right, right).astype(bf16)
    put_corner(corner_ref, 0, WIDE, left_ref, (count + -(-count // per)) * half)


def right_body(place, row_ref, low_ref, corner_ref, right_ref, low_t_ref):
    count, _, width = row_ref.shape
    half = width // 2
    for j in range(count):
        right_ref[j * half : (j + 1) * half, :] = row_ref[j].T[half:]
    put_corner(corner_ref, WIDE, corner_ref.shape[1], right_ref, count * half)
    low_t_ref[...] = low_ref[place[0]].T


def diagonal_body(count, parts, place, *refs):
    lefts = refs[:parts]
    left_ref, own0_ref, own1_ref, away0_ref, away1_ref, total, turned = refs[parts:]
    slab = lefts[0].shape[1]
    half = turned.shape[0] // count
    per = max(slab // half, 1)
    core, z = place[0], place[1]
    for d in range(parts):
        source = lax.rem(z - d + parts, parts)
        left_ref[:, pl.ds(pl.multiple_of(source * slab, HALF), slab)] = lefts[d][: count * half]
    for j in range(count):
        rows = slice(j * half, (j + 1) * half)
        top, at = count * half + (j // per) * half, (j % per) * half
        core_sum = sum(lefts[d][top : top + half, at : at + half].astype(f32) for d in range(parts))
        turned[rows, :] = (-nn(core_sum.astype(bf16), left_ref[rows, :])).astype(bf16)
    total[...] = tn(turned[...], left_ref[...])
    order = total.shape[0]
    for out0, out1, side in ((own0_ref, own1_ref, core), (away0_ref, away1_ref, 1 - core)):
        fill = 0
        for g in range(order // WIDE):
            for b in range(g, order // WIDE):
                from_row = pl.multiple_of(b * WIDE + side * HALF, HALF)
                value = total[pl.ds(from_row, HALF), g * WIDE : (g + 1) * WIDE].astype(bf16)
                if g == 0:
                    out0[b * HALF : (b + 1) * HALF, :] = value
                else:
                    out1[fill : fill + HALF, :] = value
                    fill += HALF


def join_body(at, start, stop, place, own_ref, got_ref, *refs):
    shards, out_ref, acc = refs[:-2], refs[-2], refs[-1]
    z, chip, parts = place[1], place[2], len(shards)
    acc[...] = own_ref[...].astype(f32) + got_ref[...].astype(f32)
    slab = shards[0].shape[1]
    per, blocks = WIDE // slab, parts * slab // WIDE
    rows = (shards[0].shape[0] - at) // (per * (stop - start))
    for d in range(parts):
        block = lax.rem(z - d + parts, parts) // per
        base = 0
        for g in range(start, stop):

            @pl.when(block >= g)
            def _(base=base, g=g):
                into = pl.ds(pl.multiple_of(base + (block - g) * HALF + chip * rows, 8), rows)
                for k in range(per):
                    lanes = slice(k * slab, (k + 1) * slab)
                    top = at + ((g - start) * per + k) * rows
                    acc[into, lanes] = acc[into, lanes] + shards[d][top : top + rows, :].astype(f32)

            base += (blocks - g) * HALF
    out_ref[...] = acc[...].astype(bf16)


def factor_body(group, at, place, own_ref, other_ref, *refs):
    earlier = refs[:group]
    slab_ref, half_ref, inverse_ref, whole = refs[group:]
    core, z = place[0], place[1]
    order = whole.shape[0]
    first, wide = group * HALF, group * HALF // WIDE
    lanes = slice(first - wide * WIDE, first - wide * WIDE + HALF)
    blocks = []
    for r in range(group, order // HALF):
        rows = slice(at + (r // 2 - wide) * HALF, at + (r // 2 - wide + 1) * HALF)
        mine = own_ref[rows, lanes].astype(f32)
        blocks.append(jnp.where(core == r % 2, mine, other_ref[rows, lanes].astype(f32)))
    total = jnp.concatenate(blocks, axis=0)
    for h in range(group):
        skip = (group - h) * HALF
        total = total - nt(earlier[h][skip:, :], earlier[h][skip : skip + HALF, :])
    upper, inverse = eliminate(total[:HALF], place[4].astype(f32))
    inverse = inverse.astype(bf16)
    lower = upper.T
    if group:
        whole[:first, :] = jnp.zeros((first, HALF), f32)
    whole[first : first + HALF, :] = lower
    half_ref[:HALF, :] = lower.astype(bf16)
    inverse_ref[...] = inverse
    if first + HALF < order:
        under = nt(total[HALF:].astype(bf16), inverse)
        whole[first + HALF :, :] = under
        half_ref[HALF:, :] = under.astype(bf16)
    slab = slab_ref.shape[0]
    slab_ref[...] = whole[pl.ds(pl.multiple_of(z * slab, slab), slab), :]


def mixed_body(parts, place, mask_ref, *refs):
    rights, panel_ref = refs[:parts], refs[parts]
    own_ref, away_ref, right = refs[parts + 1 :]
    slab = rights[0].shape[1]
    core, z = place[0], place[1]
    for d in range(parts):
        source = lax.rem(z - d + parts, parts)
        right[:, pl.ds(pl.multiple_of(source * slab, HALF), slab)] = rights[d][: right.shape[0]]
    count, half = panel_ref.shape[1], panel_ref.shape[3] // 2
    for out, row in ((own_ref, core), (away_ref, 1 - core)):
        for j in range(count):
            rows = slice(j * half, (j + 1) * half)
            both = nn(right[rows, :], panel_ref[row, j])
            sign = -mask_ref[row, j].astype(f32)
            inner = (both[:, half:] * sign).astype(bf16)
            out[rows, :] = nt(inner, panel_ref[row, j, :, :half]).astype(bf16)


def apply_stage(value, inners, outers):
    total = None
    for inner, outer in zip(inners, outers):
        part = nn(nt(value, inner).astype(bf16), outer)
        total = part if total is None else total + part
    return total.astype(bf16)


def low_body(forward, place, value_ref, low_ref, out_ref):
    half = low_ref.shape[0] // 2
    up, down = low_ref[:half], low_ref[half:]
    inner, outer = (down, up) if forward else (up, down)
    out_ref[...] = nn(nt(value_ref[...], inner).astype(bf16), outer)


def first_body(place, value_ref, u0, u1, m0, m1, out_ref):
    out_ref[...] = apply_stage(value_ref[...], (u0[...], u1[...]), (m0[...], m1[...]))


def joined(own, got, low):
    return low[...] + (own[...].astype(f32) + got[...].astype(f32))


def middle_body(forward, place, own, got, low, u0, u1, m0, m1, value_ref, out_ref):
    ups, downs = (m0[...], m1[...]), (u0[...], u1[...])
    value = joined(own, got, low).astype(bf16)
    value_ref[...] = value
    inners, outers = (downs, ups) if forward else (ups, downs)
    out_ref[...] = apply_stage(value, inners, outers)


def basis_body(place, own, got, low, u0, u1, m0, m1, basis_ref, out_ref):
    third = joined(own, got, low)
    gram = nt(third, third, precision=lax.Precision.HIGHEST)
    _, inverse = eliminate(gram, place[4].astype(f32))
    basis = nn(inverse, third, precision=lax.Precision.HIGHEST).astype(bf16)
    basis_ref[...] = basis
    out_ref[...] = apply_stage(basis, (m0[...], m1[...]), (u0[...], u1[...]))


def solve_body(groups, place, basis, own, got, low, *refs):
    factors, inverses, out_ref = refs[:groups], refs[groups : 2 * groups], refs[2 * groups]
    rest = joined(own, got, low)
    rank = rest.shape[0]
    out_ref[:rank] = basis[...]
    for g in range(groups):
        solved = nt(rest[:, :HALF].astype(bf16), inverses[g][...]).astype(bf16)
        out_ref[rank:, g * HALF : (g + 1) * HALF] = solved
        if g < groups - 1:
            rest = rest[:, HALF:] - nt(solved, factors[g][HALF:, :])


def finish_body(place, own, other, out_ref):
    out_ref[place[0]] = own[...].astype(f32).T
    out_ref[1 - place[0]] = other[...].astype(f32).T


def after(value, *others):
    return lax.optimization_barrier((value, *others))[0]


def panel_step(panel, row_k, mask, a_low, a_diag, sketch):
    cols, parts = lax.axis_size("cols"), lax.axis_size("rows")
    here, z = lax.axis_index("cols"), lax.axis_index("rows")
    core, chip, chips = here % 2, here // 2, cols // 2
    count, slab, width = row_k.shape
    half = width // 2
    order, rank = sketch.shape
    groups = order // HALF
    partner = [(i, i ^ 1) for i in range(cols)]
    masks = [2 << i for i in range((cols // 2).bit_length() - 1)]
    place = jnp.stack([core, z, chip, here, here * 0]).astype(jnp.int32)

    def swap(value):
        return lax.ppermute(value, "cols", partner)

    def cross(value, step):
        bits = masks[step], masks[len(masks) - 1 - step]
        return lax.ppermute(value, "cols", [(i, i ^ bits[i % 2]) for i in range(cols)])

    def spread_rows(value):
        return [value] + [
            lax.ppermute(value, "rows", [(i, (i + d) % parts) for i in range(parts)])
            for d in range(1, parts)
        ]

    def add(*values):
        return sum(value.astype(f32) for value in values).astype(bf16)

    def sum_chips(value, fill=lambda value: ()):
        for step in range(len(masks)):
            got = cross(value, step)
            got = after(got, *fill(value))
            if step == len(masks) - 1:
                return value, got
            value = add(value, got)

    own_rows = a_diag[:HALF] if slab == HALF else lax.dynamic_slice_in_dim(a_diag, core * HALF, HALF, 0)
    corner = lax.dynamic_slice_in_dim(own_rows, chip * (HALF // chips), HALF // chips, 0)
    if slab == HALF:
        corner = jnp.where(z % 2 == core, corner, 0.0)
    corner = corner.astype(bf16)
    left_rows = (count + -(-count // max(slab // half, 1))) * half
    left = call(
        left_body,
        shaped((left_rows + WIDE // slab * (HALF // chips), slab), bf16),
        place,
        row_k,
        corner,
    )
    lefts = spread_rows(left)
    right, low_t = call(
        right_body,
        (
            shaped((count * half + (order - WIDE) // slab * (HALF // chips), slab), bf16),
            shaped((width, order), bf16),
        ),
        place,
        row_k,
        a_low,
        corner,
    )
    sketch_t = sketch.T
    rights = spread_rows(after(right, *lefts))
    rest_rows = sum(order // 2 - g * HALF for g in range(1, order // WIDE))
    left_t, own0, own1, away0, away1 = call(
        functools.partial(diagonal_body, count, parts),
        (
            shaped((count * half, order), bf16),
            shaped((order // 2, WIDE), bf16),
            shaped((rest_rows, WIDE), bf16),
            shaped((order // 2, WIDE), bf16),
            shaped((rest_rows, WIDE), bf16),
        ),
        place,
        after(lefts[0], right),
        *lefts[1:],
        scratch=(shaped((order, order), f32), shaped((count * half, order), bf16)),
    )

    def chunk_half(own, away, shards, at, start, stop, fill=lambda value: ()):
        got = swap(away)
        value = call(
            functools.partial(join_body, at, start, stop),
            shaped(own.shape, bf16),
            place,
            own,
            got,
            *shards,
            scratch=(shaped(own.shape, f32),),
        )
        return add(*sum_chips(value, fill))

    head_half = chunk_half(own0, away0, lefts, left_rows, 0, 1)
    head = head_half, swap(head_half)
    left_other = swap(left_t)
    chunks, mixed = [head], []
    slabs, halves, inverses = [], [], []

    def factor(*earlier):
        g = len(halves)
        if g >= groups:
            return ()
        wide = g * HALF // WIDE
        own, other = chunks[min(wide, 1)]
        done = sum(order // 2 - w * HALF for w in range(1, wide))
        slab_part, half_part, inverse = call(
            functools.partial(factor_body, g, done),
            (
                shaped((slab, HALF), f32),
                shaped((order - g * HALF, HALF), bf16),
                shaped((HALF, HALF), bf16),
            ),
            place,
            after(own, *earlier),
            other,
            *halves,
            scratch=(shaped((order, HALF), f32),),
        )
        slabs.append(slab_part)
        halves.append(half_part)
        inverses.append(inverse)
        return (inverse,)

    def mix(*earlier):
        if not mixed:
            mixed.extend(
                call(
                    functools.partial(mixed_body, parts),
                    (shaped((count * half, order), bf16),) * 2,
                    place,
                    mask,
                    after(rights[0], *earlier),
                    *rights[1:],
                    panel,
                    scratch=(shaped((count * half, order), bf16),),
                    scalars=2,
                )
            )
        return tuple(mixed)

    def tail_fill(value):
        return mix(value) if halves else factor(value)

    tail_half = chunk_half(
        own1, after(away1, head_half), rights, count * half, 1, order // WIDE, tail_fill
    )
    chunks.append((tail_half, swap(tail_half)))
    mixed_own, mixed_away = mix()
    mixed_other = swap(mixed_away)
    factors = (left_t, left_other, mixed_own, mixed_other)
    whole = shaped((rank, order), bf16)

    def low_term(value, forward):
        return call(
            functools.partial(low_body, forward), shaped((rank, order), f32), place, value, low_t
        )

    def fill(value):
        return factor(value)

    low = low_term(sketch_t, True)
    done = factor(mixed_away)
    value = call(first_body, whole, place, after(sketch_t, *done, tail_half), *factors)
    value = sum_chips(value, fill)
    for forward in (False, True):
        start, value = call(
            functools.partial(middle_body, forward), (whole, whole), place, *value, low, *factors
        )
        low = low_term(start, forward)
        value = sum_chips(value, fill)
    basis, value = call(basis_body, (whole, whole), place, *value, low, *factors)
    low = low_term(basis, False)
    value = sum_chips(value, fill)
    while len(halves) < groups:
        factor()
    diag_out = jnp.concatenate(slabs, axis=1)
    both = call(
        functools.partial(solve_body, groups),
        shaped((2 * rank, order), bf16),
        place,
        basis,
        *value,
        low,
        *halves,
        *inverses,
    )
    panel_out = call(finish_body, shaped((2, order, 2 * rank), f32), place, both, swap(both))
    return panel_out, diag_out


def solution(mesh):
    return jax.shard_map(
        panel_step,
        mesh=mesh,
        in_specs=(
            P("rows", "cols", None, None),
            P("cols", "rows", None),
            P("rows", "cols"),
            P("rows", None, None),
            P("rows", None),
            P(),
        ),
        out_specs=(P("rows", None, None), P("rows", None)),
        check_vma=False,
    )
```

time: 187 us -> 130 us (0.70); the launches traced: 184 us -> 129 us
  Pallas kernels: 85.4 us -> 52.3 us
  starting transfers between devices: 43.7 us -> 29.7 us
  local copies, waits for them, and re-layouts: 11.7 us -> 4.3 us
  waiting for transfers between devices: 34.7 us -> 41.2 us
  other arithmetic: 6.82 us -> 0.51 us
    pallas_call x17 -> x24, Pallas kernels: 85.4 us -> 52.3 us  [call(): pl.pallas_call(body, out_shape=outs, in_specs=[SMEM] * scalars + [VMEM] *...]
    ppermute x24 -> x12, starting transfers between devices: 26.7 us -> 15.7 us  [cross(): lax.ppermute(value, 'cols', [(i, i ^ bits[i % 2]) for i in range(cols)])]
    unnamed x89 -> x23, local copies, waits for them, and re-layouts: 11 us -> 4.18 us
    ppermute x24 -> x12, waiting for transfers between devices: 14.9 us -> 21.6 us  [cross(): lax.ppermute(value, 'cols', [(i, i ^ bits[i % 2]) for i in range(cols)])]
    convert_element_type x16 -> x8, other arithmetic: 5.66 us -> 0.51 us  [add(): return sum((value.astype(f32) for value in values)).astype(bf16)]
    ppermute x9 -> x6, waiting for transfers between devices: 19.7 us -> 15.1 us  [spread_rows(): lax.ppermute(value, 'rows', [(i, (i + d) % parts) for i in range(parts)])]
    ppermute x8 -> x7, waiting for transfers between devices: 0.09 us -> 4.53 us  [swap(): return lax.ppermute(value, 'cols', partner)]
    ppermute x9 -> x6, starting transfers between devices: 15.7 us -> 13.2 us  [spread_rows(): lax.ppermute(value, 'rows', [(i, (i + d) % parts) for i in range(parts)])]
  transfers between devices with their start and end apart: 41 -> 25, of which waited for: 17 -> 13; matrix products, arithmetic and copies ran while one was open for 4% -> 0% of each run, Pallas kernels for 42% -> 30%
where the time goes in v2:
time: 130 us; the launch traced here: 129 us
  Pallas kernels  52.3 us (40%)
  waiting for transfers between devices  41.2 us (32%)
  starting transfers between devices  29.7 us (23%)
  local copies, waits for them, and re-layouts  4.3 us (3%)
    pallas_call x24, Pallas kernels, call(): pl.pallas_call(body, out_shape=outs, in_specs=[SMEM] * scalars + [VMEM] *...  52.3 us
    ppermute x12, waiting for transfers between devices, cross(): lax.ppermute(value, 'cols', [(i, i ^ bits[i % 2]) for i in range(cols)])  21.6 us
    ppermute x12, starting transfers between devices, cross(): lax.ppermute(value, 'cols', [(i, i ^ bits[i % 2]) for i in range(cols)])  15.7 us
    ppermute x6, waiting for transfers between devices, spread_rows(): lax.ppermute(value, 'rows', [(i, (i + d) % parts) for i in range(parts)])  15.1 us
    ppermute x6, starting transfers between devices, spread_rows(): lax.ppermute(value, 'rows', [(i, (i + d) % parts) for i in range(parts)])  13.2 us
    ppermute x7, waiting for transfers between devices, swap(): return lax.ppermute(value, 'cols', partner)  4.53 us
    unnamed x23, local copies, waits for them, and re-layouts  4.18 us
  transfers between devices with their start and end apart: 25, of which 13 were waited for; matrix products, arithmetic and copies ran while one was open for 0% of the time, Pallas kernels for 30%

profile of v2, /device:TPU:0, one launch (start us, length us, event | category | flops | bytes accessed | tf_op | source)
XLA Modules:
  0.0 129.0 jit_solution(691186143516922721)
XLA Ops:
  0.7 1.2 copy-done
  1.9 0.1 stack.19.place
  2.0 0.9 copy-done.2
  2.9 0.9 shard_map.77.refs_0_
  3.8 3.1 %collective-permute-start = (bf16[288,256]{1,0:T(8,128)(2,1)S(1)}, bf16[288,256]{1,0:T(8,128)(2,1)S(1)}, u32[]{:S(2)}, u32[]{:S(2)}) collective-permute-start(bf16[288,256]{1,0:T(8,128)(2,1)S(1)} %shard_map.77.refs_0_), channel_id=1, source_target_pairs={{0,1},{1,2},{2,3},{3,0},{4,5},{5,6},{6,7},{7,4},{8,9},{9,10},{10,1... | collective-permute-start | bytes 442376 | tf_op jit(solution)/shard_map/ppermute | solution.py:336
  6.9 2.6 %collective-permute-start.1 = (bf16[288,256]{1,0:T(8,128)(2,1)S(1)}, bf16[288,256]{1,0:T(8,128)(2,1)S(1)}, u32[]{:S(2)}, u32[]{:S(2)}) collective-permute-start(bf16[288,256]{1,0:T(8,128)(2,1)S(1)} %shard_map.77.refs_0_), channel_id=1, source_target_pairs={{0,2},{1,3},{2,0},{3,1},{4,6},{5,7},{6,4},{7,5},{8,10},{9,11},{10,... | collective-permute-start | bytes 442376 | tf_op jit(solution)/shard_map/ppermute | solution.py:336
  9.5 1.3 %collective-permute-start.2 = (bf16[288,256]{1,0:T(8,128)(2,1)S(1)}, bf16[288,256]{1,0:T(8,128)(2,1)S(1)}, u32[]{:S(2)}, u32[]{:S(2)}) collective-permute-start(bf16[288,256]{1,0:T(8,128)(2,1)S(1)} %shard_map.77.refs_0_), channel_id=1, source_target_pairs={{0,3},{1,0},{2,1},{3,2},{4,7},{5,4},{6,5},{7,6},{8,11},{9,8},{10,9... | collective-permute-start | bytes 442376 | tf_op jit(solution)/shard_map/ppermute | solution.py:336
  10.8 0.9 copy-done.3
  11.7 1.0 copy-done.4
  12.8 0.7 shard_map.78
  13.5 0.2 collective-permute-done.refs_1_
  13.7 5.5 %collective-permute-done.1.refs_2_ = bf16[288,256]{1,0:T(8,128)(2,1)S(1)} collective-permute-done((bf16[288,256]{1,0:T(8,128)(2,1)S(1)}, bf16[288,256]{1,0:T(8,128)(2,1)S(1)}, u32[]{:S(2)}, u32[]{:S(2)}) %collective-permute-start.1) | collective-permute-done | bytes 147488 | tf_op jit(solution)/shard_map/ppermute | solution.py:336
  19.2 1.7 %shard_map.79 = (bf16[192,1024]{1,0:T(8,128)(2,1)S(1)}, bf16[512,256]{1,0:T(8,128)(2,1)S(1)}, bf16[768,256]{1,0:T(8,128)(2,1)S(1)}, bf16[512,256]{1,0:T(8,128)(2,1)S(1)}, bf16[768,256]{1,0:T(8,128)(2,1)S(1)}) custom-call(s32[5]{0:T(128)S(1)} %stack.19.place, bf16[288,256]{1,0:T(8,128)(2,1)S(1)} %shard_map.77.refs_0_, ...), custom_call_target="tpu_custom_call" | custom-call | tf_op jit(solution)/shard_map/pallas_call | solution.py:47
  21.0 1.5 %collective-permute-done.3.got_ref = bf16[512,256]{1,0:T(8,128)(2,1)S(1)} collective-permute-done((bf16[512,256]{1,0:T(8,128)(2,1)S(1)}, bf16[512,256]{1,0:T(8,128)(2,1)S(1)}, u32[]{:S(2)}, u32[]{:S(2)}) %collective-permute-start.3) | collective-permute-done | bytes 262176 | tf_op jit(solution)/shard_map/ppermute | solution.py:328
  22.5 0.7 shard_map.80
  23.2 1.6 %collective-permute-start.4 = (bf16[512,256]{1,0:T(8,128)(2,1)S(1)}, bf16[512,256]{1,0:T(8,128)(2,1)S(1)}, u32[]{:S(2)}, u32[]{:S(2)}) collective-permute-start(bf16[512,256]{1,0:T(8,128)(2,1)S(1)} %shard_map.80), channel_id=1, source_target_pairs={{0,8},{4,20},{8,0},{12,28},{16,24},{20,4},{24,16},{28,12},{1,9},{5... | collective-permute-start | bytes 786440 | tf_op jit(solution)/shard_map/ppermute | solution.py:332
  24.7 4.9 %collective-permute-done.4 = bf16[512,256]{1,0:T(8,128)(2,1)S(1)} collective-permute-done((bf16[512,256]{1,0:T(8,128)(2,1)S(1)}, bf16[512,256]{1,0:T(8,128)(2,1)S(1)}, u32[]{:S(2)}, u32[]{:S(2)}) %collective-permute-start.4) | collective-permute-done | bytes 262176 | tf_op jit(solution)/shard_map/ppermute | solution.py:332
  29.6 0.1 add_convert_fusion.3
  29.7 1.6 %collective-permute-start.5 = (bf16[512,256]{1,0:T(8,128)(2,1)S(1)}, bf16[512,256]{1,0:T(8,128)(2,1)S(1)}, u32[]{:S(2)}, u32[]{:S(2)}) collective-permute-start(bf16[512,256]{1,0:T(8,128)(2,1)S(1)} %add_convert_fusion.3), channel_id=1, source_target_pairs={{0,16},{4,12},{8,24},{12,4},{16,0},{20,28},{24,8},{28,20},{1,17},{... | collective-permute-start | bytes 786440 | tf_op jit(solution)/shard_map/ppermute | solution.py:332
  31.3 4.9 %collective-permute-done.5 = bf16[512,256]{1,0:T(8,128)(2,1)S(1)} collective-permute-done((bf16[512,256]{1,0:T(8,128)(2,1)S(1)}, bf16[512,256]{1,0:T(8,128)(2,1)S(1)}, u32[]{:S(2)}, u32[]{:S(2)}) %collective-permute-start.5) | collective-permute-done | bytes 262176 | tf_op jit(solution)/shard_map/ppermute | solution.py:332
  36.3 3.7 %collective-permute-start.7 = (bf16[288,256]{1,0:T(8,128)(2,1)S(1)}, bf16[288,256]{1,0:T(8,128)(2,1)S(1)}, u32[]{:S(2)}, u32[]{:S(2)}) collective-permute-start(bf16[288,256]{1,0:T(8,128)(2,1)S(1)} %get-tuple-element.73.refs_0_), channel_id=1, source_target_pairs={{0,1},{1,2},{2,3},{3,0},{4,5},{5,6},{6,7},{7,4},{8,9},{9,10},{10,1... | collective-permute-start | bytes 442376 | tf_op jit(solution)/shard_map/ppermute | solution.py:336
  39.9 1.6 %collective-permute-start.8 = (bf16[288,256]{1,0:T(8,128)(2,1)S(1)}, bf16[288,256]{1,0:T(8,128)(2,1)S(1)}, u32[]{:S(2)}, u32[]{:S(2)}) collective-permute-start(bf16[288,256]{1,0:T(8,128)(2,1)S(1)} %get-tuple-element.73.refs_0_), channel_id=1, source_target_pairs={{0,2},{1,3},{2,0},{3,1},{4,6},{5,7},{6,4},{7,5},{8,10},{9,11},{10,... | collective-permute-start | bytes 442376 | tf_op jit(solution)/shard_map/ppermute | solution.py:336
  41.6 0.8 collective-permute-start.9
  42.4 3.4 %collective-permute-done.7.refs_1_ = bf16[288,256]{1,0:T(8,128)(2,1)S(1)} collective-permute-done((bf16[288,256]{1,0:T(8,128)(2,1)S(1)}, bf16[288,256]{1,0:T(8,128)(2,1)S(1)}, u32[]{:S(2)}, u32[]{:S(2)}) %collective-permute-start.7) | collective-permute-done | bytes 147488 | tf_op jit(solution)/shard_map/ppermute | solution.py:336
  45.8 6.0 %collective-permute-done.8.refs_2_ = bf16[288,256]{1,0:T(8,128)(2,1)S(1)} collective-permute-done((bf16[288,256]{1,0:T(8,128)(2,1)S(1)}, bf16[288,256]{1,0:T(8,128)(2,1)S(1)}, u32[]{:S(2)}, u32[]{:S(2)}) %collective-permute-start.8) | collective-permute-done | bytes 147488 | tf_op jit(solution)/shard_map/ppermute | solution.py:336
  51.9 0.9 shard_map.81
  52.8 1.6 %collective-permute-start.10 = (bf16[768,256]{1,0:T(8,128)(2,1)S(1)}, bf16[768,256]{1,0:T(8,128)(2,1)S(1)}, u32[]{:S(2)}, u32[]{:S(2)}) collective-permute-start(bf16[768,256]{1,0:T(8,128)(2,1)S(1)} %shard_map.81), channel_id=1, source_target_pairs={{0,8},{4,20},{8,0},{12,28},{16,24},{20,4},{24,16},{28,12},{1,9},{5... | collective-permute-start | bytes 1179656 | tf_op jit(solution)/shard_map/ppermute | solution.py:332
  54.4 1.5 %collective-permute-done.11.other_ref = bf16[512,256]{1,0:T(8,128)(2,1)S(1)} collective-permute-done((bf16[512,256]{1,0:T(8,128)(2,1)S(1)}, bf16[512,256]{1,0:T(8,128)(2,1)S(1)}, u32[]{:S(2)}, u32[]{:S(2)}) %collective-permute-start.11) | collective-permute-done | bytes 262176 | tf_op jit(solution)/shard_map/ppermute | solution.py:328
  55.9 3.6 %shard_map.82 = (f32[256,128]{1,0:T(8,128)S(1)}, bf16[1024,128]{1,0:T(8,128)(2,1)S(1)}, bf16[128,128]{1,0:T(8,128)(2,1)S(1)}) custom-call(s32[5]{0:T(128)S(1)} %stack.19.place, bf16[512,256]{1,0:T(8,128)(2,1)S(1)} %add_convert_fusion.2.own_ref, bf16[512,256]{1,0:T(8,128)(2,1)S(1)} %collective-permute-done.11.other_ref), custom_call_target="tpu_custom_call" | custom-call | tf_op jit(solution)/shard_map/pallas_call | solution.py:47
  59.5 1.1 collective-permute-done.10
  60.7 0.1 add_convert_fusion.1
  60.8 1.6 %collective-permute-start.12 = (bf16[768,256]{1,0:T(8,128)(2,1)S(1)}, bf16[768,256]{1,0:T(8,128)(2,1)S(1)}, u32[]{:S(2)}, u32[]{:S(2)}) collective-permute-start(bf16[768,256]{1,0:T(8,128)(2,1)S(1)} %add_convert_fusion.1), channel_id=1, source_target_pairs={{0,16},{4,12},{8,24},{12,4},{16,0},{20,28},{24,8},{28,20},{1,17},{... | collective-permute-start | bytes 1179656 | tf_op jit(solution)/shard_map/ppermute | solution.py:332
  62.4 2.4 %shard_map.83 = (bf16[192,1024]{1,0:T(8,128)(2,1)S(1)}, bf16[192,1024]{1,0:T(8,128)(2,1)S(1)}) custom-call(s32[5]{0:T(128)S(1)} %stack.19.place, s32[2,3]{1,0:T(2,128)S(1)} %copy-done.6, bf16[288,256]{1,0:T(8,128)(2,1)S(1)} %get-tuple-element.73.refs_0_, bf16[288,256]{1,0:T(8,128)(2,1)S(1)} %collective-permute-done.7.refs_1_, ...), custom_call_target="tpu_custom_call" | custom-call | tf_op jit(solution)/shard_map/pallas_call | solution.py:47
  64.8 0.6 collective-permute-start.14
  65.3 3.3 %collective-permute-done.12 = bf16[768,256]{1,0:T(8,128)(2,1)S(1)} collective-permute-done((bf16[768,256]{1,0:T(8,128)(2,1)S(1)}, bf16[768,256]{1,0:T(8,128)(2,1)S(1)}, u32[]{:S(2)}, u32[]{:S(2)}) %collective-permute-start.12) | collective-permute-done | bytes 393248 | tf_op jit(solution)/shard_map/ppermute | solution.py:332
  68.6 0.1 add_convert_fusion.own_ref
  68.8 3.9 %shard_map.84 = (f32[256,128]{1,0:T(8,128)S(1)}, bf16[896,128]{1,0:T(8,128)(2,1)S(1)}, bf16[128,128]{1,0:T(8,128)(2,1)S(1)}) custom-call(s32[5]{0:T(128)S(1)} %stack.19.place, bf16[512,256]{1,0:T(8,128)(2,1)S(1)} %add_convert_fusion.2.own_ref, bf16[512,256]{1,0:T(8,128)(2,1)S(1)} %collective-permute-done.11.other_ref, ...), custom_call_target="tpu_custom_call" | custom-call | tf_op jit(solution)/shard_map/pallas_call | solution.py:47
  72.7 1.1 shard_map.85
  73.8 1.6 %collective-permute-start.15 = (bf16[64,1024]{1,0:T(8,128)(2,1)S(1)}, bf16[64,1024]{1,0:T(8,128)(2,1)S(1)}, u32[]{:S(2)}, u32[]{:S(2)}) collective-permute-start(bf16[64,1024]{1,0:T(8,128)(2,1)S(1)} %shard_map.85), channel_id=1, source_target_pairs={{0,8},{4,20},{8,0},{12,28},{16,24},{20,4},{24,16},{28,12},{1,9},{5... | collective-permute-start | bytes 393224 | tf_op jit(solution)/shard_map/ppermute | solution.py:332
  75.4 3.8 %shard_map.86 = (f32[256,128]{1,0:T(8,128)S(1)}, bf16[768,128]{1,0:T(8,128)(2,1)S(1)}, bf16[128,128]{1,0:T(8,128)(2,1)S(1)}) custom-call(s32[5]{0:T(128)S(1)} %stack.19.place, bf16[768,256]{1,0:T(8,128)(2,1)S(1)} %add_convert_fusion.own_ref, bf16[768,256]{1,0:T(8,128)(2,1)S(1)} %collective-permute-done.16.other_ref, ...), custom_call_target="tpu_custom_call" | custom-call | tf_op jit(solution)/shard_map/pallas_call | solution.py:47
  79.2 1.6 %collective-permute-start.17 = (bf16[64,1024]{1,0:T(8,128)(2,1)S(1)}, bf16[64,1024]{1,0:T(8,128)(2,1)S(1)}, u32[]{:S(2)}, u32[]{:S(2)}) collective-permute-start(bf16[64,1024]{1,0:T(8,128)(2,1)S(1)} %add_convert_fusion.7.own), channel_id=1, source_target_pairs={{0,16},{4,12},{8,24},{12,4},{16,0},{20,28},{24,8},{28,20},{1,17},{... | collective-permute-start | bytes 393224 | tf_op jit(solution)/shard_map/ppermute | solution.py:332
  80.8 0.9 shard_map.88.low
  81.7 3.8 %shard_map.87 = (f32[256,128]{1,0:T(8,128)S(1)}, bf16[640,128]{1,0:T(8,128)(2,1)S(1)}, bf16[128,128]{1,0:T(8,128)(2,1)S(1)}) custom-call(s32[5]{0:T(128)S(1)} %stack.19.place, bf16[768,256]{1,0:T(8,128)(2,1)S(1)} %add_convert_fusion.own_ref, bf16[768,256]{1,0:T(8,128)(2,1)S(1)} %collective-permute-done.16.other_ref, ...), custom_call_target="tpu_custom_call" | custom-call | tf_op jit(solution)/shard_map/pallas_call | solution.py:47
  85.5 1.3 %shard_map.89 = (bf16[64,1024]{1,0:T(8,128)(2,1)S(1)}, bf16[64,1024]{1,0:T(8,128)(2,1)S(1)}) custom-call(s32[5]{0:T(128)S(1)} %stack.19.place, bf16[64,1024]{1,0:T(8,128)(2,1)S(1)} %add_convert_fusion.7.own, bf16[64,1024]{1,0:T(8,128)(2,1)S(1)} %collective-permute-done.17.got, f32[64,1024]{1,0:T(8,128)S(1)} %shard_map.88.low, ...), custom_call_target="tpu_custom_call" | custom-call | tf_op jit(solution)/shard_map/pallas_call | solution.py:47
  86.9 1.2 collective-permute-start.18
  88.1 3.8 %shard_map.90 = (f32[256,128]{1,0:T(8,128)S(1)}, bf16[512,128]{1,0:T(8,128)(2,1)S(1)}, bf16[128,128]{1,0:T(8,128)(2,1)S(1)}) custom-call(s32[5]{0:T(128)S(1)} %stack.19.place, bf16[768,256]{1,0:T(8,128)(2,1)S(1)} %add_convert_fusion.own_ref, bf16[768,256]{1,0:T(8,128)(2,1)S(1)} %collective-permute-done.16.other_ref, ...), custom_call_target="tpu_custom_call" | custom-call | tf_op jit(solution)/shard_map/pallas_call | solution.py:47
  92.0 0.6 collective-permute-start.19
  92.6 0.9 shard_map.92.low
  93.5 3.9 %shard_map.91 = (f32[256,128]{1,0:T(8,128)S(1)}, bf16[384,128]{1,0:T(8,128)(2,1)S(1)}, bf16[128,128]{1,0:T(8,128)(2,1)S(1)}) custom-call(s32[5]{0:T(128)S(1)} %stack.19.place, bf16[768,256]{1,0:T(8,128)(2,1)S(1)} %add_convert_fusion.own_ref, bf16[768,256]{1,0:T(8,128)(2,1)S(1)} %collective-permute-done.16.other_ref, ...), custom_call_target="tpu_custom_call" | custom-call | tf_op jit(solution)/shard_map/pallas_call | solution.py:47
  97.3 1.1 shard_map.93
  98.5 1.2 collective-permute-start.20
  99.7 3.9 %shard_map.94 = (f32[256,128]{1,0:T(8,128)S(1)}, bf16[256,128]{1,0:T(8,128)(2,1)S(1)}, bf16[128,128]{1,0:T(8,128)(2,1)S(1)}) custom-call(s32[5]{0:T(128)S(1)} %stack.19.place, bf16[768,256]{1,0:T(8,128)(2,1)S(1)} %add_convert_fusion.own_ref, bf16[768,256]{1,0:T(8,128)(2,1)S(1)} %collective-permute-done.16.other_ref, ...), custom_call_target="tpu_custom_call" | custom-call | tf_op jit(solution)/shard_map/pallas_call | solution.py:47
  103.6 1.6 %collective-permute-start.21 = (bf16[64,1024]{1,0:T(8,128)(2,1)S(1)}, bf16[64,1024]{1,0:T(8,128)(2,1)S(1)}, u32[]{:S(2)}, u32[]{:S(2)}) collective-permute-start(bf16[64,1024]{1,0:T(8,128)(2,1)S(1)} %add_convert_fusion.5.own), channel_id=1, source_target_pairs={{0,16},{4,12},{8,24},{12,4},{16,0},{20,28},{24,8},{28,20},{1,17},{... | collective-permute-start | bytes 393224 | tf_op jit(solution)/shard_map/ppermute | solution.py:332
  105.2 0.9 shard_map.96.low
  106.1 3.8 %shard_map.95 = (f32[256,128]{1,0:T(8,128)S(1)}, bf16[128,128]{1,0:T(8,128)(2,1)S(1)}, bf16[128,128]{1,0:T(8,128)(2,1)S(1)}) custom-call(s32[5]{0:T(128)S(1)} %stack.19.place, bf16[768,256]{1,0:T(8,128)(2,1)S(1)} %add_convert_fusion.own_ref, bf16[768,256]{1,0:T(8,128)(2,1)S(1)} %collective-permute-done.16.other_ref, ...), custom_call_target="tpu_custom_call" | custom-call | tf_op jit(solution)/shard_map/pallas_call | solution.py:47
  109.9 3.4 %shard_map.97 = (bf16[64,1024]{1,0:T(8,128)(2,1)S(1)}, bf16[64,1024]{1,0:T(8,128)(2,1)S(1)}) custom-call(s32[5]{0:T(128)S(1)} %stack.19.place, bf16[64,1024]{1,0:T(8,128)(2,1)S(1)} %add_convert_fusion.5.own, bf16[64,1024]{1,0:T(8,128)(2,1)S(1)} %collective-permute-done.21.got, f32[64,1024]{1,0:T(8,128)S(1)} %shard_map.96.low, ...), custom_call_target="tpu_custom_call" | custom-call | tf_op jit(solution)/shard_map/pallas_call | solution.py:47
  113.3 1.2 collective-permute-start.22
  114.5 3.8 %collective-permute-done.22 = bf16[64,1024]{1,0:T(8,128)(2,1)S(1)} collective-permute-done((bf16[64,1024]{1,0:T(8,128)(2,1)S(1)}, bf16[64,1024]{1,0:T(8,128)(2,1)S(1)}, u32[]{:S(2)}, u32[]{:S(2)}) %collective-permute-start.22) | collective-permute-done | bytes 131104 | tf_op jit(solution)/shard_map/ppermute | solution.py:332
  118.4 0.6 collective-permute-start.23
  119.0 0.9 shard_map.98.low
  119.9 3.5 %collective-permute-done.23.got = bf16[64,1024]{1,0:T(8,128)(2,1)S(1)} collective-permute-done((bf16[64,1024]{1,0:T(8,128)(2,1)S(1)}, bf16[64,1024]{1,0:T(8,128)(2,1)S(1)}, u32[]{:S(2)}, u32[]{:S(2)}) %collective-permute-start.23) | collective-permute-done | bytes 131104 | tf_op jit(solution)/shard_map/ppermute | solution.py:332
  123.4 2.4 %shard_map.99.own = bf16[128,1024]{1,0:T(8,128)(2,1)S(1)} custom-call(s32[5]{0:T(128)S(1)} %stack.19.place, bf16[64,1024]{1,0:T(8,128)(2,1)S(1)} %get-tuple-element.111.value_ref.basis, bf16[64,1024]{1,0:T(8,128)(2,1)S(1)} %add_convert_fusion.4.own, bf16[64,1024]{1,0:T(8,128)(2,1)S(1)} %collective-permute-done.23.got, f32[64,1024]{1,0:T(8,128)S(1)} %shard_map.98.low, ...), custom_call_target="tpu_custom_call" | custom-call | tf_op jit(solution)/shard_map/pallas_call | solution.py:47
  125.9 1.5 %collective-permute-done.24.other = bf16[128,1024]{1,0:T(8,128)(2,1)S(1)} collective-permute-done((bf16[128,1024]{1,0:T(8,128)(2,1)S(1)}, bf16[128,1024]{1,0:T(8,128)(2,1)S(1)}, u32[]{:S(2)}, u32[]{:S(2)}) %collective-permute-start.24) | collective-permute-done | bytes 262176 | tf_op jit(solution)/shard_map/ppermute | solution.py:328
  127.3 1.7 %shard_map.100 = f32[2,1024,128]{2,1,0:T(8,128)} custom-call(s32[5]{0:T(128)S(1)} %stack.19.place, bf16[128,1024]{1,0:T(8,128)(2,1)S(1)} %shard_map.99.own, bf16[128,1024]{1,0:T(8,128)(2,1)S(1)} %collective-permute-done.24.other), custom_call_target="tpu_custom_call" | custom-call | tf_op jit(solution)/shard_map/pallas_call | solution.py:47
  (44 shorter events, 0.6 us)
Async XLA Ops:
  0.6 1.2 copy-start
  2.0 0.9 copy-start.2
  3.8 9.9 %collective-permute-start = (bf16[288,256]{1,0:T(8,128)(2,1)S(1)}, bf16[288,256]{1,0:T(8,128)(2,1)S(1)}, u32[]{:S(2)}, u32[]{:S(2)}) collective-permute-start(bf16[288,256]{1,0:T(8,128)(2,1)S(1)} %shard_map.77.refs_0_), channel_id=1, source_target_pairs={{0,1},{1,2},{2,3},{3,0},{4,5},{5,6},{6,7},{7,4},{8,9},{9,10},{10,1... | collective-permute-start | bytes 442376 | tf_op jit(solution)/shard_map/ppermute | solution.py:336
  6.9 12.3 %collective-permute-start.1 = (bf16[288,256]{1,0:T(8,128)(2,1)S(1)}, bf16[288,256]{1,0:T(8,128)(2,1)S(1)}, u32[]{:S(2)}, u32[]{:S(2)}) collective-permute-start(bf16[288,256]{1,0:T(8,128)(2,1)S(1)} %shard_map.77.refs_0_), channel_id=1, source_target_pairs={{0,2},{1,3},{2,0},{3,1},{4,6},{5,7},{6,4},{7,5},{8,10},{9,11},{10,... | collective-permute-start | bytes 442376 | tf_op jit(solution)/shard_map/ppermute | solution.py:336
  9.5 9.7 %collective-permute-start.2 = (bf16[288,256]{1,0:T(8,128)(2,1)S(1)}, bf16[288,256]{1,0:T(8,128)(2,1)S(1)}, u32[]{:S(2)}, u32[]{:S(2)}) collective-permute-start(bf16[288,256]{1,0:T(8,128)(2,1)S(1)} %shard_map.77.refs_0_), channel_id=1, source_target_pairs={{0,3},{1,0},{2,1},{3,2},{4,7},{5,4},{6,5},{7,6},{8,11},{9,8},{10,9... | collective-permute-start | bytes 442376 | tf_op jit(solution)/shard_map/ppermute | solution.py:336
  10.8 0.9 copy-start.3
  11.7 1.0 copy-start.4
  20.9 1.6 %collective-permute-start.3 = (bf16[512,256]{1,0:T(8,128)(2,1)S(1)}, bf16[512,256]{1,0:T(8,128)(2,1)S(1)}, u32[]{:S(2)}, u32[]{:S(2)}) collective-permute-start(bf16[512,256]{1,0:T(8,128)(2,1)S(1)} %get-tuple-element.65), channel_id=1, source_target_pairs={{0,4},{4,0},{8,12},{12,8},{16,20},{20,16},{24,28},{28,24},{1,5},{5... | collective-permute-start | bytes 786440 | tf_op jit(solution)/shard_map/ppermute | solution.py:328
  23.2 6.4 %collective-permute-start.4 = (bf16[512,256]{1,0:T(8,128)(2,1)S(1)}, bf16[512,256]{1,0:T(8,128)(2,1)S(1)}, u32[]{:S(2)}, u32[]{:S(2)}) collective-permute-start(bf16[512,256]{1,0:T(8,128)(2,1)S(1)} %shard_map.80), channel_id=1, source_target_pairs={{0,8},{4,20},{8,0},{12,28},{16,24},{20,4},{24,16},{28,12},{1,9},{5... | collective-permute-start | bytes 786440 | tf_op jit(solution)/shard_map/ppermute | solution.py:332
  29.7 6.4 %collective-permute-start.5 = (bf16[512,256]{1,0:T(8,128)(2,1)S(1)}, bf16[512,256]{1,0:T(8,128)(2,1)S(1)}, u32[]{:S(2)}, u32[]{:S(2)}) collective-permute-start(bf16[512,256]{1,0:T(8,128)(2,1)S(1)} %add_convert_fusion.3), channel_id=1, source_target_pairs={{0,16},{4,12},{8,24},{12,4},{16,0},{20,28},{24,8},{28,20},{1,17},{... | collective-permute-start | bytes 786440 | tf_op jit(solution)/shard_map/ppermute | solution.py:332
  36.2 15.7 %collective-permute-start.6 = (bf16[768,256]{1,0:T(8,128)(2,1)S(1)}, bf16[768,256]{1,0:T(8,128)(2,1)S(1)}, u32[]{:S(2)}, u32[]{:S(2)}) collective-permute-start(bf16[768,256]{1,0:T(8,128)(2,1)S(1)} %get-tuple-element.69), channel_id=1, source_target_pairs={{0,4},{4,0},{8,12},{12,8},{16,20},{20,16},{24,28},{28,24},{1,5},{5... | collective-permute-start | bytes 1179656 | tf_op jit(solution)/shard_map/ppermute | solution.py:328
  36.3 9.5 %collective-permute-start.7 = (bf16[288,256]{1,0:T(8,128)(2,1)S(1)}, bf16[288,256]{1,0:T(8,128)(2,1)S(1)}, u32[]{:S(2)}, u32[]{:S(2)}) collective-permute-start(bf16[288,256]{1,0:T(8,128)(2,1)S(1)} %get-tuple-element.73.refs_0_), channel_id=1, source_target_pairs={{0,1},{1,2},{2,3},{3,0},{4,5},{5,6},{6,7},{7,4},{8,9},{9,10},{10,1... | collective-permute-start | bytes 442376 | tf_op jit(solution)/shard_map/ppermute | solution.py:336
  39.9 11.9 %collective-permute-start.8 = (bf16[288,256]{1,0:T(8,128)(2,1)S(1)}, bf16[288,256]{1,0:T(8,128)(2,1)S(1)}, u32[]{:S(2)}, u32[]{:S(2)}) collective-permute-start(bf16[288,256]{1,0:T(8,128)(2,1)S(1)} %get-tuple-element.73.refs_0_), channel_id=1, source_target_pairs={{0,2},{1,3},{2,0},{3,1},{4,6},{5,7},{6,4},{7,5},{8,10},{9,11},{10,... | collective-permute-start | bytes 442376 | tf_op jit(solution)/shard_map/ppermute | solution.py:336
  41.6 10.3 %collective-permute-start.9 = (bf16[288,256]{1,0:T(8,128)(2,1)S(1)}, bf16[288,256]{1,0:T(8,128)(2,1)S(1)}, u32[]{:S(2)}, u32[]{:S(2)}) collective-permute-start(bf16[288,256]{1,0:T(8,128)(2,1)S(1)} %get-tuple-element.73.refs_0_), channel_id=1, source_target_pairs={{0,3},{1,0},{2,1},{3,2},{4,7},{5,4},{6,5},{7,6},{8,11},{9,8},{10,9... | collective-permute-start | bytes 442376 | tf_op jit(solution)/shard_map/ppermute | solution.py:336
  51.9 10.5 %copy-start.1 = (bf16[2,3,1024,128]{3,2,1,0:T(8,128)(2,1)S(1)}, bf16[2,3,1024,128]{3,2,1,0:T(8,128)(2,1)}, u32[]{:S(2)}) copy-start(bf16[2,3,1024,128]{3,2,1,0:T(8,128)(2,1)} %refs_4_.1) | copy-start | bytes 4718596
  51.9 10.5 %copy-start.6 = (s32[2,3]{1,0:T(2,128)S(1)}, s32[2,3]{1,0:T(2,128)}, u32[]{:S(2)}) copy-start(s32[2,3]{1,0:T(2,128)} %mask_ref.1) | copy-start | bytes 76
  52.8 7.8 %collective-permute-start.10 = (bf16[768,256]{1,0:T(8,128)(2,1)S(1)}, bf16[768,256]{1,0:T(8,128)(2,1)S(1)}, u32[]{:S(2)}, u32[]{:S(2)}) collective-permute-start(bf16[768,256]{1,0:T(8,128)(2,1)S(1)} %shard_map.81), channel_id=1, source_target_pairs={{0,8},{4,20},{8,0},{12,28},{16,24},{20,4},{24,16},{28,12},{1,9},{5... | collective-permute-start | bytes 1179656 | tf_op jit(solution)/shard_map/ppermute | solution.py:332
  54.4 1.5 %collective-permute-start.11 = (bf16[512,256]{1,0:T(8,128)(2,1)S(1)}, bf16[512,256]{1,0:T(8,128)(2,1)S(1)}, u32[]{:S(2)}, u32[]{:S(2)}) collective-permute-start(bf16[512,256]{1,0:T(8,128)(2,1)S(1)} %add_convert_fusion.2.own_ref), channel_id=1, source_target_pairs={{0,4},{4,0},{8,12},{12,8},{16,20},{20,16},{24,28},{28,24},{1,5},{5... | collective-permute-start | bytes 786440 | tf_op jit(solution)/shard_map/ppermute | solution.py:328
  60.8 7.8 %collective-permute-start.12 = (bf16[768,256]{1,0:T(8,128)(2,1)S(1)}, bf16[768,256]{1,0:T(8,128)(2,1)S(1)}, u32[]{:S(2)}, u32[]{:S(2)}) collective-permute-start(bf16[768,256]{1,0:T(8,128)(2,1)S(1)} %add_convert_fusion.1), channel_id=1, source_target_pairs={{0,16},{4,12},{8,24},{12,4},{16,0},{20,28},{24,8},{28,20},{1,17},{... | collective-permute-start | bytes 1179656 | tf_op jit(solution)/shard_map/ppermute | solution.py:332
  62.4 10.3 %copy-start.5 = (bf16[1024,64]{0,1:T(8,128)(2,1)S(1)}, bf16[1024,64]{0,1:T(8,128)(2,1)}, u32[]{:S(2)}) copy-start(bf16[1024,64]{0,1:T(8,128)(2,1)} %param.11) | copy-start | bytes 393220
  62.4 10.3 %collective-permute-start.13 = (bf16[192,1024]{1,0:T(8,128)(2,1)S(1)}, bf16[192,1024]{1,0:T(8,128)(2,1)S(1)}, u32[]{:S(2)}, u32[]{:S(2)}) collective-permute-start(bf16[192,1024]{1,0:T(8,128)(2,1)S(1)} %get-tuple-element.81.u0), channel_id=1, source_target_pairs={{0,4},{4,0},{8,12},{12,8},{16,20},{20,16},{24,28},{28,24},{1,5},{5... | collective-permute-start | bytes 1179656 | tf_op jit(solution)/shard_map/ppermute | solution.py:328
  64.8 7.9 %collective-permute-start.14 = (bf16[192,1024]{1,0:T(8,128)(2,1)S(1)}, bf16[192,1024]{1,0:T(8,128)(2,1)S(1)}, u32[]{:S(2)}, u32[]{:S(2)}) collective-permute-start(bf16[192,1024]{1,0:T(8,128)(2,1)S(1)} %get-tuple-element.74), channel_id=1, source_target_pairs={{0,4},{4,0},{8,12},{12,8},{16,20},{20,16},{24,28},{28,24},{1,5},{5... | collective-permute-start | bytes 1179656 | tf_op jit(solution)/shard_map/ppermute | solution.py:328
  68.7 6.7 %collective-permute-start.16 = (bf16[768,256]{1,0:T(8,128)(2,1)S(1)}, bf16[768,256]{1,0:T(8,128)(2,1)S(1)}, u32[]{:S(2)}, u32[]{:S(2)}) collective-permute-start(bf16[768,256]{1,0:T(8,128)(2,1)S(1)} %add_convert_fusion.own_ref), channel_id=1, source_target_pairs={{0,4},{4,0},{8,12},{12,8},{16,20},{20,16},{24,28},{28,24},{1,5},{5... | collective-permute-start | bytes 1179656 | tf_op jit(solution)/shard_map/ppermute | solution.py:328
  73.8 5.3 %collective-permute-start.15 = (bf16[64,1024]{1,0:T(8,128)(2,1)S(1)}, bf16[64,1024]{1,0:T(8,128)(2,1)S(1)}, u32[]{:S(2)}, u32[]{:S(2)}) collective-permute-start(bf16[64,1024]{1,0:T(8,128)(2,1)S(1)} %shard_map.85), channel_id=1, source_target_pairs={{0,8},{4,20},{8,0},{12,28},{16,24},{20,4},{24,16},{28,12},{1,9},{5... | collective-permute-start | bytes 393224 | tf_op jit(solution)/shard_map/ppermute | solution.py:332
  79.2 6.3 %collective-permute-start.17 = (bf16[64,1024]{1,0:T(8,128)(2,1)S(1)}, bf16[64,1024]{1,0:T(8,128)(2,1)S(1)}, u32[]{:S(2)}, u32[]{:S(2)}) collective-permute-start(bf16[64,1024]{1,0:T(8,128)(2,1)S(1)} %add_convert_fusion.7.own), channel_id=1, source_target_pairs={{0,16},{4,12},{8,24},{12,4},{16,0},{20,28},{24,8},{28,20},{1,17},{... | collective-permute-start | bytes 393224 | tf_op jit(solution)/shard_map/ppermute | solution.py:332
  86.9 5.1 %collective-permute-start.18 = (bf16[64,1024]{1,0:T(8,128)(2,1)S(1)}, bf16[64,1024]{1,0:T(8,128)(2,1)S(1)}, u32[]{:S(2)}, u32[]{:S(2)}) collective-permute-start(bf16[64,1024]{1,0:T(8,128)(2,1)S(1)} %get-tuple-element.91), channel_id=1, source_target_pairs={{0,8},{4,20},{8,0},{12,28},{16,24},{20,4},{24,16},{28,12},{1,9},{5... | collective-permute-start | bytes 393224 | tf_op jit(solution)/shard_map/ppermute | solution.py:332
  92.0 5.3 %collective-permute-start.19 = (bf16[64,1024]{1,0:T(8,128)(2,1)S(1)}, bf16[64,1024]{1,0:T(8,128)(2,1)S(1)}, u32[]{:S(2)}, u32[]{:S(2)}) collective-permute-start(bf16[64,1024]{1,0:T(8,128)(2,1)S(1)} %add_convert_fusion.6.own), channel_id=1, source_target_pairs={{0,16},{4,12},{8,24},{12,4},{16,0},{20,28},{24,8},{28,20},{1,17},{... | collective-permute-start | bytes 393224 | tf_op jit(solution)/shard_map/ppermute | solution.py:332
  98.5 5.1 %collective-permute-start.20 = (bf16[64,1024]{1,0:T(8,128)(2,1)S(1)}, bf16[64,1024]{1,0:T(8,128)(2,1)S(1)}, u32[]{:S(2)}, u32[]{:S(2)}) collective-permute-start(bf16[64,1024]{1,0:T(8,128)(2,1)S(1)} %get-tuple-element.101), channel_id=1, source_target_pairs={{0,8},{4,20},{8,0},{12,28},{16,24},{20,4},{24,16},{28,12},{1,9},{5... | collective-permute-start | bytes 393224 | tf_op jit(solution)/shard_map/ppermute | solution.py:332
  103.6 6.3 %collective-permute-start.21 = (bf16[64,1024]{1,0:T(8,128)(2,1)S(1)}, bf16[64,1024]{1,0:T(8,128)(2,1)S(1)}, u32[]{:S(2)}, u32[]{:S(2)}) collective-permute-start(bf16[64,1024]{1,0:T(8,128)(2,1)S(1)} %add_convert_fusion.5.own), channel_id=1, source_target_pairs={{0,16},{4,12},{8,24},{12,4},{16,0},{20,28},{24,8},{28,20},{1,17},{... | collective-permute-start | bytes 393224 | tf_op jit(solution)/shard_map/ppermute | solution.py:332
  113.3 5.0 %collective-permute-start.22 = (bf16[64,1024]{1,0:T(8,128)(2,1)S(1)}, bf16[64,1024]{1,0:T(8,128)(2,1)S(1)}, u32[]{:S(2)}, u32[]{:S(2)}) collective-permute-start(bf16[64,1024]{1,0:T(8,128)(2,1)S(1)} %get-tuple-element.112), channel_id=1, source_target_pairs={{0,8},{4,20},{8,0},{12,28},{16,24},{20,4},{24,16},{28,12},{1,9},{5... | collective-permute-start | bytes 393224 | tf_op jit(solution)/shard_map/ppermute | solution.py:332
  118.4 5.0 %collective-permute-start.23 = (bf16[64,1024]{1,0:T(8,128)(2,1)S(1)}, bf16[64,1024]{1,0:T(8,128)(2,1)S(1)}, u32[]{:S(2)}, u32[]{:S(2)}) collective-permute-start(bf16[64,1024]{1,0:T(8,128)(2,1)S(1)} %add_convert_fusion.4.own), channel_id=1, source_target_pairs={{0,16},{4,12},{8,24},{12,4},{16,0},{20,28},{24,8},{28,20},{1,17},{... | collective-permute-start | bytes 393224 | tf_op jit(solution)/shard_map/ppermute | solution.py:332
  125.8 1.6 %collective-permute-start.24 = (bf16[128,1024]{1,0:T(8,128)(2,1)S(1)}, bf16[128,1024]{1,0:T(8,128)(2,1)S(1)}, u32[]{:S(2)}, u32[]{:S(2)}) collective-permute-start(bf16[128,1024]{1,0:T(8,128)(2,1)S(1)} %shard_map.99.own), channel_id=1, source_target_pairs={{0,4},{4,0},{8,12},{12,8},{16,20},{20,16},{24,28},{28,24},{1,5},{5... | collective-permute-start | bytes 786440 | tf_op jit(solution)/shard_map/ppermute | solution.py:328
  125.8 3.2 %copy-start.7 = (f32[256,1024]{1,0:T(8,128)}, f32[256,1024]{1,0:T(8,128)S(1)}, u32[]{:S(2)}) copy-start(f32[256,1024]{1,0:T(8,128)S(1)} %constant_dynamic-update-slice_fusion) | copy-start | bytes 3145732

commit v3 on v2

--- a/solution.py
+++ b/solution.py
@@ -177,9 +177,9 @@
                     fill += HALF
 
 
-def join_body(at, start, stop, place, own_ref, got_ref, *refs):
-    shards, out_ref, acc = refs[:-2], refs[-2], refs[-1]
-    z, chip, parts = place[1], place[2], len(shards)
+def join_body(at, parts, start, stop, place, own_ref, got_ref, *refs):
+    shards, outs, acc = refs[:parts], refs[parts:-1], refs[-1]
+    z, chip = place[1], place[2]
     acc[...] = own_ref[...].astype(f32) + got_ref[...].astype(f32)
     slab = shards[0].shape[1]
     per, blocks = WIDE // slab, parts * slab // WIDE
@@ -198,7 +198,10 @@
                     acc[into, lanes] = acc[into, lanes] + shards[d][top : top + rows, :].astype(f32)
 
             base += (blocks - g) * HALF
-    out_ref[...] = acc[...].astype(bf16)
+    top = 0
+    for out in outs:
+        out[...] = acc[top : top + out.shape[0], :].astype(bf16)
+        top += out.shape[0]
 
 
 def factor_body(group, at, place, own_ref, other_ref, *refs):
@@ -340,14 +343,6 @@
     def add(*values):
         return sum(value.astype(f32) for value in values).astype(bf16)
 
-    def sum_chips(value, fill=lambda value: ()):
-        for step in range(len(masks)):
-            got = cross(value, step)
-            got = after(got, *fill(value))
-            if step == len(masks) - 1:
-                return value, got
-            value = add(value, got)
-
     own_rows = a_diag[:HALF] if slab == HALF else lax.dynamic_slice_in_dim(a_diag, core * HALF, HALF, 0)
     corner = lax.dynamic_slice_in_dim(own_rows, chip * (HALF // chips), HALF // chips, 0)
     if slab == HALF:
@@ -391,32 +386,30 @@
         scratch=(shaped((order, order), f32), shaped((count * half, order), bf16)),
     )
 
-    def chunk_half(own, away, shards, at, start, stop, fill=lambda value: ()):
+    def join(own, away, shards, at, start, stop, outs):
         got = swap(away)
-        value = call(
-            functools.partial(join_body, at, start, stop),
-            shaped(own.shape, bf16),
+        return call(
+            functools.partial(join_body, at, parts, start, stop),
+            outs,
             place,
             own,
             got,
             *shards,
             scratch=(shaped(own.shape, f32),),
         )
-        return add(*sum_chips(value, fill))
-
-    head_half = chunk_half(own0, away0, lefts, left_rows, 0, 1)
-    head = head_half, swap(head_half)
-    left_other = swap(left_t)
-    chunks, mixed = [head], []
+
+    whole = shaped((rank, order), bf16)
+    steps, chunks = len(masks), []
     slabs, halves, inverses = [], [], []
 
     def factor(*earlier):
         g = len(halves)
         if g >= groups:
             return ()
-        wide = g * HALF // WIDE
-        own, other = chunks[min(wide, 1)]
-        done = sum(order // 2 - w * HALF for w in range(1, wide))
+        index, done = place_of[g * HALF // WIDE]
+        if index >= len(chunks):
+            return ()
+        own, other = chunks[index]
         slab_part, half_part, inverse = call(
             functools.partial(factor_body, g, done),
             (
@@ -435,56 +428,91 @@
         inverses.append(inverse)
         return (inverse,)
 
-    def mix(*earlier):
-        if not mixed:
-            mixed.extend(
-                call(
-                    functools.partial(mixed_body, parts),
-                    (shaped((count * half, order), bf16),) * 2,
-                    place,
-                    mask,
-                    after(rights[0], *earlier),
-                    *rights[1:],
-                    panel,
-                    scratch=(shaped((count * half, order), bf16),),
-                    scalars=2,
-                )
-            )
-        return tuple(mixed)
-
-    def tail_fill(value):
-        return mix(value) if halves else factor(value)
-
-    tail_half = chunk_half(
-        own1, after(away1, head_half), rights, count * half, 1, order // WIDE, tail_fill
-    )
-    chunks.append((tail_half, swap(tail_half)))
-    mixed_own, mixed_away = mix()
-    mixed_other = swap(mixed_away)
-    factors = (left_t, left_other, mixed_own, mixed_other)
-    whole = shaped((rank, order), bf16)
-
     def low_term(value, forward):
         return call(
             functools.partial(low_body, forward), shaped((rank, order), f32), place, value, low_t
         )
 
-    def fill(value):
-        return factor(value)
-
-    low = low_term(sketch_t, True)
-    done = factor(mixed_away)
-    value = call(first_body, whole, place, after(sketch_t, *done, tail_half), *factors)
-    value = sum_chips(value, fill)
+    head = join(own0, away0, lefts, left_rows, 0, 1, shaped(own0.shape, bf16))
+    low = low_term(after(sketch_t, right), True)
+    left_other = swap(left_t)
+    mixed_own, mixed_away = call(
+        functools.partial(mixed_body, parts),
+        (shaped((count * half, order), bf16),) * 2,
+        place,
+        mask,
+        after(rights[0], head, low),
+        *rights[1:],
+        panel,
+        scratch=(shaped((count * half, order), bf16),),
+        scalars=2,
+    )
+    mixed_other = swap(mixed_away)
+    factors = (left_t, left_other, mixed_own, mixed_other)
+    for step in range(steps):
+        got = cross(after(head, mixed_away) if step == 1 else head, step)
+        head = add(head, got)
+    chunks.append((head, swap(head)))
+
+    wides = order // WIDE
+    sizes = [order // 2 - g * HALF for g in range(wides)]
+    split = next(g for g in range(2, wides + 1) if 2 * sum(sizes[1:g]) >= rest_rows)
+    place_of = {0: (0, 0)}
+    for g in range(1, wides):
+        start = 1 if g < split else split
+        place_of[g] = (1 if g < split else 2, sum(sizes[start:g]))
+    value = call(first_body, whole, place, after(sketch_t, low), *factors)
+    parts_of_tail = (
+        shaped((sum(sizes[1:split]), WIDE), bf16),
+        shaped((sum(sizes[split:]), WIDE), bf16),
+    )
+    tail = list(join(own1, away1, rights, count * half, 1, wides, parts_of_tail))
+    queue = [(i, step) for i in range(2) for step in range(steps)]
+    flying = {}
+
+    def launch(*earlier):
+        if queue:
+            i, step = queue.pop(0)
+            tail[i] = after(tail[i], *earlier)
+            flying[i] = cross(tail[i], step), step
+
+    def land(*earlier):
+        if not flying:
+            return ()
+        i, (got, step) = flying.popitem()
+        tail[i] = add(tail[i], after(got, *earlier))
+        if step == steps - 1:
+            chunks.append((tail[i], swap(tail[i])))
+        return (tail[i],)
+
+    def sum_chips(value):
+        for step in range(steps):
+            got = cross(value, step)
+            if not flying:
+                launch(value)
+            done = factor(value)
+            got = after(got, *done)
+            landed = land(*done)
+            launch(*landed)
+            if step == steps - 1:
+                return value, after(got, *landed)
+            value = add(value, got)
+            value = after(value, *landed)
+
+    launch(value)
+    value = sum_chips(value)
     for forward in (False, True):
         start, value = call(
             functools.partial(middle_body, forward), (whole, whole), place, *value, low, *factors
         )
         low = low_term(start, forward)
-        value = sum_chips(value, fill)
+        value = sum_chips(value)
     basis, value = call(basis_body, (whole, whole), place, *value, low, *factors)
     low = low_term(basis, False)
-    value = sum_chips(value, fill)
+    value = sum_chips(value)
+    while queue or flying:
+        land()
+        launch()
     while len(halves) < groups:
         factor()
     diag_out = jnp.concatenate(slabs, axis=1)

time: 130 us -> 120 us (0.923)
  waiting for transfers between devices: 41.2 us -> 34.4 us
  starting transfers between devices: 29.7 us -> 26.8 us
    ppermute x12 -> x14, waiting for transfers between devices: 21.6 us -> 12.2 us  [cross(): lax.ppermute(value, 'cols', [(i, i ^ bits[i % 2]) for i in range(cols)])]
    ppermute x6, waiting for transfers between devices: 15.1 us -> 19.2 us  [spread_rows(): lax.ppermute(value, 'rows', [(i, (i + d) % parts) for i in range(parts)])]
    ppermute x6, starting transfers between devices: 13.2 us -> 11 us  [spread_rows(): lax.ppermute(value, 'rows', [(i, (i + d) % parts) for i in range(parts)])]
    ppermute x7 -> x8, waiting for transfers between devices: 4.53 us -> 3 us  [swap(): return lax.ppermute(value, 'cols', partner)]
    ppermute x12 -> x14, starting transfers between devices: 15.7 us -> 14.5 us  [cross(): lax.ppermute(value, 'cols', [(i, i ^ bits[i % 2]) for i in range(cols)])]
  transfers between devices with their start and end apart: 25 -> 28, of which waited for: 13 -> 11; matrix products, arithmetic and copies ran while one was open for 0% -> 0% of each run, Pallas kernels for 30% -> 35%
where the time goes in v3:
time: 120 us; the launch traced here: 119 us
  Pallas kernels  52.3 us (44%)
  waiting for transfers between devices  34.4 us (29%)
  starting transfers between devices  26.8 us (22%)
  local copies, waits for them, and re-layouts  4.3 us (4%)
    pallas_call x24, Pallas kernels, call(): pl.pallas_call(body, out_shape=outs, in_specs=[SMEM] * scalars + [VMEM] *...  52.3 us
    ppermute x6, waiting for transfers between devices, spread_rows(): lax.ppermute(value, 'rows', [(i, (i + d) % parts) for i in range(parts)])  19.2 us
    ppermute x14, starting transfers between devices, cross(): lax.ppermute(value, 'cols', [(i, i ^ bits[i % 2]) for i in range(cols)])  14.5 us
    ppermute x14, waiting for transfers between devices, cross(): lax.ppermute(value, 'cols', [(i, i ^ bits[i % 2]) for i in range(cols)])  12.2 us
    ppermute x6, starting transfers between devices, spread_rows(): lax.ppermute(value, 'rows', [(i, (i + d) % parts) for i in range(parts)])  11 us
    unnamed x23, local copies, waits for them, and re-layouts  4.18 us
    ppermute x8, waiting for transfers between devices, swap(): return lax.ppermute(value, 'cols', partner)  3 us
  transfers between devices with their start and end apart: 28, of which 11 were waited for; matrix products, arithmetic and copies ran while one was open for 0% of the time, Pallas kernels for 35%

profile of v3, /device:TPU:0, one launch (start us, length us, event | category | flops | bytes accessed | tf_op | source)
XLA Modules:
  0.0 119.4 jit_solution(6888745122280037610)
XLA Ops:
  0.7 1.2 copy-done
  1.9 0.1 stack.19.place
  2.0 0.9 copy-done.2
  2.9 0.9 shard_map.79.refs_0_
  3.8 5.1 %collective-permute-start.2 = (bf16[288,256]{1,0:T(8,128)(2,1)S(1)}, bf16[288,256]{1,0:T(8,128)(2,1)S(1)}, u32[]{:S(2)}, u32[]{:S(2)}) collective-permute-start(bf16[288,256]{1,0:T(8,128)(2,1)S(1)} %shard_map.79.refs_0_), channel_id=1, source_target_pairs={{0,3},{1,0},{2,1},{3,2},{4,7},{5,4},{6,5},{7,6},{8,11},{9,8},{10,9... | collective-permute-start | bytes 442376 | tf_op jit(solution)/shard_map/ppermute | solution.py:339
  8.9 1.0 collective-permute-start
  9.9 0.9 copy-done.3
  10.9 1.0 copy-done.4
  11.9 0.7 shard_map.77
  12.6 0.6 collective-permute-done.2.refs_3_
  13.2 8.2 %collective-permute-done.1.refs_2_ = bf16[288,256]{1,0:T(8,128)(2,1)S(1)} collective-permute-done((bf16[288,256]{1,0:T(8,128)(2,1)S(1)}, bf16[288,256]{1,0:T(8,128)(2,1)S(1)}, u32[]{:S(2)}, u32[]{:S(2)}) %collective-permute-start.1) | collective-permute-done | bytes 147488 | tf_op jit(solution)/shard_map/ppermute | solution.py:339
  21.4 1.7 %shard_map.80 = (bf16[192,1024]{1,0:T(8,128)(2,1)S(1)}, bf16[512,256]{1,0:T(8,128)(2,1)S(1)}, bf16[768,256]{1,0:T(8,128)(2,1)S(1)}, bf16[512,256]{1,0:T(8,128)(2,1)S(1)}, bf16[768,256]{1,0:T(8,128)(2,1)S(1)}) custom-call(s32[5]{0:T(128)S(1)} %stack.19.place, bf16[288,256]{1,0:T(8,128)(2,1)S(1)} %shard_map.79.refs_0_, ...), custom_call_target="tpu_custom_call" | custom-call | tf_op jit(solution)/shard_map/pallas_call | solution.py:47
  23.1 0.1 collective-permute-start.4
  23.2 1.5 %collective-permute-done.4.got_ref = bf16[512,256]{1,0:T(8,128)(2,1)S(1)} collective-permute-done((bf16[512,256]{1,0:T(8,128)(2,1)S(1)}, bf16[512,256]{1,0:T(8,128)(2,1)S(1)}, u32[]{:S(2)}, u32[]{:S(2)}) %collective-permute-start.4) | collective-permute-done | bytes 262176 | tf_op jit(solution)/shard_map/ppermute | solution.py:331
  24.7 0.7 shard_map.81
  25.4 1.6 %collective-permute-start.10 = (bf16[512,256]{1,0:T(8,128)(2,1)S(1)}, bf16[512,256]{1,0:T(8,128)(2,1)S(1)}, u32[]{:S(2)}, u32[]{:S(2)}) collective-permute-start(bf16[512,256]{1,0:T(8,128)(2,1)S(1)} %shard_map.81), channel_id=1, source_target_pairs={{0,8},{4,20},{8,0},{12,28},{16,24},{20,4},{24,16},{28,12},{1,9},{5... | collective-permute-start | bytes 786440 | tf_op jit(solution)/shard_map/ppermute | solution.py:335
  26.9 1.4 %collective-permute-start.7 = (bf16[288,256]{1,0:T(8,128)(2,1)S(1)}, bf16[288,256]{1,0:T(8,128)(2,1)S(1)}, u32[]{:S(2)}, u32[]{:S(2)}) collective-permute-start(bf16[288,256]{1,0:T(8,128)(2,1)S(1)} %get-tuple-element.86.refs_0_), channel_id=1, source_target_pairs={{0,3},{1,0},{2,1},{3,2},{4,7},{5,4},{6,5},{7,6},{8,11},{9,8},{10,9... | collective-permute-start | bytes 442376 | tf_op jit(solution)/shard_map/ppermute | solution.py:339
  28.3 1.4 %collective-permute-start.6 = (bf16[288,256]{1,0:T(8,128)(2,1)S(1)}, bf16[288,256]{1,0:T(8,128)(2,1)S(1)}, u32[]{:S(2)}, u32[]{:S(2)}) collective-permute-start(bf16[288,256]{1,0:T(8,128)(2,1)S(1)} %get-tuple-element.86.refs_0_), channel_id=1, source_target_pairs={{0,2},{1,3},{2,0},{3,1},{4,6},{5,7},{6,4},{7,5},{8,10},{9,11},{10,... | collective-permute-start | bytes 442376 | tf_op jit(solution)/shard_map/ppermute | solution.py:339
  29.7 2.0 %collective-permute-start.5 = (bf16[288,256]{1,0:T(8,128)(2,1)S(1)}, bf16[288,256]{1,0:T(8,128)(2,1)S(1)}, u32[]{:S(2)}, u32[]{:S(2)}) collective-permute-start(bf16[288,256]{1,0:T(8,128)(2,1)S(1)} %get-tuple-element.86.refs_0_), channel_id=1, source_target_pairs={{0,1},{1,2},{2,3},{3,0},{4,5},{5,6},{6,7},{7,4},{8,9},{9,10},{10,1... | collective-permute-start | bytes 442376 | tf_op jit(solution)/shard_map/ppermute | solution.py:339
  31.8 0.9 shard_map.78.low
  32.7 10.4 %collective-permute-done.6.refs_2_ = bf16[288,256]{1,0:T(8,128)(2,1)S(1)} collective-permute-done((bf16[288,256]{1,0:T(8,128)(2,1)S(1)}, bf16[288,256]{1,0:T(8,128)(2,1)S(1)}, u32[]{:S(2)}, u32[]{:S(2)}) %collective-permute-start.6) | collective-permute-done | bytes 147488 | tf_op jit(solution)/shard_map/ppermute | solution.py:339
  43.1 2.4 %shard_map.82 = (bf16[192,1024]{1,0:T(8,128)(2,1)S(1)}, bf16[192,1024]{1,0:T(8,128)(2,1)S(1)}) custom-call(s32[5]{0:T(128)S(1)} %stack.19.place, s32[2,3]{1,0:T(2,128)S(1)} %copy-done.6, bf16[288,256]{1,0:T(8,128)(2,1)S(1)} %get-tuple-element.86.refs_0_, bf16[288,256]{1,0:T(8,128)(2,1)S(1)} %collective-permute-done.5.refs_1_, ...), custom_call_target="tpu_custom_call" | custom-call | tf_op jit(solution)/shard_map/pallas_call | solution.py:47
  45.5 0.1 add_convert_fusion.1
  45.6 0.6 collective-permute-start.11
  46.2 0.5 collective-permute-start.13
  46.7 0.5 collective-permute-start.8
  47.2 4.8 %collective-permute-done.11 = bf16[512,256]{1,0:T(8,128)(2,1)S(1)} collective-permute-done((bf16[512,256]{1,0:T(8,128)(2,1)S(1)}, bf16[512,256]{1,0:T(8,128)(2,1)S(1)}, u32[]{:S(2)}, u32[]{:S(2)}) %collective-permute-start.11) | collective-permute-done | bytes 262176 | tf_op jit(solution)/shard_map/ppermute | solution.py:335
  52.1 0.1 collective-permute-start.12
  52.2 0.9 shard_map.85
  53.2 1.1 shard_map.83
  54.3 1.2 %collective-permute-start.14 = (bf16[384,256]{1,0:T(8,128)(2,1)S(1)}, bf16[384,256]{1,0:T(8,128)(2,1)S(1)}, u32[]{:S(2)}, u32[]{:S(2)}) collective-permute-start(bf16[384,256]{1,0:T(8,128)(2,1)S(1)} %get-tuple-element.96), channel_id=1, source_target_pairs={{0,8},{4,20},{8,0},{12,28},{16,24},{20,4},{24,16},{28,12},{1,9},{5... | collective-permute-start | bytes 589832 | tf_op jit(solution)/shard_map/ppermute | solution.py:335
  55.5 0.8 collective-permute-start.9
  56.4 3.6 %shard_map.84 = (f32[256,128]{1,0:T(8,128)S(1)}, bf16[1024,128]{1,0:T(8,128)(2,1)S(1)}, bf16[128,128]{1,0:T(8,128)(2,1)S(1)}) custom-call(s32[5]{0:T(128)S(1)} %stack.19.place, bf16[512,256]{1,0:T(8,128)(2,1)S(1)} %add_convert_fusion.own_ref, bf16[512,256]{1,0:T(8,128)(2,1)S(1)} %collective-permute-done.12.other_ref), custom_call_target="tpu_custom_call" | custom-call | tf_op jit(solution)/shard_map/pallas_call | solution.py:47
  60.1 1.3 %collective-permute-done.9 = bf16[64,1024]{1,0:T(8,128)(2,1)S(1)} collective-permute-done((bf16[64,1024]{1,0:T(8,128)(2,1)S(1)}, bf16[64,1024]{1,0:T(8,128)(2,1)S(1)}, u32[]{:S(2)}, u32[]{:S(2)}) %collective-permute-start.9) | collective-permute-done | bytes 131104 | tf_op jit(solution)/shard_map/ppermute | solution.py:335
  61.4 0.5 collective-permute-start.16
  62.0 3.9 %shard_map.86 = (f32[256,128]{1,0:T(8,128)S(1)}, bf16[896,128]{1,0:T(8,128)(2,1)S(1)}, bf16[128,128]{1,0:T(8,128)(2,1)S(1)}) custom-call(s32[5]{0:T(128)S(1)} %stack.19.place, bf16[512,256]{1,0:T(8,128)(2,1)S(1)} %add_convert_fusion.own_ref, bf16[512,256]{1,0:T(8,128)(2,1)S(1)} %collective-permute-done.12.other_ref, ...), custom_call_target="tpu_custom_call" | custom-call | tf_op jit(solution)/shard_map/pallas_call | solution.py:47
  65.8 1.3 %collective-permute-done.16 = bf16[384,256]{1,0:T(8,128)(2,1)S(1)} collective-permute-done((bf16[384,256]{1,0:T(8,128)(2,1)S(1)}, bf16[384,256]{1,0:T(8,128)(2,1)S(1)}, u32[]{:S(2)}, u32[]{:S(2)}) %collective-permute-start.16) | collective-permute-done | bytes 196640 | tf_op jit(solution)/shard_map/ppermute | solution.py:335
  67.2 1.2 %collective-permute-start.19 = (bf16[384,256]{1,0:T(8,128)(2,1)S(1)}, bf16[384,256]{1,0:T(8,128)(2,1)S(1)}, u32[]{:S(2)}, u32[]{:S(2)}) collective-permute-start(bf16[384,256]{1,0:T(8,128)(2,1)S(1)} %get-tuple-element.112), channel_id=1, source_target_pairs={{0,8},{4,20},{8,0},{12,28},{16,24},{20,4},{24,16},{28,12},{1,9},{5... | collective-permute-start | bytes 589832 | tf_op jit(solution)/shard_map/ppermute | solution.py:335
  68.5 0.8 collective-permute-start.15
  69.3 4.5 %collective-permute-done.15.got = bf16[64,1024]{1,0:T(8,128)(2,1)S(1)} collective-permute-done((bf16[64,1024]{1,0:T(8,128)(2,1)S(1)}, bf16[64,1024]{1,0:T(8,128)(2,1)S(1)}, u32[]{:S(2)}, u32[]{:S(2)}) %collective-permute-start.15) | collective-permute-done | bytes 131104 | tf_op jit(solution)/shard_map/ppermute | solution.py:335
  73.8 1.1 shard_map.87
  75.0 1.3 %collective-permute-start.17 = (bf16[64,1024]{1,0:T(8,128)(2,1)S(1)}, bf16[64,1024]{1,0:T(8,128)(2,1)S(1)}, u32[]{:S(2)}, u32[]{:S(2)}) collective-permute-start(bf16[64,1024]{1,0:T(8,128)(2,1)S(1)} %get-tuple-element.106), channel_id=1, source_target_pairs={{0,8},{4,20},{8,0},{12,28},{16,24},{20,4},{24,16},{28,12},{1,9},{5... | collective-permute-start | bytes 393224 | tf_op jit(solution)/shard_map/ppermute | solution.py:335
  76.2 3.8 %shard_map.88 = (f32[256,128]{1,0:T(8,128)S(1)}, bf16[768,128]{1,0:T(8,128)(2,1)S(1)}, bf16[128,128]{1,0:T(8,128)(2,1)S(1)}) custom-call(s32[5]{0:T(128)S(1)} %stack.19.place, bf16[384,256]{1,0:T(8,128)(2,1)S(1)} %add_convert_fusion.4.own_ref, bf16[384,256]{1,0:T(8,128)(2,1)S(1)} %collective-permute-done.18.other_ref, ...), custom_call_target="tpu_custom_call" | custom-call | tf_op jit(solution)/shard_map/pallas_call | solution.py:47
  80.1 0.9 collective-permute-start.21
  81.0 1.3 %collective-permute-start.20 = (bf16[64,1024]{1,0:T(8,128)(2,1)S(1)}, bf16[64,1024]{1,0:T(8,128)(2,1)S(1)}, u32[]{:S(2)}, u32[]{:S(2)}) collective-permute-start(bf16[64,1024]{1,0:T(8,128)(2,1)S(1)} %add_convert_fusion.8.own), channel_id=1, source_target_pairs={{0,16},{4,12},{8,24},{12,4},{16,0},{20,28},{24,8},{28,20},{1,17},{... | collective-permute-start | bytes 393224 | tf_op jit(solution)/shard_map/ppermute | solution.py:335
  82.3 3.8 %shard_map.89 = (f32[256,128]{1,0:T(8,128)S(1)}, bf16[640,128]{1,0:T(8,128)(2,1)S(1)}, bf16[128,128]{1,0:T(8,128)(2,1)S(1)}) custom-call(s32[5]{0:T(128)S(1)} %stack.19.place, bf16[384,256]{1,0:T(8,128)(2,1)S(1)} %add_convert_fusion.4.own_ref, bf16[384,256]{1,0:T(8,128)(2,1)S(1)} %collective-permute-done.18.other_ref, ...), custom_call_target="tpu_custom_call" | custom-call | tf_op jit(solution)/shard_map/pallas_call | solution.py:47
  86.2 0.1 collective-permute-start.23
  86.2 0.9 shard_map.90.low
  87.1 0.1 collective-permute-done.20.got
  87.2 1.1 shard_map.91
  88.4 1.1 collective-permute-start.22
  89.5 4.0 %shard_map.92 = (f32[256,128]{1,0:T(8,128)S(1)}, bf16[512,128]{1,0:T(8,128)(2,1)S(1)}, bf16[128,128]{1,0:T(8,128)(2,1)S(1)}) custom-call(s32[5]{0:T(128)S(1)} %stack.19.place, bf16[384,256]{1,0:T(8,128)(2,1)S(1)} %add_convert_fusion.2.own_ref, bf16[384,256]{1,0:T(8,128)(2,1)S(1)} %collective-permute-done.23.other_ref, ...), custom_call_target="tpu_custom_call" | custom-call | tf_op jit(solution)/shard_map/pallas_call | solution.py:47
  93.6 0.9 collective-permute-start.24
  94.5 0.9 shard_map.94.low
  95.4 3.9 %shard_map.93 = (f32[256,128]{1,0:T(8,128)S(1)}, bf16[384,128]{1,0:T(8,128)(2,1)S(1)}, bf16[128,128]{1,0:T(8,128)(2,1)S(1)}) custom-call(s32[5]{0:T(128)S(1)} %stack.19.place, bf16[384,256]{1,0:T(8,128)(2,1)S(1)} %add_convert_fusion.2.own_ref, bf16[384,256]{1,0:T(8,128)(2,1)S(1)} %collective-permute-done.23.other_ref, ...), custom_call_target="tpu_custom_call" | custom-call | tf_op jit(solution)/shard_map/pallas_call | solution.py:47
  99.3 3.4 %shard_map.95 = (bf16[64,1024]{1,0:T(8,128)(2,1)S(1)}, bf16[64,1024]{1,0:T(8,128)(2,1)S(1)}) custom-call(s32[5]{0:T(128)S(1)} %stack.19.place, bf16[64,1024]{1,0:T(8,128)(2,1)S(1)} %add_convert_fusion.7.own, bf16[64,1024]{1,0:T(8,128)(2,1)S(1)} %collective-permute-done.24.got, f32[64,1024]{1,0:T(8,128)S(1)} %shard_map.94.low, ...), custom_call_target="tpu_custom_call" | custom-call | tf_op jit(solution)/shard_map/pallas_call | solution.py:47
  102.7 1.1 collective-permute-start.25
  103.8 3.9 %shard_map.96 = (f32[256,128]{1,0:T(8,128)S(1)}, bf16[256,128]{1,0:T(8,128)(2,1)S(1)}, bf16[128,128]{1,0:T(8,128)(2,1)S(1)}) custom-call(s32[5]{0:T(128)S(1)} %stack.19.place, bf16[384,256]{1,0:T(8,128)(2,1)S(1)} %add_convert_fusion.2.own_ref, bf16[384,256]{1,0:T(8,128)(2,1)S(1)} %collective-permute-done.23.other_ref, ...), custom_call_target="tpu_custom_call" | custom-call | tf_op jit(solution)/shard_map/pallas_call | solution.py:47
  107.7 1.3 %collective-permute-start.26 = (bf16[64,1024]{1,0:T(8,128)(2,1)S(1)}, bf16[64,1024]{1,0:T(8,128)(2,1)S(1)}, u32[]{:S(2)}, u32[]{:S(2)}) collective-permute-start(bf16[64,1024]{1,0:T(8,128)(2,1)S(1)} %add_convert_fusion.6.own), channel_id=1, source_target_pairs={{0,16},{4,12},{8,24},{12,4},{16,0},{20,28},{24,8},{28,20},{1,17},{... | collective-permute-start | bytes 393224 | tf_op jit(solution)/shard_map/ppermute | solution.py:335
  109.1 0.9 shard_map.98.low
  110.0 3.8 %shard_map.97 = (f32[256,128]{1,0:T(8,128)S(1)}, bf16[128,128]{1,0:T(8,128)(2,1)S(1)}, bf16[128,128]{1,0:T(8,128)(2,1)S(1)}) custom-call(s32[5]{0:T(128)S(1)} %stack.19.place, bf16[384,256]{1,0:T(8,128)(2,1)S(1)} %add_convert_fusion.2.own_ref, bf16[384,256]{1,0:T(8,128)(2,1)S(1)} %collective-permute-done.23.other_ref, ...), custom_call_target="tpu_custom_call" | custom-call | tf_op jit(solution)/shard_map/pallas_call | solution.py:47
  113.8 2.4 %shard_map.99.own = bf16[128,1024]{1,0:T(8,128)(2,1)S(1)} custom-call(s32[5]{0:T(128)S(1)} %stack.19.place, bf16[64,1024]{1,0:T(8,128)(2,1)S(1)} %get-tuple-element.133.value_ref.basis, bf16[64,1024]{1,0:T(8,128)(2,1)S(1)} %add_convert_fusion.6.own, bf16[64,1024]{1,0:T(8,128)(2,1)S(1)} %collective-permute-done.26.got, f32[64,1024]{1,0:T(8,128)S(1)} %shard_map.98.low, ...), custom_call_target="tpu_custom_call" | custom-call | tf_op jit(solution)/shard_map/pallas_call | solution.py:47
  116.2 1.5 %collective-permute-done.27.other = bf16[128,1024]{1,0:T(8,128)(2,1)S(1)} collective-permute-done((bf16[128,1024]{1,0:T(8,128)(2,1)S(1)}, bf16[128,1024]{1,0:T(8,128)(2,1)S(1)}, u32[]{:S(2)}, u32[]{:S(2)}) %collective-permute-start.27) | collective-permute-done | bytes 262176 | tf_op jit(solution)/shard_map/ppermute | solution.py:331
  117.7 1.7 %shard_map.100 = f32[2,1024,128]{2,1,0:T(8,128)} custom-call(s32[5]{0:T(128)S(1)} %stack.19.place, bf16[128,1024]{1,0:T(8,128)(2,1)S(1)} %shard_map.99.own, bf16[128,1024]{1,0:T(8,128)(2,1)S(1)} %collective-permute-done.27.other), custom_call_target="tpu_custom_call" | custom-call | tf_op jit(solution)/shard_map/pallas_call | solution.py:47
  (52 shorter events, 0.8 us)
Async XLA Ops:
  0.6 1.2 %copy-start = (f32[256,1024]{1,0:T(8,128)S(1)}, f32[256,1024]{1,0:T(8,128)}, u32[]{:S(2)}) copy-start(f32[256,1024]{1,0:T(8,128)} %param.10) | copy-start | bytes 3145732
  2.0 0.9 copy-start.2
  2.9 28.9 %copy-start.5 = (bf16[1024,64]{0,1:T(8,128)(2,1)S(1)}, bf16[1024,64]{0,1:T(8,128)(2,1)}, u32[]{:S(2)}) copy-start(bf16[1024,64]{0,1:T(8,128)(2,1)} %param.11) | copy-start | bytes 393220
  2.9 40.2 %copy-start.6 = (s32[2,3]{1,0:T(2,128)S(1)}, s32[2,3]{1,0:T(2,128)}, u32[]{:S(2)}) copy-start(s32[2,3]{1,0:T(2,128)} %mask_ref.1) | copy-start | bytes 76
  3.8 39.4 %copy-start.1 = (bf16[2,3,1024,128]{3,2,1,0:T(8,128)(2,1)S(1)}, bf16[2,3,1024,128]{3,2,1,0:T(8,128)(2,1)}, u32[]{:S(2)}) copy-start(bf16[2,3,1024,128]{3,2,1,0:T(8,128)(2,1)} %refs_4_.1) | copy-start | bytes 4718596
  3.8 9.4 %collective-permute-start.2 = (bf16[288,256]{1,0:T(8,128)(2,1)S(1)}, bf16[288,256]{1,0:T(8,128)(2,1)S(1)}, u32[]{:S(2)}, u32[]{:S(2)}) collective-permute-start(bf16[288,256]{1,0:T(8,128)(2,1)S(1)} %shard_map.79.refs_0_), channel_id=1, source_target_pairs={{0,3},{1,0},{2,1},{3,2},{4,7},{5,4},{6,5},{7,6},{8,11},{9,8},{10,9... | collective-permute-start | bytes 442376 | tf_op jit(solution)/shard_map/ppermute | solution.py:339
  8.9 12.5 %collective-permute-start.1 = (bf16[288,256]{1,0:T(8,128)(2,1)S(1)}, bf16[288,256]{1,0:T(8,128)(2,1)S(1)}, u32[]{:S(2)}, u32[]{:S(2)}) collective-permute-start(bf16[288,256]{1,0:T(8,128)(2,1)S(1)} %shard_map.79.refs_0_), channel_id=1, source_target_pairs={{0,2},{1,3},{2,0},{3,1},{4,6},{5,7},{6,4},{7,5},{8,10},{9,11},{10,... | collective-permute-start | bytes 442376 | tf_op jit(solution)/shard_map/ppermute | solution.py:339
  8.9 12.5 %collective-permute-start = (bf16[288,256]{1,0:T(8,128)(2,1)S(1)}, bf16[288,256]{1,0:T(8,128)(2,1)S(1)}, u32[]{:S(2)}, u32[]{:S(2)}) collective-permute-start(bf16[288,256]{1,0:T(8,128)(2,1)S(1)} %shard_map.79.refs_0_), channel_id=1, source_target_pairs={{0,1},{1,2},{2,3},{3,0},{4,5},{5,6},{6,7},{7,4},{8,9},{9,10},{10,1... | collective-permute-start | bytes 442376 | tf_op jit(solution)/shard_map/ppermute | solution.py:339
  9.9 0.9 copy-start.3
  10.9 1.0 copy-start.4
  23.1 1.6 %collective-permute-start.4 = (bf16[512,256]{1,0:T(8,128)(2,1)S(1)}, bf16[512,256]{1,0:T(8,128)(2,1)S(1)}, u32[]{:S(2)}, u32[]{:S(2)}) collective-permute-start(bf16[512,256]{1,0:T(8,128)(2,1)S(1)} %get-tuple-element.85), channel_id=1, source_target_pairs={{0,4},{4,0},{8,12},{12,8},{16,20},{20,16},{24,28},{28,24},{1,5},{5... | collective-permute-start | bytes 786440 | tf_op jit(solution)/shard_map/ppermute | solution.py:331
  25.4 20.1 %collective-permute-start.10 = (bf16[512,256]{1,0:T(8,128)(2,1)S(1)}, bf16[512,256]{1,0:T(8,128)(2,1)S(1)}, u32[]{:S(2)}, u32[]{:S(2)}) collective-permute-start(bf16[512,256]{1,0:T(8,128)(2,1)S(1)} %shard_map.81), channel_id=1, source_target_pairs={{0,8},{4,20},{8,0},{12,28},{16,24},{20,4},{24,16},{28,12},{1,9},{5... | collective-permute-start | bytes 786440 | tf_op jit(solution)/shard_map/ppermute | solution.py:335
  26.9 5.7 %collective-permute-start.7 = (bf16[288,256]{1,0:T(8,128)(2,1)S(1)}, bf16[288,256]{1,0:T(8,128)(2,1)S(1)}, u32[]{:S(2)}, u32[]{:S(2)}) collective-permute-start(bf16[288,256]{1,0:T(8,128)(2,1)S(1)} %get-tuple-element.86.refs_0_), channel_id=1, source_target_pairs={{0,3},{1,0},{2,1},{3,2},{4,7},{5,4},{6,5},{7,6},{8,11},{9,8},{10,9... | collective-permute-start | bytes 442376 | tf_op jit(solution)/shard_map/ppermute | solution.py:339
  28.3 14.8 %collective-permute-start.6 = (bf16[288,256]{1,0:T(8,128)(2,1)S(1)}, bf16[288,256]{1,0:T(8,128)(2,1)S(1)}, u32[]{:S(2)}, u32[]{:S(2)}) collective-permute-start(bf16[288,256]{1,0:T(8,128)(2,1)S(1)} %get-tuple-element.86.refs_0_), channel_id=1, source_target_pairs={{0,2},{1,3},{2,0},{3,1},{4,6},{5,7},{6,4},{7,5},{8,10},{9,11},{10,... | collective-permute-start | bytes 442376 | tf_op jit(solution)/shard_map/ppermute | solution.py:339
  29.7 13.4 %collective-permute-start.5 = (bf16[288,256]{1,0:T(8,128)(2,1)S(1)}, bf16[288,256]{1,0:T(8,128)(2,1)S(1)}, u32[]{:S(2)}, u32[]{:S(2)}) collective-permute-start(bf16[288,256]{1,0:T(8,128)(2,1)S(1)} %get-tuple-element.86.refs_0_), channel_id=1, source_target_pairs={{0,1},{1,2},{2,3},{3,0},{4,5},{5,6},{6,7},{7,4},{8,9},{9,10},{10,1... | collective-permute-start | bytes 442376 | tf_op jit(solution)/shard_map/ppermute | solution.py:339
  45.6 6.4 %collective-permute-start.11 = (bf16[512,256]{1,0:T(8,128)(2,1)S(1)}, bf16[512,256]{1,0:T(8,128)(2,1)S(1)}, u32[]{:S(2)}, u32[]{:S(2)}) collective-permute-start(bf16[512,256]{1,0:T(8,128)(2,1)S(1)} %add_convert_fusion.1), channel_id=1, source_target_pairs={{0,16},{4,12},{8,24},{12,4},{16,0},{20,28},{24,8},{28,20},{1,17},{... | collective-permute-start | bytes 786440 | tf_op jit(solution)/shard_map/ppermute | solution.py:335
  46.2 6.0 %collective-permute-start.13 = (bf16[768,256]{1,0:T(8,128)(2,1)S(1)}, bf16[768,256]{1,0:T(8,128)(2,1)S(1)}, u32[]{:S(2)}, u32[]{:S(2)}) collective-permute-start(bf16[768,256]{1,0:T(8,128)(2,1)S(1)} %get-tuple-element.94), channel_id=1, source_target_pairs={{0,4},{4,0},{8,12},{12,8},{16,20},{20,16},{24,28},{28,24},{1,5},{5... | collective-permute-start | bytes 1179656 | tf_op jit(solution)/shard_map/ppermute | solution.py:331
  46.7 6.4 %collective-permute-start.3 = (bf16[192,1024]{1,0:T(8,128)(2,1)S(1)}, bf16[192,1024]{1,0:T(8,128)(2,1)S(1)}, u32[]{:S(2)}, u32[]{:S(2)}) collective-permute-start(bf16[192,1024]{1,0:T(8,128)(2,1)S(1)} %get-tuple-element.82.u0), channel_id=1, source_target_pairs={{0,4},{4,0},{8,12},{12,8},{16,20},{20,16},{24,28},{28,24},{1,5},{5... | collective-permute-start | bytes 1179656 | tf_op jit(solution)/shard_map/ppermute | solution.py:331
  46.7 6.5 %collective-permute-start.8 = (bf16[192,1024]{1,0:T(8,128)(2,1)S(1)}, bf16[192,1024]{1,0:T(8,128)(2,1)S(1)}, u32[]{:S(2)}, u32[]{:S(2)}) collective-permute-start(bf16[192,1024]{1,0:T(8,128)(2,1)S(1)} %get-tuple-element.88), channel_id=1, source_target_pairs={{0,4},{4,0},{8,12},{12,8},{16,20},{20,16},{24,28},{28,24},{1,5},{5... | collective-permute-start | bytes 1179656 | tf_op jit(solution)/shard_map/ppermute | solution.py:331
  52.1 4.3 %collective-permute-start.12 = (bf16[512,256]{1,0:T(8,128)(2,1)S(1)}, bf16[512,256]{1,0:T(8,128)(2,1)S(1)}, u32[]{:S(2)}, u32[]{:S(2)}) collective-permute-start(bf16[512,256]{1,0:T(8,128)(2,1)S(1)} %add_convert_fusion.own_ref), channel_id=1, source_target_pairs={{0,4},{4,0},{8,12},{12,8},{16,20},{20,16},{24,28},{28,24},{1,5},{5... | collective-permute-start | bytes 786440 | tf_op jit(solution)/shard_map/ppermute | solution.py:331
  54.3 5.7 %collective-permute-start.14 = (bf16[384,256]{1,0:T(8,128)(2,1)S(1)}, bf16[384,256]{1,0:T(8,128)(2,1)S(1)}, u32[]{:S(2)}, u32[]{:S(2)}) collective-permute-start(bf16[384,256]{1,0:T(8,128)(2,1)S(1)} %get-tuple-element.96), channel_id=1, source_target_pairs={{0,8},{4,20},{8,0},{12,28},{16,24},{20,4},{24,16},{28,12},{1,9},{5... | collective-permute-start | bytes 589832 | tf_op jit(solution)/shard_map/ppermute | solution.py:335
  55.5 5.9 %collective-permute-start.9 = (bf16[64,1024]{1,0:T(8,128)(2,1)S(1)}, bf16[64,1024]{1,0:T(8,128)(2,1)S(1)}, u32[]{:S(2)}, u32[]{:S(2)}) collective-permute-start(bf16[64,1024]{1,0:T(8,128)(2,1)S(1)} %shard_map.83), channel_id=1, source_target_pairs={{0,8},{4,20},{8,0},{12,28},{16,24},{20,4},{24,16},{28,12},{1,9},{5... | collective-permute-start | bytes 393224 | tf_op jit(solution)/shard_map/ppermute | solution.py:335
  61.4 5.7 %collective-permute-start.16 = (bf16[384,256]{1,0:T(8,128)(2,1)S(1)}, bf16[384,256]{1,0:T(8,128)(2,1)S(1)}, u32[]{:S(2)}, u32[]{:S(2)}) collective-permute-start(bf16[384,256]{1,0:T(8,128)(2,1)S(1)} %add_convert_fusion.5), channel_id=1, source_target_pairs={{0,16},{4,12},{8,24},{12,4},{16,0},{20,28},{24,8},{28,20},{1,17},{... | collective-permute-start | bytes 589832 | tf_op jit(solution)/shard_map/ppermute | solution.py:335
  67.2 9.1 %collective-permute-start.18 = (bf16[384,256]{1,0:T(8,128)(2,1)S(1)}, bf16[384,256]{1,0:T(8,128)(2,1)S(1)}, u32[]{:S(2)}, u32[]{:S(2)}) collective-permute-start(bf16[384,256]{1,0:T(8,128)(2,1)S(1)} %add_convert_fusion.4.own_ref), channel_id=1, source_target_pairs={{0,4},{4,0},{8,12},{12,8},{16,20},{20,16},{24,28},{28,24},{1,5},{5... | collective-permute-start | bytes 589832 | tf_op jit(solution)/shard_map/ppermute | solution.py:331
  67.2 12.8 %collective-permute-start.19 = (bf16[384,256]{1,0:T(8,128)(2,1)S(1)}, bf16[384,256]{1,0:T(8,128)(2,1)S(1)}, u32[]{:S(2)}, u32[]{:S(2)}) collective-permute-start(bf16[384,256]{1,0:T(8,128)(2,1)S(1)} %get-tuple-element.112), channel_id=1, source_target_pairs={{0,8},{4,20},{8,0},{12,28},{16,24},{20,4},{24,16},{28,12},{1,9},{5... | collective-permute-start | bytes 589832 | tf_op jit(solution)/shard_map/ppermute | solution.py:335
  68.5 5.4 %collective-permute-start.15 = (bf16[64,1024]{1,0:T(8,128)(2,1)S(1)}, bf16[64,1024]{1,0:T(8,128)(2,1)S(1)}, u32[]{:S(2)}, u32[]{:S(2)}) collective-permute-start(bf16[64,1024]{1,0:T(8,128)(2,1)S(1)} %add_convert_fusion.9.own), channel_id=1, source_target_pairs={{0,16},{4,12},{8,24},{12,4},{16,0},{20,28},{24,8},{28,20},{1,17},{... | collective-permute-start | bytes 393224 | tf_op jit(solution)/shard_map/ppermute | solution.py:335
  75.0 5.1 %collective-permute-start.17 = (bf16[64,1024]{1,0:T(8,128)(2,1)S(1)}, bf16[64,1024]{1,0:T(8,128)(2,1)S(1)}, u32[]{:S(2)}, u32[]{:S(2)}) collective-permute-start(bf16[64,1024]{1,0:T(8,128)(2,1)S(1)} %get-tuple-element.106), channel_id=1, source_target_pairs={{0,8},{4,20},{8,0},{12,28},{16,24},{20,4},{24,16},{28,12},{1,9},{5... | collective-permute-start | bytes 393224 | tf_op jit(solution)/shard_map/ppermute | solution.py:335
  80.1 6.0 %collective-permute-start.21 = (bf16[384,256]{1,0:T(8,128)(2,1)S(1)}, bf16[384,256]{1,0:T(8,128)(2,1)S(1)}, u32[]{:S(2)}, u32[]{:S(2)}) collective-permute-start(bf16[384,256]{1,0:T(8,128)(2,1)S(1)} %add_convert_fusion.3), channel_id=1, source_target_pairs={{0,16},{4,12},{8,24},{12,4},{16,0},{20,28},{24,8},{28,20},{1,17},{... | collective-permute-start | bytes 589832 | tf_op jit(solution)/shard_map/ppermute | solution.py:335
  81.0 6.2 %collective-permute-start.20 = (bf16[64,1024]{1,0:T(8,128)(2,1)S(1)}, bf16[64,1024]{1,0:T(8,128)(2,1)S(1)}, u32[]{:S(2)}, u32[]{:S(2)}) collective-permute-start(bf16[64,1024]{1,0:T(8,128)(2,1)S(1)} %add_convert_fusion.8.own), channel_id=1, source_target_pairs={{0,16},{4,12},{8,24},{12,4},{16,0},{20,28},{24,8},{28,20},{1,17},{... | collective-permute-start | bytes 393224 | tf_op jit(solution)/shard_map/ppermute | solution.py:335
  86.2 3.3 %collective-permute-start.23 = (bf16[384,256]{1,0:T(8,128)(2,1)S(1)}, bf16[384,256]{1,0:T(8,128)(2,1)S(1)}, u32[]{:S(2)}, u32[]{:S(2)}) collective-permute-start(bf16[384,256]{1,0:T(8,128)(2,1)S(1)} %add_convert_fusion.2.own_ref), channel_id=1, source_target_pairs={{0,4},{4,0},{8,12},{12,8},{16,20},{20,16},{24,28},{28,24},{1,5},{5... | collective-permute-start | bytes 589832 | tf_op jit(solution)/shard_map/ppermute | solution.py:331
  88.4 5.2 %collective-permute-start.22 = (bf16[64,1024]{1,0:T(8,128)(2,1)S(1)}, bf16[64,1024]{1,0:T(8,128)(2,1)S(1)}, u32[]{:S(2)}, u32[]{:S(2)}) collective-permute-start(bf16[64,1024]{1,0:T(8,128)(2,1)S(1)} %get-tuple-element.123), channel_id=1, source_target_pairs={{0,8},{4,20},{8,0},{12,28},{16,24},{20,4},{24,16},{28,12},{1,9},{5... | collective-permute-start | bytes 393224 | tf_op jit(solution)/shard_map/ppermute | solution.py:335
  93.6 5.7 %collective-permute-start.24 = (bf16[64,1024]{1,0:T(8,128)(2,1)S(1)}, bf16[64,1024]{1,0:T(8,128)(2,1)S(1)}, u32[]{:S(2)}, u32[]{:S(2)}) collective-permute-start(bf16[64,1024]{1,0:T(8,128)(2,1)S(1)} %add_convert_fusion.7.own), channel_id=1, source_target_pairs={{0,16},{4,12},{8,24},{12,4},{16,0},{20,28},{24,8},{28,20},{1,17},{... | collective-permute-start | bytes 393224 | tf_op jit(solution)/shard_map/ppermute | solution.py:335
  102.7 5.0 %collective-permute-start.25 = (bf16[64,1024]{1,0:T(8,128)(2,1)S(1)}, bf16[64,1024]{1,0:T(8,128)(2,1)S(1)}, u32[]{:S(2)}, u32[]{:S(2)}) collective-permute-start(bf16[64,1024]{1,0:T(8,128)(2,1)S(1)} %get-tuple-element.134), channel_id=1, source_target_pairs={{0,8},{4,20},{8,0},{12,28},{16,24},{20,4},{24,16},{28,12},{1,9},{5... | collective-permute-start | bytes 393224 | tf_op jit(solution)/shard_map/ppermute | solution.py:335
  107.7 6.0 %collective-permute-start.26 = (bf16[64,1024]{1,0:T(8,128)(2,1)S(1)}, bf16[64,1024]{1,0:T(8,128)(2,1)S(1)}, u32[]{:S(2)}, u32[]{:S(2)}) collective-permute-start(bf16[64,1024]{1,0:T(8,128)(2,1)S(1)} %add_convert_fusion.6.own), channel_id=1, source_target_pairs={{0,16},{4,12},{8,24},{12,4},{16,0},{20,28},{24,8},{28,20},{1,17},{... | collective-permute-start | bytes 393224 | tf_op jit(solution)/shard_map/ppermute | solution.py:335
  116.1 1.6 %collective-permute-start.27 = (bf16[128,1024]{1,0:T(8,128)(2,1)S(1)}, bf16[128,1024]{1,0:T(8,128)(2,1)S(1)}, u32[]{:S(2)}, u32[]{:S(2)}) collective-permute-start(bf16[128,1024]{1,0:T(8,128)(2,1)S(1)} %shard_map.99.own), channel_id=1, source_target_pairs={{0,4},{4,0},{8,12},{12,8},{16,20},{20,16},{24,28},{28,24},{1,5},{5... | collective-permute-start | bytes 786440 | tf_op jit(solution)/shard_map/ppermute | solution.py:331
  116.2 3.2 %copy-start.7 = (f32[256,1024]{1,0:T(8,128)}, f32[256,1024]{1,0:T(8,128)S(1)}, u32[]{:S(2)}) copy-start(f32[256,1024]{1,0:T(8,128)S(1)} %constant_dynamic-update-slice_fusion) | copy-start | bytes 3145732
